TPU v7x, 512 devices: a whole 4x8x8 slice. The times are simulated.
512 devices in a mesh: path: 64 (over x, z, core), shard: 8 (over y).
Axes of the slice: x: 4, y: 8, z: 8, core: 2. Of those that a mesh axis runs over, the one named last changes fastest.
Arguments:
- deltas: bfloat16 [64, 128, 4096], P('path', 'shard'), may hold values from -96 to 96
- momentum: float32 [16, 128, 4096], P(None, 'shard', 'path'), may hold values from -4 to 4
- path_module: int32 [64], replicated, may hold values from 0 to 15, as said below
Outputs:
- path_update: bfloat16 [64, 128, 4096], P('path', 'shard')
- new_momentum: float32 [16, 128, 4096], P(None, 'shard', 'path')
Inputs may be any that keep to these rules, and one draw needn't show every extreme that they name: `path_module`: every module is used by at least one and at most seven paths.
All inputs are finite; a program needn't handle non-finite values.
Results may differ from a plain program's by a relative error of at most 0.0004.
Values may be sent and summed in bfloat16 or wider, within the bound.
No kernel may reach another device: no remote copies, remote signals or barrier semaphores. Data moves between devices by JAX's collectives and lax.ppermute only.
A program may use at most 64 MiB of HBM per device.

v0:
```python
import jax
import jax.numpy as jnp
from jax import lax
from jax.sharding import Mesh
from jax.sharding import PartitionSpec as P

D = 4096
PATH = ("path_0", "path_1", "path_2")


outer_rate = 0.7
momentum_rate = 0.9
clip_ratio = 2.0


def cut_along(array, dim, peers):
    before, after = (array.shape[:dim], array.shape[dim + 1 :])
    return jnp.moveaxis(array.reshape(*before, peers, -1, *after), dim, 0)


def joined_along(pieces, dim):
    pieces = jnp.moveaxis(pieces, 0, dim)
    lengths = pieces.shape
    return pieces.reshape(*lengths[:dim], lengths[dim] * lengths[dim + 1], *lengths[dim + 2 :])


def exchange_in_order(pieces, axes, turns):
    inside = pieces.shape[1:]
    whole = pieces.reshape(*(lax.axis_size(a) for a in axes), *inside)
    for k in turns:
        whole = lax.all_to_all(whole, axes[k], k, k, tiled=True)
    return whole.reshape(-1, *inside)


def two_step_exchange(array, groups, turns, split_dim, concat_dim):
    peers = lax.axis_size(groups[0]) * lax.axis_size(groups[1])
    pieces = cut_along(array, split_dim, peers)
    return joined_along(exchange_in_order(pieces, groups, turns), concat_dim)


def copy_for_each(array, axis):
    copies = jnp.broadcast_to(array, (lax.axis_size(axis), *array.shape))
    return lax.all_to_all(copies, axis, split_axis=0, concat_axis=0, tiled=True)


def of_everyone(array, axis):
    return copy_for_each(array, axis).sum(axis=0)


def by_axis(array, axes):
    far, near = axes
    return of_everyone(of_everyone(array, near), far)


def local(deltas, momentum, path_module):
    modules = momentum.shape[0]
    row_count = deltas.shape[1]
    onehot = (path_module[:, None] == jnp.arange(modules, dtype=jnp.int32)[None, :]).astype(
        jnp.float32
    )
    counts = jnp.sum(onehot, axis=0)
    column_pieces = two_step_exchange(deltas, (("path_0", "path_1"), "path_2"), (1, 0), 2, 0)
    totals = jnp.einsum(
        "pm,prc->mrc",
        onehot.astype(jnp.bfloat16),
        column_pieces,
        preferred_element_type=jnp.float32,
    )
    outer_grad = totals / counts[:, None, None]
    local_squares = jnp.sum(outer_grad * outer_grad, axis=(1, 2))
    norm_squares = by_axis(local_squares, (("path_0", "path_1"), ("path_2", "shard")))
    limit = clip_ratio * jnp.sqrt(jnp.float32(row_count * lax.axis_size("shard") * D))
    shrink = jnp.minimum(1.0, limit / jnp.sqrt(norm_squares + 1e-06))
    clipped = outer_grad * shrink[:, None, None]
    new_momentum = momentum_rate * momentum + clipped
    outer_step = (outer_rate * (clipped + momentum_rate * new_momentum)).astype(jnp.bfloat16)
    per_path = jnp.einsum(
        "pm,mrc->prc", onehot.astype(jnp.bfloat16), outer_step, preferred_element_type=jnp.float32
    ).astype(jnp.bfloat16)
    path_update = lax.all_to_all(per_path, PATH, split_axis=0, concat_axis=2, tiled=True)
    return (path_update, new_momentum)


def solution(mesh):
    finer = Mesh(
        mesh.devices.reshape(4, 8, 2, mesh.shape["shard"]), ("path_0", "path_1", "path_2", "shard")
    )
    in_specs = (P(PATH, "shard", None), P(None, "shard", PATH), P())
    out_specs = (P(PATH, "shard", None), P(None, "shard", PATH))
    return jax.shard_map(local, mesh=finer, in_specs=in_specs, out_specs=out_specs, check_vma=False)
```

profile of v0, /device:TPU:1, one launch (start us, length us, event | category | flops | bytes accessed | tf_op | source)
XLA Modules:
  0.0 78.6 jit_solution(14814683300214480118)
XLA Ops:
  0.6 1.2 %reshape.26 = bf16[1,16,64,64]{3,2,1,0:T(8,128)(2,1)S(1)} reshape(bf16[1,16,4096]{2,1,0:T(8,128)(2,1)} %param.3) | data formatting | bytes 262144 | tf_op jit(solution)/shard_map/reshape | solution.py:18
  1.9 0.2 reshape.29
  2.1 10.4 %all_to_all.40 = bf16[2,2,16384]{2,1,0:T(2,128)(2,1)S(1)} all-to-all(bf16[2,2,16384]{2,1,0:T(2,128)(2,1)S(1)} %reshape.29), channel_id=1, replica_groups=mesh['path_0'=4,'path_1'=8,'path_2'=2,'shard'=8] {'path_2'}, dimensions={0} | all-to-all | bytes 262144 | tf_op jit(solution)/shard_map/all_to_all | solution.py:31
  12.5 0.2 reshape.30
  12.7 0.3 copy.57
  13.0 0.8 %reshape.31 = bf16[32,2,1024]{2,1,0:T(2,128)(2,1)} reshape(bf16[32,1,16,2,64]{4,3,2,1,0:T(2,128)(2,1)S(1)} %bitcast.27) | data formatting | bytes 262144
  13.8 0.0 copy-start.1
  13.8 7.6 %all-to-all-start.1 = ((bf16[32,2,1024]{2,1,0:T(2,128)(2,1)}), bf16[32,2,1024]{2,1,0:T(2,128)(2,1)S(1)}, u32[]{:S(2)}, u32[]{:S(2)}) async-start(bf16[32,2,1024]{2,1,0:T(2,128)(2,1)} %reshape.31), calls=%async_computation.1 | async-start | bytes 262144 | tf_op jit(solution)/shard_map/all_to_all | solution.py:31
  21.5 0.0 copy-done.1
  21.5 0.1 convert_reduce_fusion
  21.6 9.0 %all-to-all-done.1 = bf16[32,2,1024]{2,1,0:T(2,128)(2,1)S(1)} async-done(((bf16[32,2,1024]{2,1,0:T(2,128)(2,1)}), bf16[32,2,1024]{2,1,0:T(2,128)(2,1)S(1)}, u32[]{:S(2)}, u32[]{:S(2)}) %all-to-all-start.1) | async-done | bytes 131104 | tf_op jit(solution)/shard_map/all_to_all | solution.py:31
  30.6 0.2 reshape.32
  30.9 0.2 copy.38
  31.1 0.0 copy-start
  31.1 0.3 multiply_reduce_fusion
  31.4 16.0 %all_to_all.41 = f32[16,1,16]{2,1,0:T(1,128)S(1)} all-to-all(f32[16,1,16]{2,1,0:T(1,128)S(1)} %broadcast_in_dim.4), channel_id=1, replica_groups=mesh['path_0'=4,'path_1'=8,'path_2'=2,'shard'=8] {'path_2','shard'}, dimensions={0} | all-to-all | bytes 2048 | tf_op jit(solution)/shard_map/all_to_all | solution.py:43
  47.4 11.9 %all_to_all.42 = f32[32,1,16]{2,1,0:T(1,128)S(1)} all-to-all(f32[32,1,16]{2,1,0:T(1,128)S(1)} %broadcast_in_dim.5), channel_id=1, replica_groups=mesh['path_0'=4,'path_1'=8,'path_2'=2,'shard'=8] {'path_0','path_1'}, dimensions={0} | all-to-all | bytes 4096 | tf_op jit(solution)/shard_map/all_to_all | solution.py:43
  59.3 0.1 reduce_sum.39
  59.4 0.0 copy-done
  59.4 0.3 convolution_convert_fusion
  59.7 0.2 copy.42
  59.8 0.8 %reshape.33 = bf16[64,2,512]{2,1,0:T(2,128)(2,1)} reshape(bf16[64,16,64]{2,1,0:T(8,128)(2,1)S(1)} %copy.42) | data formatting | bytes 262144
  60.7 6.2 %all-to-all-start.4 = ((bf16[64,2,512]{2,1,0:T(2,128)(2,1)}), bf16[64,2,512]{2,1,0:T(2,128)(2,1)S(1)}, u32[]{:S(2)}, u32[]{:S(2)}) async-start(bf16[64,2,512]{2,1,0:T(2,128)(2,1)} %reshape.33), calls=%async_computation.4 | async-start | bytes 262144 | tf_op jit(solution)/shard_map/all_to_all | solution.py:80
  66.9 0.1 fusion
  67.0 0.7 copy.44
  67.7 9.7 %all-to-all-done.4 = bf16[64,2,512]{2,1,0:T(2,128)(2,1)S(1)} async-done(((bf16[64,2,512]{2,1,0:T(2,128)(2,1)}), bf16[64,2,512]{2,1,0:T(2,128)(2,1)S(1)}, u32[]{:S(2)}, u32[]{:S(2)}) %all-to-all-start.4) | async-done | bytes 131104 | tf_op jit(solution)/shard_map/all_to_all | solution.py:80
  77.4 0.2 reshape.34
  77.6 0.1 copy.43
  77.7 0.9 %all_to_all.34 = bf16[1,16,4096]{2,1,0:T(8,128)(2,1)} reshape(bf16[1,16,64,64]{3,2,1,0:T(8,128)(2,1)S(1)} %copy.43) | data formatting | bytes 262144 | tf_op jit(solution)/shard_map/all_to_all | solution.py:80
  (5 shorter events, 0.1 us)
Async XLA Ops:
  13.8 7.7 %copy-start.1 = (s32[64]{0:T(128)S(1)}, s32[64]{0:T(128)}, u32[]{:S(2)}) copy-start(s32[64]{0:T(128)} %param.5) | copy-start | bytes 772
  13.8 16.8 %all-to-all-start.1 = ((bf16[32,2,1024]{2,1,0:T(2,128)(2,1)}), bf16[32,2,1024]{2,1,0:T(2,128)(2,1)S(1)}, u32[]{:S(2)}, u32[]{:S(2)}) async-start(bf16[32,2,1024]{2,1,0:T(2,128)(2,1)} %reshape.31), calls=%async_computation.1 | async-start | bytes 262144 | tf_op jit(solution)/shard_map/all_to_all | solution.py:31
  31.1 28.3 %copy-start = (f32[16,16,64]{2,1,0:T(8,128)S(1)}, f32[16,16,64]{2,1,0:T(8,128)}, u32[]{:S(2)}) copy-start(f32[16,16,64]{2,1,0:T(8,128)} %param.4) | copy-start | bytes 196612
  60.7 16.7 %all-to-all-start.4 = ((bf16[64,2,512]{2,1,0:T(2,128)(2,1)}), bf16[64,2,512]{2,1,0:T(2,128)(2,1)S(1)}, u32[]{:S(2)}, u32[]{:S(2)}) async-start(bf16[64,2,512]{2,1,0:T(2,128)(2,1)} %reshape.33), calls=%async_computation.4 | async-start | bytes 262144 | tf_op jit(solution)/shard_map/all_to_all | solution.py:80
where the time goes:
time: 78.9 us; the launch traced here: 78.6 us
  blocking collectives  38.2 us (48%)
  waiting for transfers between devices  18.7 us (24%)
  starting transfers between devices  13.8 us (17%)
  local copies, waits for them, and re-layouts  6.22 us (8%)
    all_to_all x2, blocking collectives, copy_for_each(): return lax.all_to_all(copies, axis, split_axis=0, concat_axis=0, tiled=True)  27.9 us
    all_to_all x1, blocking collectives, exchange_in_order(): whole = lax.all_to_all(whole, axes[k], k, k, tiled=True)  10.4 us
    all_to_all x1, waiting for transfers between devices, local(): lax.all_to_all(per_path, PATH, split_axis=0, concat_axis=2, tiled=True)  9.69 us
    all_to_all x1, waiting for transfers between devices, exchange_in_order(): whole = lax.all_to_all(whole, axes[k], k, k, tiled=True)  9.03 us
    all_to_all x1, starting transfers between devices, exchange_in_order(): whole = lax.all_to_all(whole, axes[k], k, k, tiled=True)  7.64 us
    all_to_all x1, starting transfers between devices, local(): lax.all_to_all(per_path, PATH, split_axis=0, concat_axis=2, tiled=True)  6.19 us
    unnamed x11, local copies, waits for them, and re-layouts  3.29 us
  transfers between devices with their start and end apart: 2, of which 2 were waited for; matrix products, arithmetic and copies ran while one was open for 1% of the time, Pallas kernels for 0%

commit v1 on v0

v1 whole, which is shorter than its diff:
```python
import jax
import jax.numpy as jnp
from jax import lax
from jax.experimental import pallas as pl
from jax.experimental.pallas import tpu as pltpu
from jax.sharding import Mesh
from jax.sharding import PartitionSpec as P

PATH = ("path_0", "path_1", "path_2")
TILES = ("path_2", "path_0", "path_1")

outer_rate = 0.7
momentum_rate = 0.9
clip_ratio = 2.0

GRAD, MOMENTUM, SQUARES, CHUNK = 0, 8, 16, 17
KERNEL_BYTES = 4 << 20
VMEM = pl.BlockSpec(memory_space=pltpu.VMEM)
SMEM = pl.BlockSpec(memory_space=pltpu.SMEM)


def path_of(peer, chips):
    return (peer % chips) * 2 + peer // chips


def lanes():
    return lax.broadcasted_iota(jnp.int32, (8, 128), 1)


def gather_kernel(module_ref, column_ref, momentum_ref, chunk_ref, grad_ref, *scratch):
    *sums, packed, count = scratch
    peers, modules = column_ref.shape[0], grad_ref.shape[0]
    chips = peers // 2
    for total in sums:
        total[...] = jnp.zeros_like(total)
    for m in range(modules):
        count[m] = 0
    for q in range(peers):
        m = module_ref[path_of(q, chips)]
        total = sums[q % len(sums)]
        total[m] += column_ref[q].astype(jnp.float32)
        count[m] += 1
    first_core = lax.axis_index("path_2") == 0
    for m in range(modules):
        total = sums[0][m]
        for more in sums[1:]:
            total += more[m]
        grad_ref[m] = total / count[m].astype(jnp.float32)
        top, bottom = momentum_ref[m, 0:8, :], momentum_ref[m, 8:16, :]
        packed[m] = jnp.concatenate(
            [jnp.where(first_core, top, bottom), jnp.where(first_core, bottom, top)], axis=1
        )
    grad = grad_ref[...]
    squares = jnp.sum(jnp.sum(grad * grad, axis=1), axis=1, keepdims=True)
    row = lax.broadcasted_iota(jnp.int32, (modules, 128), 0)
    lane = lax.broadcasted_iota(jnp.int32, (modules, 128), 1)
    squares = jnp.sum(jnp.where(row == lane, squares, 0.0), axis=0, keepdims=True)
    for q in range(peers):
        m = module_ref[path_of(q, chips)]
        start = q * CHUNK
        chunk_ref[start + GRAD : start + MOMENTUM, :] = grad_ref[m]
        chunk_ref[start + MOMENTUM : start + SQUARES, :] = packed[m]
        chunk_ref[start + SQUARES : start + CHUNK, :] = squares


def step_kernel(limit, module_ref, squares_ref, chunk_ref, mine_ref, other_ref, momentum_ref, update_ref, new_ref):
    peers, modules = update_ref.shape[0], mine_ref.shape[0]
    chips = peers // 2
    core = lax.axis_index("path_2")
    chip = lax.axis_index("path_0") * lax.axis_size("path_1") + lax.axis_index("path_1")
    norm_squares = jnp.sum(squares_ref[...], axis=0, keepdims=True)
    shrink = jnp.minimum(1.0, limit / jnp.sqrt(norm_squares + 1e-06))
    lane = lax.broadcasted_iota(jnp.int32, (1, 128), 1)

    def of_module(m):
        return jnp.sum(jnp.where(lane == m, shrink, 0.0), axis=1, keepdims=True)

    own = jnp.broadcast_to(of_module(module_ref[chip * 2 + core]), (8, 128))
    left = lanes() < 64
    for q in range(peers):
        half, at = q // chips, q % chips
        start = q * CHUNK
        one = chunk_ref[at * CHUNK + MOMENTUM : at * CHUNK + SQUARES, :]
        two = chunk_ref[(chips + at) * CHUNK + MOMENTUM : (chips + at) * CHUNK + SQUARES, :]
        if half == 0:
            momentum = jnp.where(left, one, two)
        else:
            momentum = pltpu.roll(jnp.where(left, two, one), 64, 1)
        clipped = chunk_ref[start + GRAD : start + MOMENTUM, :] * own
        new_momentum = momentum_rate * momentum + clipped
        step = outer_rate * (clipped + momentum_rate * new_momentum)
        update_ref[q] = step.astype(jnp.bfloat16)
    first_core = core == 0
    for m in range(modules):
        k = jnp.broadcast_to(of_module(m), (8, 128))
        for half in range(2):
            grad = jnp.where(core == half, mine_ref[m], other_ref[m]) * k
            grad = jnp.where(first_core, grad, pltpu.roll(grad, 64, 1))
            rows = slice(half * 8, half * 8 + 8)
            new_ref[m, rows, :] = momentum_rate * momentum_ref[m, rows, :] + grad[:, 0:64]


def local(deltas, momentum, path_module):
    modules, rows, _ = momentum.shape
    columns = deltas.shape[2]
    peers = lax.axis_size(PATH)
    shards = lax.axis_size("shard")
    tiles = deltas.reshape(2, 8, peers // 2, 128).transpose(0, 2, 1, 3).reshape(peers, 8, 128)
    column_tiles = lax.all_to_all(tiles, TILES, 0, 0, tiled=True)
    chunks, grad = pl.pallas_call(
        gather_kernel,
        out_shape=(
            jax.ShapeDtypeStruct((peers * CHUNK, 128), jnp.float32),
            jax.ShapeDtypeStruct((modules, 8, 128), jnp.float32),
        ),
        in_specs=[SMEM, VMEM, VMEM],
        out_specs=(VMEM, VMEM),
        scratch_shapes=[pltpu.VMEM((modules, 8, 128), jnp.float32)] * 5
        + [pltpu.SMEM((modules,), jnp.int32)],
        compiler_params=pltpu.CompilerParams(vmem_limit_bytes=KERNEL_BYTES),
        name="gather_modules",
    )(path_module, column_tiles, momentum)
    chunks = lax.all_to_all(chunks.reshape(peers, CHUNK, 1, 128), TILES, 0, 0, tiled=True)
    other = lax.ppermute(grad, "path_2", [(0, 1), (1, 0)])
    squares = jnp.sum(chunks[:, SQUARES], axis=0)
    squares = lax.all_to_all(
        jnp.broadcast_to(squares, (shards, 1, 128)), "shard", 0, 0, tiled=True
    )
    limit = clip_ratio * float(rows * shards * columns) ** 0.5
    update, new_momentum = pl.pallas_call(
        lambda *refs: step_kernel(limit, *refs),
        out_shape=(
            jax.ShapeDtypeStruct((peers, 8, 128), jnp.bfloat16),
            jax.ShapeDtypeStruct(momentum.shape, jnp.float32),
        ),
        in_specs=[SMEM, VMEM, VMEM, VMEM, VMEM, VMEM],
        out_specs=(VMEM, VMEM),
        compiler_params=pltpu.CompilerParams(vmem_limit_bytes=KERNEL_BYTES),
        name="step",
    )(
        path_module,
        squares.reshape(shards, 128),
        chunks.reshape(peers * CHUNK, 128),
        grad,
        other,
        momentum,
    )
    update = update.reshape(2, peers // 2, 8, 128).transpose(0, 2, 1, 3).reshape(deltas.shape)
    return (update, new_momentum)


def solution(mesh):
    finer = Mesh(
        mesh.devices.reshape(4, 8, 2, mesh.shape["shard"]), ("path_0", "path_1", "path_2", "shard")
    )
    in_specs = (P(PATH, "shard", None), P(None, "shard", PATH), P())
    out_specs = (P(PATH, "shard", None), P(None, "shard", PATH))
    return jax.shard_map(local, mesh=finer, in_specs=in_specs, out_specs=out_specs, check_vma=False)
```

time: 78.9 us -> 69.8 us (0.88)
  blocking collectives: 38.2 us -> 25.8 us
  local copies, waits for them, and re-layouts: 6.22 us -> 0.61 us
  waiting for transfers between devices: 18.7 us -> 23.5 us
  Pallas kernels: 0 us -> 3.92 us
  starting transfers between devices: 13.8 us -> 14.6 us
    all_to_all x3 -> x1, blocking collectives: 38.2 us -> 25.8 us  [local(): column_tiles = lax.all_to_all(tiles, TILES, 0, 0, tiled=True)]
    all_to_all x2, waiting for transfers between devices: 18.7 us -> 23.5 us  [the longest x1 17.1 us: local(): lax.all_to_all(chunks.reshape(peers, CHUNK, 1, 128), TILES, 0, 0, tiled=T...]
    pallas_call x0 -> x2, Pallas kernels: none -> 3.92 us  [the longest x1 2.11 us: local(): pl.pallas_call(lambda *refs: step_kernel(limit, *refs), out_shape=(jax.Sh...]
    unnamed x11 -> x4, local copies, waits for them, and re-layouts: 3.29 us -> 0.01 us
    ppermute x0 -> x1, starting transfers between devices: none -> 2.26 us  [local(): other = lax.ppermute(grad, 'path_2', [(0, 1), (1, 0)])]
    all_to_all x4 -> x0, local copies, waits for them, and re-layouts: 1.51 us -> none  [the longest x2 1 us: local(): lax.all_to_all(per_path, PATH, split_axis=0, concat_axis=2, tiled=True)]
    all_to_all x2, starting transfers between devices: 13.8 us -> 12.4 us  [the longest x1 6.82 us: local(): lax.all_to_all(jnp.broadcast_to(squares, (shards, 1, 128)), 'shard', 0, 0...]
    reshape x2 -> x0, local copies, waits for them, and re-layouts: 1.22 us -> none  [the longest x1 1.18 us: cut_along(): return jnp.moveaxis(array.reshape(*before, peers, -1, *after), dim, 0)]
  transfers between devices with their start and end apart: 2 -> 3, of which waited for: 2 -> 2; matrix products, arithmetic and copies ran while one was open for 1% -> 1% of each run, Pallas kernels for 0% -> 0%
where the time goes in v1:
time: 69.8 us; the launch traced here: 69.2 us
  blocking collectives  25.8 us (37%)
  waiting for transfers between devices  23.5 us (34%)
  starting transfers between devices  14.6 us (21%)
  Pallas kernels  3.92 us (6%)
    all_to_all x1, blocking collectives, local(): column_tiles = lax.all_to_all(tiles, TILES, 0, 0, tiled=True)  25.8 us
    all_to_all x1, waiting for transfers between devices, local(): lax.all_to_all(chunks.reshape(peers, CHUNK, 1, 128), TILES, 0, 0, tiled=T...  17.1 us
    all_to_all x1, starting transfers between devices, local(): lax.all_to_all(jnp.broadcast_to(squares, (shards, 1, 128)), 'shard', 0, 0...  6.82 us
    all_to_all x1, waiting for transfers between devices, local(): lax.all_to_all(jnp.broadcast_to(squares, (shards, 1, 128)), 'shard', 0, 0...  6.45 us
    all_to_all x1, starting transfers between devices, local(): lax.all_to_all(chunks.reshape(peers, CHUNK, 1, 128), TILES, 0, 0, tiled=T...  5.54 us
    ppermute x1, starting transfers between devices, local(): other = lax.ppermute(grad, 'path_2', [(0, 1), (1, 0)])  2.26 us
    pallas_call x1, Pallas kernels, local(): pl.pallas_call(lambda *refs: step_kernel(limit, *refs), out_shape=(jax.Sh...  2.11 us
    pallas_call x1, Pallas kernels, local(): pl.pallas_call(gather_kernel, out_shape=(jax.ShapeDtypeStruct((peers * CH...  1.81 us
  transfers between devices with their start and end apart: 3, of which 2 were waited for; matrix products, arithmetic and copies ran while one was open for 1% of the time, Pallas kernels for 0%

profile of v1, /device:TPU:1, one launch (start us, length us, event | category | flops | bytes accessed | tf_op | source)
XLA Modules:
  0.0 69.2 jit_solution(5584183034933922586)
XLA Ops:
  0.6 0.0 copy-start
  0.6 0.0 copy-start.1
  0.6 25.8 %all_to_all.15.column_ref = bf16[64,8,128]{2,1,0:T(8,128)(2,1)S(1)} all-to-all(bf16[64,8,128]{2,1,0:T(8,128)(2,1)} %bitcast.15), channel_id=1, replica_groups=mesh['path_0'=4,'path_1'=8,'path_2'=2,'shard'=8] {'path_2','path_0','pat..., dimensions={0} | all-to-all | bytes 262144 | tf_op jit(solution)/shard_map/all_to_all | solution.py:109
  26.5 0.0 copy-done
  26.5 0.0 copy-done.1
  26.5 1.8 %gather_modules.1 = (f32[1088,128]{1,0:T(8,128)}, f32[16,8,128]{2,1,0:T(8,128)S(1)}) custom-call(s32[64]{0:T(128)S(1)} %copy-done.1, bf16[64,8,128]{2,1,0:T(8,128)(2,1)S(1)} %all_to_all.15.column_ref, f32[16,16,64]{2,1,0:T(8,128)S(1)} %copy-done), custom_call_target="tpu_custom_call" | custom-call | tf_op jit(solution)/shard_map/gather_modules/pallas_call | solution.py:110
  28.3 5.5 %all-to-all-start.1 = ((f32[64,17,1,128]{3,2,1,0:T(1,128)}), f32[64,17,1,128]{3,2,1,0:T(1,128)S(1)}, u32[]{:S(2)}, u32[]{:S(2)}) async-start(f32[64,17,1,128]{3,2,1,0:T(1,128)} %bitcast.3), calls=%async_computation.1 | async-start | bytes 1114112 | tf_op jit(solution)/shard_map/all_to_all | solution.py:123
  33.8 2.3 %collective-permute-start = (f32[16,8,128]{2,1,0:T(8,128)S(1)}, f32[16,8,128]{2,1,0:T(8,128)S(1)}, u32[]{:S(2)}, u32[]{:S(2)}) collective-permute-start(f32[16,8,128]{2,1,0:T(8,128)S(1)} %get-tuple-element.7.refs_3_), channel_id=1, source_target_pairs={{0,8},{8,0},{1,9},{9,1},{2,10},{10,2},{3,11},{11,3},{4,12},{12,4},... | collective-permute-start | bytes 196616 | tf_op jit(solution)/shard_map/ppermute | solution.py:124
  36.1 17.1 %all-to-all-done.1 = f32[64,17,1,128]{3,2,1,0:T(1,128)S(1)} async-done(((f32[64,17,1,128]{3,2,1,0:T(1,128)}), f32[64,17,1,128]{3,2,1,0:T(1,128)S(1)}, u32[]{:S(2)}, u32[]{:S(2)}) %all-to-all-start.1) | async-done | bytes 557088 | tf_op jit(solution)/shard_map/all_to_all | solution.py:123
  53.1 0.1 slice_reduce_fusion
  53.2 0.6 broadcast_in_dim.3
  53.8 6.8 %all-to-all-start.2 = ((f32[8,1,128]{2,1,0:T(1,128)}), f32[8,1,128]{2,1,0:T(1,128)S(1)}, u32[]{:S(2)}, u32[]{:S(2)}) async-start(f32[8,1,128]{2,1,0:T(1,128)} %broadcast_in_dim.3), calls=%async_computation.2 | async-start | bytes 8192 | tf_op jit(solution)/shard_map/all_to_all | solution.py:126
  60.6 0.0 collective-permute-done.refs_4_
  60.7 6.4 %all-to-all-done.2 = f32[8,1,128]{2,1,0:T(1,128)S(1)} async-done(((f32[8,1,128]{2,1,0:T(1,128)}), f32[8,1,128]{2,1,0:T(1,128)S(1)}, u32[]{:S(2)}, u32[]{:S(2)}) %all-to-all-start.2) | async-done | bytes 4128 | tf_op jit(solution)/shard_map/all_to_all | solution.py:126
  67.1 2.1 %step.1 = (bf16[64,8,128]{2,1,0:T(8,128)(2,1)}, f32[16,16,64]{2,1,0:T(8,128)}) custom-call(s32[64]{0:T(128)S(1)} %copy-done.1, f32[8,128]{1,0:T(8,128)S(1)} %bitcast.14, f32[1088,128]{1,0:T(8,128)S(1)} %bitcast.13, f32[16,8,128]{2,1,0:T(8,128)S(1)} %get-tuple-element.7.refs_3_, f32[16,8,128]{2,1,0:T(8,128)S(1)} %collective-permute-done.refs_4_, ...), custom_call_target="tpu_custom_call" | custom-call | tf_op jit(solution)/shard_map/step/pallas_call | solution.py:130
Async XLA Ops:
  0.6 25.8 %copy-start = (f32[16,16,64]{2,1,0:T(8,128)S(1)}, f32[16,16,64]{2,1,0:T(8,128)}, u32[]{:S(2)}) copy-start(f32[16,16,64]{2,1,0:T(8,128)} %refs_5_.1) | copy-start | bytes 196612
  0.6 25.8 %copy-start.1 = (s32[64]{0:T(128)S(1)}, s32[64]{0:T(128)}, u32[]{:S(2)}) copy-start(s32[64]{0:T(128)} %refs_0_.1) | copy-start | bytes 772
  28.3 24.9 %all-to-all-start.1 = ((f32[64,17,1,128]{3,2,1,0:T(1,128)}), f32[64,17,1,128]{3,2,1,0:T(1,128)S(1)}, u32[]{:S(2)}, u32[]{:S(2)}) async-start(f32[64,17,1,128]{3,2,1,0:T(1,128)} %bitcast.3), calls=%async_computation.1 | async-start | bytes 1114112 | tf_op jit(solution)/shard_map/all_to_all | solution.py:123
  33.8 26.8 %collective-permute-start = (f32[16,8,128]{2,1,0:T(8,128)S(1)}, f32[16,8,128]{2,1,0:T(8,128)S(1)}, u32[]{:S(2)}, u32[]{:S(2)}) collective-permute-start(f32[16,8,128]{2,1,0:T(8,128)S(1)} %get-tuple-element.7.refs_3_), channel_id=1, source_target_pairs={{0,8},{8,0},{1,9},{9,1},{2,10},{10,2},{3,11},{11,3},{4,12},{12,4},... | collective-permute-start | bytes 196616 | tf_op jit(solution)/shard_map/ppermute | solution.py:124
  53.8 13.3 %all-to-all-start.2 = ((f32[8,1,128]{2,1,0:T(1,128)}), f32[8,1,128]{2,1,0:T(1,128)S(1)}, u32[]{:S(2)}, u32[]{:S(2)}) async-start(f32[8,1,128]{2,1,0:T(1,128)} %broadcast_in_dim.3), calls=%async_computation.2 | async-start | bytes 8192 | tf_op jit(solution)/shard_map/all_to_all | solution.py:126

commit v2 on v1

v2 whole, which is shorter than its diff:
```python
import jax
import jax.numpy as jnp
from jax import lax
from jax.experimental import pallas as pl
from jax.experimental.pallas import tpu as pltpu
from jax.sharding import Mesh
from jax.sharding import PartitionSpec as P

PATH = ("path_0", "path_1", "path_2")
TILES = ("path_2", "path_0", "path_1")

outer_rate = 0.7
momentum_rate = 0.9
clip_ratio = 2.0

GRAD, MOMENTUM, SQUARES, CHUNK = 0, 8, 16, 17
KERNEL_BYTES = 4 << 20
VMEM = pl.BlockSpec(memory_space=pltpu.VMEM)
SMEM = pl.BlockSpec(memory_space=pltpu.SMEM)
HBM = pl.BlockSpec(memory_space=pl.ANY)
PIECES = 4


def path_of(peer, chips):
    return (peer % chips) * 2 + peer // chips


def kernel(body, name, **kwargs):
    params = pltpu.CompilerParams(vmem_limit_bytes=KERNEL_BYTES)
    return pl.pallas_call(body, name=name, compiler_params=params, **kwargs)


def momentum_kernel(module_ref, momentum_ref, chunk_ref, packed):
    first_core = lax.axis_index("path_2") == 0
    for m in range(momentum_ref.shape[0]):
        top, bottom = momentum_ref[m, 0:8, :], momentum_ref[m, 8:16, :]
        packed[m] = jnp.concatenate(
            [jnp.where(first_core, top, bottom), jnp.where(first_core, bottom, top)], axis=1
        )
    peers = chunk_ref.shape[0] // CHUNK
    for q in range(peers):
        start = q * CHUNK
        m = module_ref[path_of(q, peers // 2)]
        chunk_ref[start + MOMENTUM : start + SQUARES, :] = packed[m]


def gather_kernel(module_ref, column_ref, _, chunk_ref, chunk_out, grad_ref, *scratch):
    *sums, count, sems = scratch
    peers, modules = column_ref.shape[0], grad_ref.shape[0]
    chips = peers // 2
    for total in sums:
        total[...] = jnp.zeros_like(total)
    for m in range(modules):
        count[m] = 0
    for q in range(peers):
        m = module_ref[path_of(q, chips)]
        total = sums[q % len(sums)]
        total[m] += column_ref[q].astype(jnp.float32)
        count[m] += 1
    for m in range(modules):
        total = sums[0][m]
        for more in sums[1:]:
            total += more[m]
        grad_ref[m] = total / count[m].astype(jnp.float32)
    grad = grad_ref[...]
    squares = jnp.sum(jnp.sum(grad * grad, axis=1), axis=1, keepdims=True)
    row = lax.broadcasted_iota(jnp.int32, (modules, 128), 0)
    lane = lax.broadcasted_iota(jnp.int32, (modules, 128), 1)
    squares = jnp.sum(jnp.where(row == lane, squares, 0.0), axis=0, keepdims=True)
    copies = []
    for q in range(peers):
        m = module_ref[path_of(q, chips)]
        start = q * CHUNK
        chunk_ref[start + GRAD : start + MOMENTUM, :] = grad_ref[m]
        chunk_ref[start + SQUARES : start + CHUNK, :] = squares
        if (q + 1) % (peers // PIECES) == 0:
            piece = pl.ds(len(copies) * (peers // PIECES) * CHUNK, (peers // PIECES) * CHUNK)
            sem = sems.at[len(copies)]
            copies.append(pltpu.make_async_copy(chunk_ref.at[piece], chunk_out.at[piece], sem))
            copies[-1].start()
    for copy in copies:
        copy.wait()


def assemble_kernel(
    module_ref, chunk_ref, mine_ref, other_ref, grad_ref, decay_ref, own_grad_ref, own_ref
):
    peers, modules = grad_ref.shape[0], mine_ref.shape[0]
    chips = peers // 2
    core = lax.axis_index("path_2")
    chip = lax.axis_index("path_0") * lax.axis_size("path_1") + lax.axis_index("path_1")
    left = lax.broadcasted_iota(jnp.int32, (8, 128), 1) < 64
    for at in range(chips):
        first, second = at * CHUNK, (chips + at) * CHUNK
        grad_ref[at] = chunk_ref[first + GRAD : first + MOMENTUM, :]
        grad_ref[chips + at] = chunk_ref[second + GRAD : second + MOMENTUM, :]
        one = chunk_ref[first + MOMENTUM : first + SQUARES, :]
        two = chunk_ref[second + MOMENTUM : second + SQUARES, :]
        decay_ref[at] = momentum_rate * jnp.where(left, one, two)
        decay_ref[chips + at] = momentum_rate * pltpu.roll(jnp.where(left, two, one), 64, 1)
    for m in range(modules):
        for half in range(2):
            grad = jnp.where(core == half, mine_ref[m], other_ref[m])
            grad = jnp.where(core == 0, grad, pltpu.roll(grad, 64, 1))
            own_grad_ref[m, half * 8 : half * 8 + 8, :] = grad[:, 0:64]
    lane = lax.broadcasted_iota(jnp.int32, (1, 128), 1)
    own_ref[...] = (lane == module_ref[chip * 2 + core]).astype(jnp.float32)


def step_kernel(
    limit, squares_ref, grad_ref, decay_ref, own_grad_ref, own_ref, momentum_ref,
    update_out, new_out, update, new, sems,
):
    peers, modules = update.shape[0], new.shape[0]
    norm_squares = jnp.sum(squares_ref[...], axis=0, keepdims=True)
    shrink = jnp.minimum(1.0, limit / jnp.sqrt(norm_squares + 1e-06))
    own = jnp.sum(shrink * own_ref[...], axis=1, keepdims=True)
    each = peers // PIECES
    copies = []
    for piece in range(PIECES):
        tiles = slice(piece * each, (piece + 1) * each)
        clipped = grad_ref[tiles] * own.reshape(1, 1, 1)
        step = outer_rate * (clipped + momentum_rate * (decay_ref[tiles] + clipped))
        update[tiles] = step.astype(jnp.bfloat16)
        copies.append(pltpu.make_async_copy(update.at[tiles], update_out.at[tiles], sems.at[piece]))
        copies[-1].start()
    lane = lax.broadcasted_iota(jnp.int32, (1, 128), 1)
    for m in range(modules):
        k = jnp.sum(jnp.where(lane == m, shrink, 0.0), axis=1, keepdims=True)
        new[m] = momentum_rate * momentum_ref[m] + own_grad_ref[m] * k
    copies.append(pltpu.make_async_copy(new, new_out, sems.at[PIECES]))
    copies[-1].start()
    for copy in copies:
        copy.wait()


def local(deltas, momentum, path_module):
    modules, rows, width = momentum.shape
    columns = deltas.shape[2]
    peers = lax.axis_size(PATH)
    shards = lax.axis_size("shard")
    shape = jax.ShapeDtypeStruct
    tiles = deltas.reshape(2, 8, peers // 2, 128).transpose(0, 2, 1, 3).reshape(peers, 8, 128)
    column_tiles = lax.all_to_all(tiles, TILES, 0, 0, tiled=True)
    chunks = kernel(
        momentum_kernel,
        "pack_momentum",
        out_shape=shape((peers * CHUNK, 128), jnp.float32),
        in_specs=[SMEM, VMEM],
        out_specs=VMEM,
        scratch_shapes=[pltpu.VMEM((modules, 8, 128), jnp.float32)],
    )(path_module, momentum)
    _, chunks, grad = kernel(
        gather_kernel,
        "gather_modules",
        out_shape=(
            shape((peers * CHUNK, 128), jnp.float32),
            shape((peers * CHUNK, 128), jnp.float32),
            shape((modules, 8, 128), jnp.float32),
        ),
        in_specs=[SMEM, VMEM, VMEM],
        out_specs=(VMEM, HBM, VMEM),
        input_output_aliases={2: 0},
        scratch_shapes=[pltpu.VMEM((modules, 8, 128), jnp.float32)] * 4
        + [pltpu.SMEM((modules,), jnp.int32), pltpu.SemaphoreType.DMA((PIECES,))],
    )(path_module, column_tiles, chunks)
    chunks = lax.all_to_all(chunks.reshape(peers, CHUNK, 1, 128), TILES, 0, 0, tiled=True)
    other = lax.ppermute(grad, "path_2", [(0, 1), (1, 0)])
    chunks, other = lax.optimization_barrier((chunks, other))
    squares = jnp.sum(chunks[:, SQUARES], axis=0)
    squares = lax.all_to_all(
        jnp.broadcast_to(squares, (shards, 1, 128)), "shard", 0, 0, tiled=True
    )
    path_tiles = shape((peers, 8, 128), jnp.float32)
    assembled = kernel(
        assemble_kernel,
        "assemble",
        out_shape=(
            path_tiles,
            path_tiles,
            shape(momentum.shape, jnp.float32),
            shape((1, 128), jnp.float32),
        ),
        in_specs=[SMEM, VMEM, VMEM, VMEM],
        out_specs=(VMEM,) * 4,
    )(path_module, chunks.reshape(peers * CHUNK, 128), grad, other)
    limit = clip_ratio * float(rows * shards * columns) ** 0.5
    update, new_momentum = kernel(
        lambda *refs: step_kernel(limit, *refs),
        "step",
        out_shape=(
            shape((peers, 8, 128), jnp.bfloat16),
            shape(momentum.shape, jnp.float32),
        ),
        in_specs=[VMEM] * 6,
        out_specs=(HBM, HBM),
        scratch_shapes=[
            pltpu.VMEM((peers, 8, 128), jnp.bfloat16),
            pltpu.VMEM(momentum.shape, jnp.float32),
            pltpu.SemaphoreType.DMA((PIECES + 1,)),
        ],
    )(squares.reshape(shards, 128), *assembled, momentum)
    update = update.reshape(2, peers // 2, 8, 128).transpose(0, 2, 1, 3).reshape(deltas.shape)
    return (update, new_momentum)


def solution(mesh):
    finer = Mesh(
        mesh.devices.reshape(4, 8, 2, mesh.shape["shard"]), ("path_0", "path_1", "path_2", "shard")
    )
    in_specs = (P(PATH, "shard", None), P(None, "shard", PATH), P())
    out_specs = (P(PATH, "shard", None), P(None, "shard", PATH))
    return jax.shard_map(local, mesh=finer, in_specs=in_specs, out_specs=out_specs, check_vma=False)
```

time: 69.8 us -> 68.6 us (0.983)
  blocking collectives: 25.8 us -> 0 us
  starting transfers between devices: 14.6 us -> 29.7 us
  waiting for transfers between devices: 23.5 us -> 32.9 us
    all_to_all x1 -> x0, blocking collectives: 25.8 us -> none  [local(): column_tiles = lax.all_to_all(tiles, TILES, 0, 0, tiled=True)]
    all_to_all x0 -> x1, starting transfers between devices: none -> 15.1 us  [local(): column_tiles = lax.all_to_all(tiles, TILES, 0, 0, tiled=True)]
    all_to_all x0 -> x1, waiting for transfers between devices: none -> 10 us  [local(): column_tiles = lax.all_to_all(tiles, TILES, 0, 0, tiled=True)]
    all_to_all x1, waiting for transfers between devices: 17.1 us -> 16.2 us  [local(): lax.all_to_all(chunks.reshape(peers, CHUNK, 1, 128), TILES, 0, 0, tiled=T...]
    ppermute x1, waiting for transfers between devices: 0.01 us -> 0.88 us  [local(): other = lax.ppermute(grad, 'path_2', [(0, 1), (1, 0)])]
    pallas_call x2 -> x4, Pallas kernels: 3.92 us -> 4.01 us  [the longest x1 1.78 us: local(): kernel(gather_kernel, 'gather_modules', out_shape=(shape((peers * CHUNK,...]
  transfers between devices with their start and end apart: 3 -> 4, of which waited for: 2 -> 4; matrix products, arithmetic and copies ran while one was open for 1% -> 0% of each run, Pallas kernels for 0% -> 2%
where the time goes in v2:
time: 68.6 us; the launch traced here: 68 us
  waiting for transfers between devices  32.9 us (48%)
  starting transfers between devices  29.7 us (43%)
  Pallas kernels  4.01 us (6%)
  between operations  0.71 us (1%)
    all_to_all x1, waiting for transfers between devices, local(): lax.all_to_all(chunks.reshape(peers, CHUNK, 1, 128), TILES, 0, 0, tiled=T...  16.2 us
    all_to_all x1, starting transfers between devices, local(): column_tiles = lax.all_to_all(tiles, TILES, 0, 0, tiled=True)  15.1 us
    all_to_all x1, waiting for transfers between devices, local(): column_tiles = lax.all_to_all(tiles, TILES, 0, 0, tiled=True)  10 us
    all_to_all x1, starting transfers between devices, local(): lax.all_to_all(jnp.broadcast_to(squares, (shards, 1, 128)), 'shard', 0, 0...  6.82 us
    all_to_all x1, waiting for transfers between devices, local(): lax.all_to_all(jnp.broadcast_to(squares, (shards, 1, 128)), 'shard', 0, 0...  5.78 us
    all_to_all x1, starting transfers between devices, local(): lax.all_to_all(chunks.reshape(peers, CHUNK, 1, 128), TILES, 0, 0, tiled=T...  5.55 us
    ppermute x1, starting transfers between devices, local(): other = lax.ppermute(grad, 'path_2', [(0, 1), (1, 0)])  2.26 us
    pallas_call x1, Pallas kernels, local(): kernel(gather_kernel, 'gather_modules', out_shape=(shape((peers * CHUNK,...  1.78 us
  transfers between devices with their start and end apart: 4, of which 4 were waited for; matrix products, arithmetic and copies ran while one was open for 0% of the time, Pallas kernels for 2%

profile of v2, /device:TPU:1, one launch (start us, length us, event | category | flops | bytes accessed | tf_op | source)
XLA Modules:
  0.0 68.0 jit_solution(8852039867730642977)
XLA Ops:
  0.6 0.0 copy-start
  0.6 0.0 copy-start.1
  0.6 15.1 %all-to-all-start = ((bf16[64,8,128]{2,1,0:T(8,128)(2,1)}), bf16[64,8,128]{2,1,0:T(8,128)(2,1)S(1)}, u32[]{:S(2)}, u32[]{:S(2)}) async-start(bf16[64,8,128]{2,1,0:T(8,128)(2,1)} %bitcast.15), calls=%async_computation | async-start | bytes 262144 | tf_op jit(solution)/shard_map/all_to_all | solution.py:144
  15.7 0.0 copy-done
  15.7 0.0 copy-done.1
  15.8 0.7 %pack_momentum.1._ = f32[1088,128]{1,0:T(8,128)S(1)} custom-call(s32[64]{0:T(128)S(1)} %copy-done.1, f32[16,16,64]{2,1,0:T(8,128)S(1)} %copy-done), custom_call_target="tpu_custom_call" | custom-call | tf_op jit(solution)/shard_map/pack_momentum/pallas_call | solution.py:145
  16.4 10.0 %all-to-all-done.column_ref = bf16[64,8,128]{2,1,0:T(8,128)(2,1)S(1)} async-done(((bf16[64,8,128]{2,1,0:T(8,128)(2,1)}), bf16[64,8,128]{2,1,0:T(8,128)(2,1)S(1)}, u32[]{:S(2)}, u32[]{:S(2)}) %all-to-all-start) | async-done | bytes 131104 | tf_op jit(solution)/shard_map/all_to_all | solution.py:144
  26.5 1.8 %gather_modules.1 = (f32[1088,128]{1,0:T(8,128)S(1)}, f32[1088,128]{1,0:T(8,128)}, f32[16,8,128]{2,1,0:T(8,128)S(1)}) custom-call(s32[64]{0:T(128)S(1)} %copy-done.1, bf16[64,8,128]{2,1,0:T(8,128)(2,1)S(1)} %all-to-all-done.column_ref, f32[1088,128]{1,0:T(8,128)S(1)} %pack_momentum.1._), custom_call_target="tpu_custom_call", output_to_operand_aliasing={{0}: (2, {})} | custom-call | tf_op jit(solution)/shard_map/gather_modules/pallas_call | solution.py:153
  28.3 5.5 %all-to-all-start.1 = ((f32[64,17,1,128]{3,2,1,0:T(1,128)}), f32[64,17,1,128]{3,2,1,0:T(1,128)S(1)}, u32[]{:S(2)}, u32[]{:S(2)}) async-start(f32[64,17,1,128]{3,2,1,0:T(1,128)} %bitcast.3), calls=%async_computation.1 | async-start | bytes 1114112 | tf_op jit(solution)/shard_map/all_to_all | solution.py:167
  33.8 2.3 %collective-permute-start = (f32[16,8,128]{2,1,0:T(8,128)S(1)}, f32[16,8,128]{2,1,0:T(8,128)S(1)}, u32[]{:S(2)}, u32[]{:S(2)}) collective-permute-start(f32[16,8,128]{2,1,0:T(8,128)S(1)} %get-tuple-element.13.mine_ref), channel_id=1, source_target_pairs={{0,8},{8,0},{1,9},{9,1},{2,10},{10,2},{3,11},{11,3},{4,12},{12,4},... | collective-permute-start | bytes 196616 | tf_op jit(solution)/shard_map/ppermute | solution.py:168
  36.1 0.9 %collective-permute-done.other_ref = f32[16,8,128]{2,1,0:T(8,128)S(1)} collective-permute-done((f32[16,8,128]{2,1,0:T(8,128)S(1)}, f32[16,8,128]{2,1,0:T(8,128)S(1)}, u32[]{:S(2)}, u32[]{:S(2)}) %collective-permute-start) | collective-permute-done | bytes 65568 | tf_op jit(solution)/shard_map/ppermute | solution.py:168
  37.0 16.2 %all-to-all-done.1 = f32[64,17,1,128]{3,2,1,0:T(1,128)S(1)} async-done(((f32[64,17,1,128]{3,2,1,0:T(1,128)}), f32[64,17,1,128]{3,2,1,0:T(1,128)S(1)}, u32[]{:S(2)}, u32[]{:S(2)}) %all-to-all-start.1) | async-done | bytes 557088 | tf_op jit(solution)/shard_map/all_to_all | solution.py:167
  53.1 0.1 slice_reduce_fusion
  53.2 0.6 broadcast_in_dim.3
  53.8 6.8 %all-to-all-start.2 = ((f32[8,1,128]{2,1,0:T(1,128)}), f32[8,1,128]{2,1,0:T(1,128)S(1)}, u32[]{:S(2)}, u32[]{:S(2)}) async-start(f32[8,1,128]{2,1,0:T(1,128)} %broadcast_in_dim.3), calls=%async_computation.2 | async-start | bytes 8192 | tf_op jit(solution)/shard_map/all_to_all | solution.py:171
  60.6 0.7 assemble.1
  61.3 5.8 %all-to-all-done.2 = f32[8,1,128]{2,1,0:T(1,128)S(1)} async-done(((f32[8,1,128]{2,1,0:T(1,128)}), f32[8,1,128]{2,1,0:T(1,128)S(1)}, u32[]{:S(2)}, u32[]{:S(2)}) %all-to-all-start.2) | async-done | bytes 4128 | tf_op jit(solution)/shard_map/all_to_all | solution.py:171
  67.1 0.9 %step.1 = (bf16[64,8,128]{2,1,0:T(8,128)(2,1)}, f32[16,16,64]{2,1,0:T(8,128)}) custom-call(f32[8,128]{1,0:T(8,128)S(1)} %bitcast.14, f32[64,8,128]{2,1,0:T(8,128)S(1)} %get-tuple-element.16.refs_1_, f32[64,8,128]{2,1,0:T(8,128)S(1)} %get-tuple-element.17.refs_2_, f32[16,16,64]{2,1,0:T(8,128)S(1)} %get-tuple-element.18.refs_3_, ...), custom_call_target="tpu_custom_call" | custom-call | tf_op jit(solution)/shard_map/step/pallas_call | solution.py:188
Async XLA Ops:
  0.6 15.1 %copy-start = (f32[16,16,64]{2,1,0:T(8,128)S(1)}, f32[16,16,64]{2,1,0:T(8,128)}, u32[]{:S(2)}) copy-start(f32[16,16,64]{2,1,0:T(8,128)} %refs_5_.1) | copy-start | bytes 196612
  0.6 15.1 %copy-start.1 = (s32[64]{0:T(128)S(1)}, s32[64]{0:T(128)}, u32[]{:S(2)}) copy-start(s32[64]{0:T(128)} %module_ref.5) | copy-start | bytes 772
  0.6 25.8 %all-to-all-start = ((bf16[64,8,128]{2,1,0:T(8,128)(2,1)}), bf16[64,8,128]{2,1,0:T(8,128)(2,1)S(1)}, u32[]{:S(2)}, u32[]{:S(2)}) async-start(bf16[64,8,128]{2,1,0:T(8,128)(2,1)} %bitcast.15), calls=%async_computation | async-start | bytes 262144 | tf_op jit(solution)/shard_map/all_to_all | solution.py:144
  28.3 24.9 %all-to-all-start.1 = ((f32[64,17,1,128]{3,2,1,0:T(1,128)}), f32[64,17,1,128]{3,2,1,0:T(1,128)S(1)}, u32[]{:S(2)}, u32[]{:S(2)}) async-start(f32[64,17,1,128]{3,2,1,0:T(1,128)} %bitcast.3), calls=%async_computation.1 | async-start | bytes 1114112 | tf_op jit(solution)/shard_map/all_to_all | solution.py:167
  33.8 3.2 %collective-permute-start = (f32[16,8,128]{2,1,0:T(8,128)S(1)}, f32[16,8,128]{2,1,0:T(8,128)S(1)}, u32[]{:S(2)}, u32[]{:S(2)}) collective-permute-start(f32[16,8,128]{2,1,0:T(8,128)S(1)} %get-tuple-element.13.mine_ref), channel_id=1, source_target_pairs={{0,8},{8,0},{1,9},{9,1},{2,10},{10,2},{3,11},{11,3},{4,12},{12,4},... | collective-permute-start | bytes 196616 | tf_op jit(solution)/shard_map/ppermute | solution.py:168
  53.8 13.3 %all-to-all-start.2 = ((f32[8,1,128]{2,1,0:T(1,128)}), f32[8,1,128]{2,1,0:T(1,128)S(1)}, u32[]{:S(2)}, u32[]{:S(2)}) async-start(f32[8,1,128]{2,1,0:T(1,128)} %broadcast_in_dim.3), calls=%async_computation.2 | async-start | bytes 8192 | tf_op jit(solution)/shard_map/all_to_all | solution.py:171

commit v3 on v2

--- a/solution.py
+++ b/solution.py
@@ -13,7 +13,11 @@
 momentum_rate = 0.9
 clip_ratio = 2.0
 
-GRAD, MOMENTUM, SQUARES, CHUNK = 0, 8, 16, 17
+LOW, SQUARES, CHUNK = 8, 10, 11
+GRAD_BITS = 23
+MOMENTUM_SCALE = 8191.0
+SQUARES_SCALE = 128.0
+FOLD = momentum_rate * momentum_rate / (1.0 + momentum_rate)
 KERNEL_BYTES = 4 << 20
 VMEM = pl.BlockSpec(memory_space=pltpu.VMEM)
 SMEM = pl.BlockSpec(memory_space=pltpu.SMEM)
@@ -30,22 +34,39 @@
     return pl.pallas_call(body, name=name, compiler_params=params, **kwargs)
 
 
-def momentum_kernel(module_ref, momentum_ref, chunk_ref, packed):
+def nearest(x):
+    return jnp.floor(x + 0.5).astype(jnp.int32)
+
+
+def momentum_kernel(module_ref, mine_ref, other_ref, chunk_ref, high_ref, fold_ref, low):
     first_core = lax.axis_index("path_2") == 0
-    for m in range(momentum_ref.shape[0]):
-        top, bottom = momentum_ref[m, 0:8, :], momentum_ref[m, 8:16, :]
-        packed[m] = jnp.concatenate(
-            [jnp.where(first_core, top, bottom), jnp.where(first_core, bottom, top)], axis=1
+    row = lax.broadcasted_iota(jnp.int32, (8, 128), 0)
+    for m in range(mine_ref.shape[0]):
+        mine = jnp.where(first_core, mine_ref[m, 0:8, :], mine_ref[m, 8:16, :])
+        other = jnp.where(first_core, other_ref[m, 0:8, :], other_ref[m, 8:16, :])
+        momentum = jnp.concatenate(
+            [jnp.where(first_core, mine, other), jnp.where(first_core, other, mine)], axis=1
         )
+        whole = nearest(momentum * MOMENTUM_SCALE)
+        fold_ref[m] = FOLD * (momentum - whole.astype(jnp.float32) * (1.0 / MOMENTUM_SCALE))
+        whole += 32768
+        high_ref[m] = whole >> 8
+        word = (whole & 255) << ((row & 3) * 8)
+        word = word | pltpu.roll(word, 7, 0)
+        word = word | pltpu.roll(word, 6, 0)
+        low[m, 0:1, :] = word[0:1, :]
+        low[m, 1:2, :] = word[4:5, :]
     peers = chunk_ref.shape[0] // CHUNK
     for q in range(peers):
         start = q * CHUNK
         m = module_ref[path_of(q, peers // 2)]
-        chunk_ref[start + MOMENTUM : start + SQUARES, :] = packed[m]
-
-
-def gather_kernel(module_ref, column_ref, _, chunk_ref, chunk_out, grad_ref, *scratch):
-    *sums, count, sems = scratch
+        chunk_ref[start + LOW : start + SQUARES, :] = low[m, 0:2, :]
+
+
+def gather_kernel(
+    module_ref, column_ref, high_ref, fold_ref, _, chunk_ref, chunk_out, grad_ref, *scratch
+):
+    *sums, words, count, sems = scratch
     peers, modules = column_ref.shape[0], grad_ref.shape[0]
     chips = peers // 2
     for total in sums:
@@ -64,15 +85,24 @@
         grad_ref[m] = total / count[m].astype(jnp.float32)
     grad = grad_ref[...]
     squares = jnp.sum(jnp.sum(grad * grad, axis=1), axis=1, keepdims=True)
+    largest = jnp.max(jnp.max(jnp.abs(grad + fold_ref[...]), axis=1), axis=1, keepdims=True)
+    power = jnp.ceil(jnp.log2(jnp.maximum(largest, 1e-30)))
+    scale = jnp.exp2(GRAD_BITS - power)
+    limit = 2.0**GRAD_BITS - 1.0
+    for m in range(modules):
+        exact = (grad_ref[m] + fold_ref[m]) * scale[m : m + 1, :]
+        words[m] = (nearest(jnp.clip(exact, -limit, limit)) << 8) | high_ref[m]
     row = lax.broadcasted_iota(jnp.int32, (modules, 128), 0)
     lane = lax.broadcasted_iota(jnp.int32, (modules, 128), 1)
-    squares = jnp.sum(jnp.where(row == lane, squares, 0.0), axis=0, keepdims=True)
+    tail = jnp.where(row == lane, squares * SQUARES_SCALE, 0.0)
+    tail = jnp.where(row + modules == lane, power, tail)
+    tail = nearest(jnp.sum(tail, axis=0, keepdims=True))
     copies = []
     for q in range(peers):
         m = module_ref[path_of(q, chips)]
         start = q * CHUNK
-        chunk_ref[start + GRAD : start + MOMENTUM, :] = grad_ref[m]
-        chunk_ref[start + SQUARES : start + CHUNK, :] = squares
+        chunk_ref[start : start + LOW, :] = words[m]
+        chunk_ref[start + SQUARES : start + CHUNK, :] = tail
         if (q + 1) % (peers // PIECES) == 0:
             piece = pl.ds(len(copies) * (peers // PIECES) * CHUNK, (peers // PIECES) * CHUNK)
             sem = sems.at[len(copies)]
@@ -86,25 +116,30 @@
     module_ref, chunk_ref, mine_ref, other_ref, grad_ref, decay_ref, own_grad_ref, own_ref
 ):
     peers, modules = grad_ref.shape[0], mine_ref.shape[0]
-    chips = peers // 2
     core = lax.axis_index("path_2")
     chip = lax.axis_index("path_0") * lax.axis_size("path_1") + lax.axis_index("path_1")
-    left = lax.broadcasted_iota(jnp.int32, (8, 128), 1) < 64
-    for at in range(chips):
-        first, second = at * CHUNK, (chips + at) * CHUNK
-        grad_ref[at] = chunk_ref[first + GRAD : first + MOMENTUM, :]
-        grad_ref[chips + at] = chunk_ref[second + GRAD : second + MOMENTUM, :]
-        one = chunk_ref[first + MOMENTUM : first + SQUARES, :]
-        two = chunk_ref[second + MOMENTUM : second + SQUARES, :]
-        decay_ref[at] = momentum_rate * jnp.where(left, one, two)
-        decay_ref[chips + at] = momentum_rate * pltpu.roll(jnp.where(left, two, one), 64, 1)
+    module = module_ref[chip * 2 + core]
+    tail = chunk_ref[pl.ds(SQUARES, peers, stride=CHUNK), :]
+    lane = lax.broadcasted_iota(jnp.int32, (peers, 128), 1)
+    power = jnp.where(lane == module + modules, tail, 0).astype(jnp.float32)
+    power = jnp.sum(power, axis=1, keepdims=True)
+    scale = jnp.broadcast_to(1.0 / jnp.exp2(GRAD_BITS - power), (peers, 128))
+    row = lax.broadcasted_iota(jnp.int32, (8, 128), 0)
+    shift = (row & 3) * 8
+    for q in range(peers):
+        start = q * CHUNK
+        words = chunk_ref[start : start + LOW, :]
+        grad_ref[q] = (words >> 8).astype(jnp.float32) * scale[q : q + 1, :]
+        one, two = chunk_ref[start + LOW : start + LOW + 1, :], chunk_ref[start + LOW + 1 : start + SQUARES, :]
+        low = (jnp.where(row < 4, one, two) >> shift) & 255
+        whole = (((words & 255) << 8) | low) - 32768
+        decay_ref[q] = whole.astype(jnp.float32) * (momentum_rate / MOMENTUM_SCALE)
     for m in range(modules):
         for half in range(2):
             grad = jnp.where(core == half, mine_ref[m], other_ref[m])
             grad = jnp.where(core == 0, grad, pltpu.roll(grad, 64, 1))
             own_grad_ref[m, half * 8 : half * 8 + 8, :] = grad[:, 0:64]
-    lane = lax.broadcasted_iota(jnp.int32, (1, 128), 1)
-    own_ref[...] = (lane == module_ref[chip * 2 + core]).astype(jnp.float32)
+    own_ref[...] = (lane[0:1, :] == module).astype(jnp.float32)
 
 
 def step_kernel(
@@ -114,7 +149,7 @@
     peers, modules = update.shape[0], new.shape[0]
     norm_squares = jnp.sum(squares_ref[...], axis=0, keepdims=True)
     shrink = jnp.minimum(1.0, limit / jnp.sqrt(norm_squares + 1e-06))
-    own = jnp.sum(shrink * own_ref[...], axis=1, keepdims=True)
+    own = jnp.sum(jnp.where(own_ref[...] > 0.0, shrink, 0.0), axis=1, keepdims=True)
     each = peers // PIECES
     copies = []
     for piece in range(PIECES):
@@ -142,32 +177,35 @@
     shape = jax.ShapeDtypeStruct
     tiles = deltas.reshape(2, 8, peers // 2, 128).transpose(0, 2, 1, 3).reshape(peers, 8, 128)
     column_tiles = lax.all_to_all(tiles, TILES, 0, 0, tiled=True)
-    chunks = kernel(
+    other = lax.ppermute(momentum, "path_2", [(0, 1), (1, 0)])
+    module_tiles = shape((modules, 8, 128), jnp.float32)
+    chunk_rows = shape((peers * CHUNK, 128), jnp.int32)
+    chunks, high, fold = kernel(
         momentum_kernel,
         "pack_momentum",
-        out_shape=shape((peers * CHUNK, 128), jnp.float32),
-        in_specs=[SMEM, VMEM],
-        out_specs=VMEM,
-        scratch_shapes=[pltpu.VMEM((modules, 8, 128), jnp.float32)],
-    )(path_module, momentum)
+        out_shape=(chunk_rows, shape((modules, 8, 128), jnp.int32), module_tiles),
+        in_specs=[SMEM, VMEM, VMEM],
+        out_specs=(VMEM,) * 3,
+        scratch_shapes=[pltpu.VMEM((modules, 8, 128), jnp.int32)],
+    )(path_module, momentum, other)
     _, chunks, grad = kernel(
         gather_kernel,
         "gather_modules",
-        out_shape=(
-            shape((peers * CHUNK, 128), jnp.float32),
-            shape((peers * CHUNK, 128), jnp.float32),
-            shape((modules, 8, 128), jnp.float32),
-        ),
-        in_specs=[SMEM, VMEM, VMEM],
+        out_shape=(chunk_rows, chunk_rows, module_tiles),
+        in_specs=[SMEM, VMEM, VMEM, VMEM, VMEM],
         out_specs=(VMEM, HBM, VMEM),
-        input_output_aliases={2: 0},
+        input_output_aliases={4: 0},
         scratch_shapes=[pltpu.VMEM((modules, 8, 128), jnp.float32)] * 4
-        + [pltpu.SMEM((modules,), jnp.int32), pltpu.SemaphoreType.DMA((PIECES,))],
-    )(path_module, column_tiles, chunks)
+        + [
+            pltpu.VMEM((modules, 8, 128), jnp.int32),
+            pltpu.SMEM((modules,), jnp.int32),
+            pltpu.SemaphoreType.DMA((PIECES,)),
+        ],
+    )(path_module, column_tiles, high, fold, chunks)
     chunks = lax.all_to_all(chunks.reshape(peers, CHUNK, 1, 128), TILES, 0, 0, tiled=True)
     other = lax.ppermute(grad, "path_2", [(0, 1), (1, 0)])
     chunks, other = lax.optimization_barrier((chunks, other))
-    squares = jnp.sum(chunks[:, SQUARES], axis=0)
+    squares = jnp.sum(chunks[:, SQUARES].astype(jnp.float32) * (1.0 / SQUARES_SCALE), axis=0)
     squares = lax.all_to_all(
         jnp.broadcast_to(squares, (shards, 1, 128)), "shard", 0, 0, tiled=True
     )

time: 68.6 us -> 64.7 us (0.943)
  waiting for transfers between devices: 32.9 us -> 26.5 us
  starting transfers between devices: 29.7 us -> 32 us
    all_to_all x1, waiting for transfers between devices: 16.2 us -> 12.1 us  [local(): lax.all_to_all(chunks.reshape(peers, CHUNK, 1, 128), TILES, 0, 0, tiled=T...]
    all_to_all x1, waiting for transfers between devices: 10 us -> 6.76 us  [local(): column_tiles = lax.all_to_all(tiles, TILES, 0, 0, tiled=True)]
    ppermute x0 -> x1, starting transfers between devices: none -> 2.26 us  [local(): other = lax.ppermute(momentum, 'path_2', [(0, 1), (1, 0)])]
    ppermute x0 -> x1, waiting for transfers between devices: none -> 0.97 us  [local(): other = lax.ppermute(momentum, 'path_2', [(0, 1), (1, 0)])]
  transfers between devices with their start and end apart: 4 -> 5, of which waited for: 4 -> 5; matrix products, arithmetic and copies ran while one was open for 0% -> 0% of each run, Pallas kernels for 2% -> 2%
where the time goes in v3:
time: 64.7 us; the launch traced here: 63.9 us
  starting transfers between devices  32 us (49%)
  waiting for transfers between devices  26.5 us (41%)
  Pallas kernels  4.04 us (6%)
  between operations  0.71 us (1%)
    all_to_all x1, starting transfers between devices, local(): column_tiles = lax.all_to_all(tiles, TILES, 0, 0, tiled=True)  15.1 us
    all_to_all x1, waiting for transfers between devices, local(): lax.all_to_all(chunks.reshape(peers, CHUNK, 1, 128), TILES, 0, 0, tiled=T...  12.1 us
    all_to_all x1, starting transfers between devices, local(): lax.all_to_all(jnp.broadcast_to(squares, (shards, 1, 128)), 'shard', 0, 0...  6.82 us
    all_to_all x1, waiting for transfers between devices, local(): column_tiles = lax.all_to_all(tiles, TILES, 0, 0, tiled=True)  6.76 us
    all_to_all x1, waiting for transfers between devices, local(): lax.all_to_all(jnp.broadcast_to(squares, (shards, 1, 128)), 'shard', 0, 0...  5.75 us
    all_to_all x1, starting transfers between devices, local(): lax.all_to_all(chunks.reshape(peers, CHUNK, 1, 128), TILES, 0, 0, tiled=T...  5.54 us
    ppermute x1, starting transfers between devices, local(): other = lax.ppermute(momentum, 'path_2', [(0, 1), (1, 0)])  2.26 us
    ppermute x1, starting transfers between devices, local(): other = lax.ppermute(grad, 'path_2', [(0, 1), (1, 0)])  2.26 us
  transfers between devices with their start and end apart: 5, of which 5 were waited for; matrix products, arithmetic and copies ran while one was open for 0% of the time, Pallas kernels for 2%

profile of v3, /device:TPU:1, one launch (start us, length us, event | category | flops | bytes accessed | tf_op | source)
XLA Modules:
  0.0 63.9 jit_solution(10808072406316527089)
XLA Ops:
  0.6 0.0 copy-start
  0.6 0.0 copy-start.1
  0.6 15.1 %all-to-all-start = ((bf16[64,8,128]{2,1,0:T(8,128)(2,1)}), bf16[64,8,128]{2,1,0:T(8,128)(2,1)S(1)}, u32[]{:S(2)}, u32[]{:S(2)}) async-start(bf16[64,8,128]{2,1,0:T(8,128)(2,1)} %bitcast.15), calls=%async_computation | async-start | bytes 262144 | tf_op jit(solution)/shard_map/all_to_all | solution.py:179
  15.7 0.0 copy-done
  15.7 2.3 %collective-permute-start = (f32[16,16,64]{2,1,0:T(8,128)S(1)}, f32[16,16,64]{2,1,0:T(8,128)S(1)}, u32[]{:S(2)}, u32[]{:S(2)}) collective-permute-start(f32[16,16,64]{2,1,0:T(8,128)S(1)} %copy-done), channel_id=1, source_target_pairs={{0,8},{8,0},{1,9},{9,1},{2,10},{10,2},{3,11},{11,3},{4,12},{12,4},... | collective-permute-start | bytes 196616 | tf_op jit(solution)/shard_map/ppermute | solution.py:180
  18.0 1.0 %collective-permute-done.other_ref = f32[16,16,64]{2,1,0:T(8,128)S(1)} collective-permute-done((f32[16,16,64]{2,1,0:T(8,128)S(1)}, f32[16,16,64]{2,1,0:T(8,128)S(1)}, u32[]{:S(2)}, u32[]{:S(2)}) %collective-permute-start) | collective-permute-done | bytes 65568 | tf_op jit(solution)/shard_map/ppermute | solution.py:180
  19.0 0.0 copy-done.1
  19.0 0.7 %pack_momentum.1 = (s32[704,128]{1,0:T(8,128)S(1)}, s32[16,8,128]{2,1,0:T(8,128)S(1)}, f32[16,8,128]{2,1,0:T(8,128)S(1)}) custom-call(s32[64]{0:T(128)S(1)} %copy-done.1, f32[16,16,64]{2,1,0:T(8,128)S(1)} %copy-done, f32[16,16,64]{2,1,0:T(8,128)S(1)} %collective-permute-done.other_ref), custom_call_target="tpu_custom_call" | custom-call | tf_op jit(solution)/shard_map/pack_momentum/pallas_call | solution.py:183
  19.7 6.8 %all-to-all-done.column_ref = bf16[64,8,128]{2,1,0:T(8,128)(2,1)S(1)} async-done(((bf16[64,8,128]{2,1,0:T(8,128)(2,1)}), bf16[64,8,128]{2,1,0:T(8,128)(2,1)S(1)}, u32[]{:S(2)}, u32[]{:S(2)}) %all-to-all-start) | async-done | bytes 131104 | tf_op jit(solution)/shard_map/all_to_all | solution.py:179
  26.5 1.7 %gather_modules.1 = (s32[704,128]{1,0:T(8,128)S(1)}, s32[704,128]{1,0:T(8,128)}, f32[16,8,128]{2,1,0:T(8,128)S(1)}) custom-call(s32[64]{0:T(128)S(1)} %copy-done.1, bf16[64,8,128]{2,1,0:T(8,128)(2,1)S(1)} %all-to-all-done.column_ref, s32[16,8,128]{2,1,0:T(8,128)S(1)} %get-tuple-element.15.high_ref, ...), custom_call_target="tpu_custom_call", output_to_operand_aliasing={{0}: (4, {})} | custom-call | tf_op jit(solution)/shard_map/gather_modules/pallas_call | solution.py:191
  28.2 5.5 %all-to-all-start.1 = ((s32[64,11,1,128]{3,2,1,0:T(1,128)}), s32[64,11,1,128]{3,2,1,0:T(1,128)S(1)}, u32[]{:S(2)}, u32[]{:S(2)}) async-start(s32[64,11,1,128]{3,2,1,0:T(1,128)} %bitcast.3), calls=%async_computation.1 | async-start | bytes 720896 | tf_op jit(solution)/shard_map/all_to_all | solution.py:205
  33.8 2.3 %collective-permute-start.1 = (f32[16,8,128]{2,1,0:T(8,128)S(1)}, f32[16,8,128]{2,1,0:T(8,128)S(1)}, u32[]{:S(2)}, u32[]{:S(2)}) collective-permute-start(f32[16,8,128]{2,1,0:T(8,128)S(1)} %get-tuple-element.19.mine_ref), channel_id=1, source_target_pairs={{0,8},{8,0},{1,9},{9,1},{2,10},{10,2},{3,11},{11,3},{4,12},{12,4},... | collective-permute-start | bytes 196616 | tf_op jit(solution)/shard_map/ppermute | solution.py:206
  36.0 0.9 %collective-permute-done.1.other_ref = f32[16,8,128]{2,1,0:T(8,128)S(1)} collective-permute-done((f32[16,8,128]{2,1,0:T(8,128)S(1)}, f32[16,8,128]{2,1,0:T(8,128)S(1)}, u32[]{:S(2)}, u32[]{:S(2)}) %collective-permute-start.1) | collective-permute-done | bytes 65568 | tf_op jit(solution)/shard_map/ppermute | solution.py:206
  36.9 12.1 %all-to-all-done.1 = s32[64,11,1,128]{3,2,1,0:T(1,128)S(1)} async-done(((s32[64,11,1,128]{3,2,1,0:T(1,128)}), s32[64,11,1,128]{3,2,1,0:T(1,128)S(1)}, u32[]{:S(2)}, u32[]{:S(2)}) %all-to-all-start.1) | async-done | bytes 360480 | tf_op jit(solution)/shard_map/all_to_all | solution.py:205
  49.1 0.1 multiply_reduce_fusion
  49.2 0.6 broadcast_in_dim.3
  49.8 6.8 %all-to-all-start.2 = ((f32[8,1,128]{2,1,0:T(1,128)}), f32[8,1,128]{2,1,0:T(1,128)S(1)}, u32[]{:S(2)}, u32[]{:S(2)}) async-start(f32[8,1,128]{2,1,0:T(1,128)} %broadcast_in_dim.3), calls=%async_computation.2 | async-start | bytes 8192 | tf_op jit(solution)/shard_map/all_to_all | solution.py:209
  56.6 0.7 %assemble.1 = (f32[64,8,128]{2,1,0:T(8,128)S(1)}, f32[64,8,128]{2,1,0:T(8,128)S(1)}, f32[16,16,64]{2,1,0:T(8,128)S(1)}, f32[1,128]{1,0:T(1,128)S(1)}) custom-call(s32[64]{0:T(128)S(1)} %copy-done.1, s32[704,128]{1,0:T(8,128)S(1)} %bitcast.13, f32[16,8,128]{2,1,0:T(8,128)S(1)} %get-tuple-element.19.mine_ref, f32[16,8,128]{2,1,0:T(8,128)S(1)} %collective-permute-done.1.other_ref), custom_call_target="tpu_custom_call" | custom-call | tf_op jit(solution)/shard_map/assemble/pallas_call | solution.py:213
  57.3 5.7 %all-to-all-done.2 = f32[8,1,128]{2,1,0:T(1,128)S(1)} async-done(((f32[8,1,128]{2,1,0:T(1,128)}), f32[8,1,128]{2,1,0:T(1,128)S(1)}, u32[]{:S(2)}, u32[]{:S(2)}) %all-to-all-start.2) | async-done | bytes 4128 | tf_op jit(solution)/shard_map/all_to_all | solution.py:209
  63.0 0.9 %step.1 = (bf16[64,8,128]{2,1,0:T(8,128)(2,1)}, f32[16,16,64]{2,1,0:T(8,128)}) custom-call(f32[8,128]{1,0:T(8,128)S(1)} %bitcast.14, f32[64,8,128]{2,1,0:T(8,128)S(1)} %get-tuple-element.22.refs_1_, f32[64,8,128]{2,1,0:T(8,128)S(1)} %get-tuple-element.23.refs_2_, f32[16,16,64]{2,1,0:T(8,128)S(1)} %get-tuple-element.24.refs_3_, ...), custom_call_target="tpu_custom_call" | custom-call | tf_op jit(solution)/shard_map/step/pallas_call | solution.py:226
Async XLA Ops:
  0.6 15.1 %copy-start = (f32[16,16,64]{2,1,0:T(8,128)S(1)}, f32[16,16,64]{2,1,0:T(8,128)}, u32[]{:S(2)}) copy-start(f32[16,16,64]{2,1,0:T(8,128)} %refs_5_.1) | copy-start | bytes 196612
  0.6 18.4 %copy-start.1 = (s32[64]{0:T(128)S(1)}, s32[64]{0:T(128)}, u32[]{:S(2)}) copy-start(s32[64]{0:T(128)} %module_ref.5) | copy-start | bytes 772
  0.6 25.8 %all-to-all-start = ((bf16[64,8,128]{2,1,0:T(8,128)(2,1)}), bf16[64,8,128]{2,1,0:T(8,128)(2,1)S(1)}, u32[]{:S(2)}, u32[]{:S(2)}) async-start(bf16[64,8,128]{2,1,0:T(8,128)(2,1)} %bitcast.15), calls=%async_computation | async-start | bytes 262144 | tf_op jit(solution)/shard_map/all_to_all | solution.py:179
  15.7 3.2 %collective-permute-start = (f32[16,16,64]{2,1,0:T(8,128)S(1)}, f32[16,16,64]{2,1,0:T(8,128)S(1)}, u32[]{:S(2)}, u32[]{:S(2)}) collective-permute-start(f32[16,16,64]{2,1,0:T(8,128)S(1)} %copy-done), channel_id=1, source_target_pairs={{0,8},{8,0},{1,9},{9,1},{2,10},{10,2},{3,11},{11,3},{4,12},{12,4},... | collective-permute-start | bytes 196616 | tf_op jit(solution)/shard_map/ppermute | solution.py:180
  28.2 20.8 %all-to-all-start.1 = ((s32[64,11,1,128]{3,2,1,0:T(1,128)}), s32[64,11,1,128]{3,2,1,0:T(1,128)S(1)}, u32[]{:S(2)}, u32[]{:S(2)}) async-start(s32[64,11,1,128]{3,2,1,0:T(1,128)} %bitcast.3), calls=%async_computation.1 | async-start | bytes 720896 | tf_op jit(solution)/shard_map/all_to_all | solution.py:205
  33.8 3.2 %collective-permute-start.1 = (f32[16,8,128]{2,1,0:T(8,128)S(1)}, f32[16,8,128]{2,1,0:T(8,128)S(1)}, u32[]{:S(2)}, u32[]{:S(2)}) collective-permute-start(f32[16,8,128]{2,1,0:T(8,128)S(1)} %get-tuple-element.19.mine_ref), channel_id=1, source_target_pairs={{0,8},{8,0},{1,9},{9,1},{2,10},{10,2},{3,11},{11,3},{4,12},{12,4},... | collective-permute-start | bytes 196616 | tf_op jit(solution)/shard_map/ppermute | solution.py:206
  49.8 13.3 %all-to-all-start.2 = ((f32[8,1,128]{2,1,0:T(1,128)}), f32[8,1,128]{2,1,0:T(1,128)S(1)}, u32[]{:S(2)}, u32[]{:S(2)}) async-start(f32[8,1,128]{2,1,0:T(1,128)} %broadcast_in_dim.3), calls=%async_computation.2 | async-start | bytes 8192 | tf_op jit(solution)/shard_map/all_to_all | solution.py:209

commit v4 on v3

--- a/solution.py
+++ b/solution.py
@@ -13,8 +13,8 @@
 momentum_rate = 0.9
 clip_ratio = 2.0
 
-LOW, SQUARES, CHUNK = 8, 10, 11
-GRAD_BITS = 23
+UPPER, SQUARES, CHUNK = 8, 9, 10
+GRAD_BITS, LOWER_BITS = 19, 12
 MOMENTUM_SCALE = 8191.0
 SQUARES_SCALE = 128.0
 FOLD = momentum_rate * momentum_rate / (1.0 + momentum_rate)
@@ -38,10 +38,18 @@
     return jnp.floor(x + 0.5).astype(jnp.int32)
 
 
-def momentum_kernel(module_ref, mine_ref, other_ref, chunk_ref, high_ref, fold_ref, low):
+def momentum_kernel(
+    module_ref, mine_ref, other_ref, chunk_ref, lower_ref, fold_ref, count_ref, upper, count
+):
+    peers, modules = chunk_ref.shape[0] // CHUNK, mine_ref.shape[0]
+    for m in range(modules):
+        count[m] = 0
+    for q in range(peers):
+        count[module_ref[q]] += 1
     first_core = lax.axis_index("path_2") == 0
     row = lax.broadcasted_iota(jnp.int32, (8, 128), 0)
-    for m in range(mine_ref.shape[0]):
+    for m in range(modules):
+        count_ref[m : m + 1, :] = jnp.full((1, 128), count[m].astype(jnp.float32))
         mine = jnp.where(first_core, mine_ref[m, 0:8, :], mine_ref[m, 8:16, :])
         other = jnp.where(first_core, other_ref[m, 0:8, :], other_ref[m, 8:16, :])
         momentum = jnp.concatenate(
@@ -50,39 +58,34 @@
         whole = nearest(momentum * MOMENTUM_SCALE)
         fold_ref[m] = FOLD * (momentum - whole.astype(jnp.float32) * (1.0 / MOMENTUM_SCALE))
         whole += 32768
-        high_ref[m] = whole >> 8
-        word = (whole & 255) << ((row & 3) * 8)
-        word = word | pltpu.roll(word, 7, 0)
-        word = word | pltpu.roll(word, 6, 0)
-        low[m, 0:1, :] = word[0:1, :]
-        low[m, 1:2, :] = word[4:5, :]
-    peers = chunk_ref.shape[0] // CHUNK
+        lower_ref[m] = whole & ((1 << LOWER_BITS) - 1)
+        word = (whole >> LOWER_BITS) << (row * 4)
+        for rows in (4, 2, 1):
+            word = word | pltpu.roll(word, rows, 0)
+        upper[m] = word
     for q in range(peers):
         start = q * CHUNK
         m = module_ref[path_of(q, peers // 2)]
-        chunk_ref[start + LOW : start + SQUARES, :] = low[m, 0:2, :]
+        chunk_ref[start + UPPER : start + SQUARES, :] = upper[m, 0:1, :]
 
 
 def gather_kernel(
-    module_ref, column_ref, high_ref, fold_ref, _, chunk_ref, chunk_out, grad_ref, *scratch
-):
-    *sums, words, count, sems = scratch
+    module_ref, column_ref, lower_ref, fold_ref, count_ref, _, chunk_ref, chunk_out, grad_ref, *scratch
+):
+    *sums, words, sems = scratch
     peers, modules = column_ref.shape[0], grad_ref.shape[0]
     chips = peers // 2
     for total in sums:
         total[...] = jnp.zeros_like(total)
-    for m in range(modules):
-        count[m] = 0
     for q in range(peers):
         m = module_ref[path_of(q, chips)]
         total = sums[q % len(sums)]
         total[m] += column_ref[q].astype(jnp.float32)
-        count[m] += 1
     for m in range(modules):
         total = sums[0][m]
         for more in sums[1:]:
             total += more[m]
-        grad_ref[m] = total / count[m].astype(jnp.float32)
+        grad_ref[m] = total / count_ref[m : m + 1, :]
     grad = grad_ref[...]
     squares = jnp.sum(jnp.sum(grad * grad, axis=1), axis=1, keepdims=True)
     largest = jnp.max(jnp.max(jnp.abs(grad + fold_ref[...]), axis=1), axis=1, keepdims=True)
@@ -91,7 +94,7 @@
     limit = 2.0**GRAD_BITS - 1.0
     for m in range(modules):
         exact = (grad_ref[m] + fold_ref[m]) * scale[m : m + 1, :]
-        words[m] = (nearest(jnp.clip(exact, -limit, limit)) << 8) | high_ref[m]
+        words[m] = (nearest(jnp.clip(exact, -limit, limit)) << LOWER_BITS) | lower_ref[m]
     row = lax.broadcasted_iota(jnp.int32, (modules, 128), 0)
     lane = lax.broadcasted_iota(jnp.int32, (modules, 128), 1)
     tail = jnp.where(row == lane, squares * SQUARES_SCALE, 0.0)
@@ -101,7 +104,7 @@
     for q in range(peers):
         m = module_ref[path_of(q, chips)]
         start = q * CHUNK
-        chunk_ref[start : start + LOW, :] = words[m]
+        chunk_ref[start : start + UPPER, :] = words[m]
         chunk_ref[start + SQUARES : start + CHUNK, :] = tail
         if (q + 1) % (peers // PIECES) == 0:
             piece = pl.ds(len(copies) * (peers // PIECES) * CHUNK, (peers // PIECES) * CHUNK)
@@ -125,14 +128,12 @@
     power = jnp.sum(power, axis=1, keepdims=True)
     scale = jnp.broadcast_to(1.0 / jnp.exp2(GRAD_BITS - power), (peers, 128))
     row = lax.broadcasted_iota(jnp.int32, (8, 128), 0)
-    shift = (row & 3) * 8
     for q in range(peers):
         start = q * CHUNK
-        words = chunk_ref[start : start + LOW, :]
-        grad_ref[q] = (words >> 8).astype(jnp.float32) * scale[q : q + 1, :]
-        one, two = chunk_ref[start + LOW : start + LOW + 1, :], chunk_ref[start + LOW + 1 : start + SQUARES, :]
-        low = (jnp.where(row < 4, one, two) >> shift) & 255
-        whole = (((words & 255) << 8) | low) - 32768
+        words = chunk_ref[start : start + UPPER, :]
+        grad_ref[q] = (words >> LOWER_BITS).astype(jnp.float32) * scale[q : q + 1, :]
+        upper = (chunk_ref[start + UPPER : start + SQUARES, :] >> (row * 4)) & 15
+        whole = ((upper << LOWER_BITS) | (words & ((1 << LOWER_BITS) - 1))) - 32768
         decay_ref[q] = whole.astype(jnp.float32) * (momentum_rate / MOMENTUM_SCALE)
     for m in range(modules):
         for half in range(2):
@@ -180,28 +181,35 @@
     other = lax.ppermute(momentum, "path_2", [(0, 1), (1, 0)])
     module_tiles = shape((modules, 8, 128), jnp.float32)
     chunk_rows = shape((peers * CHUNK, 128), jnp.int32)
-    chunks, high, fold = kernel(
+    chunks, *packed = kernel(
         momentum_kernel,
         "pack_momentum",
-        out_shape=(chunk_rows, shape((modules, 8, 128), jnp.int32), module_tiles),
+        out_shape=(
+            chunk_rows,
+            shape((modules, 8, 128), jnp.int32),
+            module_tiles,
+            shape((modules, 128), jnp.float32),
+        ),
         in_specs=[SMEM, VMEM, VMEM],
-        out_specs=(VMEM,) * 3,
-        scratch_shapes=[pltpu.VMEM((modules, 8, 128), jnp.int32)],
+        out_specs=(VMEM,) * 4,
+        scratch_shapes=[
+            pltpu.VMEM((modules, 8, 128), jnp.int32),
+            pltpu.SMEM((modules,), jnp.int32),
+        ],
     )(path_module, momentum, other)
     _, chunks, grad = kernel(
         gather_kernel,
         "gather_modules",
         out_shape=(chunk_rows, chunk_rows, module_tiles),
-        in_specs=[SMEM, VMEM, VMEM, VMEM, VMEM],
+        in_specs=[SMEM, VMEM, VMEM, VMEM, VMEM, VMEM],
         out_specs=(VMEM, HBM, VMEM),
-        input_output_aliases={4: 0},
+        input_output_aliases={5: 0},
         scratch_shapes=[pltpu.VMEM((modules, 8, 128), jnp.float32)] * 4
         + [
             pltpu.VMEM((modules, 8, 128), jnp.int32),
-            pltpu.SMEM((modules,), jnp.int32),
             pltpu.SemaphoreType.DMA((PIECES,)),
         ],
-    )(path_module, column_tiles, high, fold, chunks)
+    )(path_module, column_tiles, *packed, chunks)
     chunks = lax.all_to_all(chunks.reshape(peers, CHUNK, 1, 128), TILES, 0, 0, tiled=True)
     other = lax.ppermute(grad, "path_2", [(0, 1), (1, 0)])
     chunks, other = lax.optimization_barrier((chunks, other))

time: 64.7 us -> 63.9 us (0.988)
  waiting for transfers between devices: 26.5 us -> 25.7 us
  transfers between devices with their start and end apart: 5 -> 5, of which waited for: 5 -> 5; matrix products, arithmetic and copies ran while one was open for 0% -> 0% of each run, Pallas kernels for 2% -> 3%
where the time goes in v4:
time: 63.9 us; the launch traced here: 63.1 us
  starting transfers between devices  32 us (50%)
  waiting for transfers between devices  25.7 us (40%)
  Pallas kernels  4.05 us (6%)
  between operations  0.71 us (1%)
    all_to_all x1, starting transfers between devices, local(): column_tiles = lax.all_to_all(tiles, TILES, 0, 0, tiled=True)  15.1 us
    all_to_all x1, waiting for transfers between devices, local(): lax.all_to_all(chunks.reshape(peers, CHUNK, 1, 128), TILES, 0, 0, tiled=T...  11.5 us
    all_to_all x1, starting transfers between devices, local(): lax.all_to_all(jnp.broadcast_to(squares, (shards, 1, 128)), 'shard', 0, 0...  6.82 us
    all_to_all x1, waiting for transfers between devices, local(): column_tiles = lax.all_to_all(tiles, TILES, 0, 0, tiled=True)  6.56 us
    all_to_all x1, waiting for transfers between devices, local(): lax.all_to_all(jnp.broadcast_to(squares, (shards, 1, 128)), 'shard', 0, 0...  5.75 us
    all_to_all x1, starting transfers between devices, local(): lax.all_to_all(chunks.reshape(peers, CHUNK, 1, 128), TILES, 0, 0, tiled=T...  5.54 us
    ppermute x1, starting transfers between devices, local(): other = lax.ppermute(momentum, 'path_2', [(0, 1), (1, 0)])  2.26 us
    ppermute x1, starting transfers between devices, local(): other = lax.ppermute(grad, 'path_2', [(0, 1), (1, 0)])  2.26 us
  transfers between devices with their start and end apart: 5, of which 5 were waited for; matrix products, arithmetic and copies ran while one was open for 0% of the time, Pallas kernels for 3%

profile of v4, /device:TPU:1, one launch (start us, length us, event | category | flops | bytes accessed | tf_op | source)
XLA Modules:
  0.0 63.1 jit_solution(265224358504365470)
XLA Ops:
  0.6 0.0 copy-start
  0.6 0.0 copy-start.1
  0.6 15.1 %all-to-all-start = ((bf16[64,8,128]{2,1,0:T(8,128)(2,1)}), bf16[64,8,128]{2,1,0:T(8,128)(2,1)S(1)}, u32[]{:S(2)}, u32[]{:S(2)}) async-start(bf16[64,8,128]{2,1,0:T(8,128)(2,1)} %bitcast.15), calls=%async_computation | async-start | bytes 262144 | tf_op jit(solution)/shard_map/all_to_all | solution.py:180
  15.7 0.0 copy-done
  15.7 2.3 %collective-permute-start = (f32[16,16,64]{2,1,0:T(8,128)S(1)}, f32[16,16,64]{2,1,0:T(8,128)S(1)}, u32[]{:S(2)}, u32[]{:S(2)}) collective-permute-start(f32[16,16,64]{2,1,0:T(8,128)S(1)} %copy-done), channel_id=1, source_target_pairs={{0,8},{8,0},{1,9},{9,1},{2,10},{10,2},{3,11},{11,3},{4,12},{12,4},... | collective-permute-start | bytes 196616 | tf_op jit(solution)/shard_map/ppermute | solution.py:181
  18.0 1.0 %collective-permute-done.other_ref = f32[16,16,64]{2,1,0:T(8,128)S(1)} collective-permute-done((f32[16,16,64]{2,1,0:T(8,128)S(1)}, f32[16,16,64]{2,1,0:T(8,128)S(1)}, u32[]{:S(2)}, u32[]{:S(2)}) %collective-permute-start) | collective-permute-done | bytes 65568 | tf_op jit(solution)/shard_map/ppermute | solution.py:181
  19.0 0.0 copy-done.1
  19.0 0.9 %pack_momentum.1 = (s32[640,128]{1,0:T(8,128)S(1)}, s32[16,8,128]{2,1,0:T(8,128)S(1)}, f32[16,8,128]{2,1,0:T(8,128)S(1)}, f32[16,128]{1,0:T(8,128)S(1)}) custom-call(s32[64]{0:T(128)S(1)} %copy-done.1, f32[16,16,64]{2,1,0:T(8,128)S(1)} %copy-done, f32[16,16,64]{2,1,0:T(8,128)S(1)} %collective-permute-done.other_ref), custom_call_target="tpu_custom_call" | custom-call | tf_op jit(solution)/shard_map/pack_momentum/pallas_call | solution.py:184
  19.9 6.6 %all-to-all-done.column_ref = bf16[64,8,128]{2,1,0:T(8,128)(2,1)S(1)} async-done(((bf16[64,8,128]{2,1,0:T(8,128)(2,1)}), bf16[64,8,128]{2,1,0:T(8,128)(2,1)S(1)}, u32[]{:S(2)}, u32[]{:S(2)}) %all-to-all-start) | async-done | bytes 131104 | tf_op jit(solution)/shard_map/all_to_all | solution.py:180
  26.5 1.6 %gather_modules.1 = (s32[640,128]{1,0:T(8,128)S(1)}, s32[640,128]{1,0:T(8,128)}, f32[16,8,128]{2,1,0:T(8,128)S(1)}) custom-call(s32[64]{0:T(128)S(1)} %copy-done.1, bf16[64,8,128]{2,1,0:T(8,128)(2,1)S(1)} %all-to-all-done.column_ref, s32[16,8,128]{2,1,0:T(8,128)S(1)} %get-tuple-element.16.lower_ref, ...), custom_call_target="tpu_custom_call", output_to_operand_aliasing={{0}: (5, {})} | custom-call | tf_op jit(solution)/shard_map/gather_modules/pallas_call | solution.py:200
  28.0 5.5 %all-to-all-start.1 = ((s32[64,10,1,128]{3,2,1,0:T(1,128)}), s32[64,10,1,128]{3,2,1,0:T(1,128)S(1)}, u32[]{:S(2)}, u32[]{:S(2)}) async-start(s32[64,10,1,128]{3,2,1,0:T(1,128)} %bitcast.3), calls=%async_computation.1 | async-start | bytes 655360 | tf_op jit(solution)/shard_map/all_to_all | solution.py:213
  33.6 2.3 %collective-permute-start.1 = (f32[16,8,128]{2,1,0:T(8,128)S(1)}, f32[16,8,128]{2,1,0:T(8,128)S(1)}, u32[]{:S(2)}, u32[]{:S(2)}) collective-permute-start(f32[16,8,128]{2,1,0:T(8,128)S(1)} %get-tuple-element.21.mine_ref), channel_id=1, source_target_pairs={{0,8},{8,0},{1,9},{9,1},{2,10},{10,2},{3,11},{11,3},{4,12},{12,4},... | collective-permute-start | bytes 196616 | tf_op jit(solution)/shard_map/ppermute | solution.py:214
  35.9 0.9 %collective-permute-done.1.other_ref = f32[16,8,128]{2,1,0:T(8,128)S(1)} collective-permute-done((f32[16,8,128]{2,1,0:T(8,128)S(1)}, f32[16,8,128]{2,1,0:T(8,128)S(1)}, u32[]{:S(2)}, u32[]{:S(2)}) %collective-permute-start.1) | collective-permute-done | bytes 65568 | tf_op jit(solution)/shard_map/ppermute | solution.py:214
  36.7 11.5 %all-to-all-done.1 = s32[64,10,1,128]{3,2,1,0:T(1,128)S(1)} async-done(((s32[64,10,1,128]{3,2,1,0:T(1,128)}), s32[64,10,1,128]{3,2,1,0:T(1,128)S(1)}, u32[]{:S(2)}, u32[]{:S(2)}) %all-to-all-start.1) | async-done | bytes 327712 | tf_op jit(solution)/shard_map/all_to_all | solution.py:213
  48.3 0.1 multiply_reduce_fusion
  48.3 0.6 broadcast_in_dim.3
  48.9 6.8 %all-to-all-start.2 = ((f32[8,1,128]{2,1,0:T(1,128)}), f32[8,1,128]{2,1,0:T(1,128)S(1)}, u32[]{:S(2)}, u32[]{:S(2)}) async-start(f32[8,1,128]{2,1,0:T(1,128)} %broadcast_in_dim.3), calls=%async_computation.2 | async-start | bytes 8192 | tf_op jit(solution)/shard_map/all_to_all | solution.py:217
  55.8 0.7 %assemble.1 = (f32[64,8,128]{2,1,0:T(8,128)S(1)}, f32[64,8,128]{2,1,0:T(8,128)S(1)}, f32[16,16,64]{2,1,0:T(8,128)S(1)}, f32[1,128]{1,0:T(1,128)S(1)}) custom-call(s32[64]{0:T(128)S(1)} %copy-done.1, s32[640,128]{1,0:T(8,128)S(1)} %bitcast.13, f32[16,8,128]{2,1,0:T(8,128)S(1)} %get-tuple-element.21.mine_ref, f32[16,8,128]{2,1,0:T(8,128)S(1)} %collective-permute-done.1.other_ref), custom_call_target="tpu_custom_call" | custom-call | tf_op jit(solution)/shard_map/assemble/pallas_call | solution.py:221
  56.5 5.7 %all-to-all-done.2 = f32[8,1,128]{2,1,0:T(1,128)S(1)} async-done(((f32[8,1,128]{2,1,0:T(1,128)}), f32[8,1,128]{2,1,0:T(1,128)S(1)}, u32[]{:S(2)}, u32[]{:S(2)}) %all-to-all-start.2) | async-done | bytes 4128 | tf_op jit(solution)/shard_map/all_to_all | solution.py:217
  62.2 0.9 %step.1 = (bf16[64,8,128]{2,1,0:T(8,128)(2,1)}, f32[16,16,64]{2,1,0:T(8,128)}) custom-call(f32[8,128]{1,0:T(8,128)S(1)} %bitcast.14, f32[64,8,128]{2,1,0:T(8,128)S(1)} %get-tuple-element.24.refs_1_, f32[64,8,128]{2,1,0:T(8,128)S(1)} %get-tuple-element.25.refs_2_, f32[16,16,64]{2,1,0:T(8,128)S(1)} %get-tuple-element.26.refs_3_, ...), custom_call_target="tpu_custom_call" | custom-call | tf_op jit(solution)/shard_map/step/pallas_call | solution.py:234
Async XLA Ops:
  0.6 15.1 %copy-start = (f32[16,16,64]{2,1,0:T(8,128)S(1)}, f32[16,16,64]{2,1,0:T(8,128)}, u32[]{:S(2)}) copy-start(f32[16,16,64]{2,1,0:T(8,128)} %refs_5_.1) | copy-start | bytes 196612
  0.6 18.4 %copy-start.1 = (s32[64]{0:T(128)S(1)}, s32[64]{0:T(128)}, u32[]{:S(2)}) copy-start(s32[64]{0:T(128)} %module_ref.5) | copy-start | bytes 772
  0.6 25.8 %all-to-all-start = ((bf16[64,8,128]{2,1,0:T(8,128)(2,1)}), bf16[64,8,128]{2,1,0:T(8,128)(2,1)S(1)}, u32[]{:S(2)}, u32[]{:S(2)}) async-start(bf16[64,8,128]{2,1,0:T(8,128)(2,1)} %bitcast.15), calls=%async_computation | async-start | bytes 262144 | tf_op jit(solution)/shard_map/all_to_all | solution.py:180
  15.7 3.2 %collective-permute-start = (f32[16,16,64]{2,1,0:T(8,128)S(1)}, f32[16,16,64]{2,1,0:T(8,128)S(1)}, u32[]{:S(2)}, u32[]{:S(2)}) collective-permute-start(f32[16,16,64]{2,1,0:T(8,128)S(1)} %copy-done), channel_id=1, source_target_pairs={{0,8},{8,0},{1,9},{9,1},{2,10},{10,2},{3,11},{11,3},{4,12},{12,4},... | collective-permute-start | bytes 196616 | tf_op jit(solution)/shard_map/ppermute | solution.py:181
  28.0 20.2 %all-to-all-start.1 = ((s32[64,10,1,128]{3,2,1,0:T(1,128)}), s32[64,10,1,128]{3,2,1,0:T(1,128)S(1)}, u32[]{:S(2)}, u32[]{:S(2)}) async-start(s32[64,10,1,128]{3,2,1,0:T(1,128)} %bitcast.3), calls=%async_computation.1 | async-start | bytes 655360 | tf_op jit(solution)/shard_map/all_to_all | solution.py:213
  33.6 3.2 %collective-permute-start.1 = (f32[16,8,128]{2,1,0:T(8,128)S(1)}, f32[16,8,128]{2,1,0:T(8,128)S(1)}, u32[]{:S(2)}, u32[]{:S(2)}) collective-permute-start(f32[16,8,128]{2,1,0:T(8,128)S(1)} %get-tuple-element.21.mine_ref), channel_id=1, source_target_pairs={{0,8},{8,0},{1,9},{9,1},{2,10},{10,2},{3,11},{11,3},{4,12},{12,4},... | collective-permute-start | bytes 196616 | tf_op jit(solution)/shard_map/ppermute | solution.py:214
  48.9 13.3 %all-to-all-start.2 = ((f32[8,1,128]{2,1,0:T(1,128)}), f32[8,1,128]{2,1,0:T(1,128)S(1)}, u32[]{:S(2)}, u32[]{:S(2)}) async-start(f32[8,1,128]{2,1,0:T(1,128)} %broadcast_in_dim.3), calls=%async_computation.2 | async-start | bytes 8192 | tf_op jit(solution)/shard_map/all_to_all | solution.py:217

commit v5 on v4

--- a/solution.py
+++ b/solution.py
@@ -13,8 +13,9 @@
 momentum_rate = 0.9
 clip_ratio = 2.0
 
-UPPER, SQUARES, CHUNK = 8, 9, 10
-GRAD_BITS, LOWER_BITS = 19, 12
+UPPER, CHUNK = 8, 9
+GRAD_BITS, LOWER_BITS = 18, 13
+EXPONENTS, BIAS = 64, 128
 MOMENTUM_SCALE = 8191.0
 SQUARES_SCALE = 128.0
 FOLD = momentum_rate * momentum_rate / (1.0 + momentum_rate)
@@ -34,14 +35,18 @@
     return pl.pallas_call(body, name=name, compiler_params=params, **kwargs)
 
 
+def lanes():
+    return lax.broadcasted_iota(jnp.int32, (8, 128), 1)
+
+
 def nearest(x):
     return jnp.floor(x + 0.5).astype(jnp.int32)
 
 
 def momentum_kernel(
-    module_ref, mine_ref, other_ref, chunk_ref, lower_ref, fold_ref, count_ref, upper, count
-):
-    peers, modules = chunk_ref.shape[0] // CHUNK, mine_ref.shape[0]
+    module_ref, mine_ref, other_ref, lower_ref, upper_ref, fold_ref, count_ref, count
+):
+    peers, modules = module_ref.shape[0], mine_ref.shape[0]
     for m in range(modules):
         count[m] = 0
     for q in range(peers):
@@ -59,20 +64,16 @@
         fold_ref[m] = FOLD * (momentum - whole.astype(jnp.float32) * (1.0 / MOMENTUM_SCALE))
         whole += 32768
         lower_ref[m] = whole & ((1 << LOWER_BITS) - 1)
-        word = (whole >> LOWER_BITS) << (row * 4)
+        word = (whole >> LOWER_BITS) << (row * 3)
         for rows in (4, 2, 1):
             word = word | pltpu.roll(word, rows, 0)
-        upper[m] = word
-    for q in range(peers):
-        start = q * CHUNK
-        m = module_ref[path_of(q, peers // 2)]
-        chunk_ref[start + UPPER : start + SQUARES, :] = upper[m, 0:1, :]
+        upper_ref[m : m + 1, :] = word[0:1, :]
 
 
 def gather_kernel(
-    module_ref, column_ref, lower_ref, fold_ref, count_ref, _, chunk_ref, chunk_out, grad_ref, *scratch
-):
-    *sums, words, sems = scratch
+    module_ref, column_ref, lower_ref, upper_ref, fold_ref, count_ref, chunk_out, grad_ref, *scratch
+):
+    *sums, words, chunk, sems = scratch
     peers, modules = column_ref.shape[0], grad_ref.shape[0]
     chips = peers // 2
     for total in sums:
@@ -88,28 +89,31 @@
         grad_ref[m] = total / count_ref[m : m + 1, :]
     grad = grad_ref[...]
     squares = jnp.sum(jnp.sum(grad * grad, axis=1), axis=1, keepdims=True)
-    largest = jnp.max(jnp.max(jnp.abs(grad + fold_ref[...]), axis=1), axis=1, keepdims=True)
-    power = jnp.ceil(jnp.log2(jnp.maximum(largest, 1e-30)))
-    scale = jnp.exp2(GRAD_BITS - power)
-    limit = 2.0**GRAD_BITS - 1.0
-    for m in range(modules):
-        exact = (grad_ref[m] + fold_ref[m]) * scale[m : m + 1, :]
-        words[m] = (nearest(jnp.clip(exact, -limit, limit)) << LOWER_BITS) | lower_ref[m]
+    squares = nearest(squares * SQUARES_SCALE)
     row = lax.broadcasted_iota(jnp.int32, (modules, 128), 0)
     lane = lax.broadcasted_iota(jnp.int32, (modules, 128), 1)
-    tail = jnp.where(row == lane, squares * SQUARES_SCALE, 0.0)
-    tail = jnp.where(row + modules == lane, power, tail)
-    tail = nearest(jnp.sum(tail, axis=0, keepdims=True))
+    norms = jnp.where(lane >> 2 == row, (squares >> ((lane & 3) * 8)) & 255, 0)
+    norms = jnp.sum(norms.astype(jnp.float32), axis=0, keepdims=True)
+    limit = 2.0**GRAD_BITS - 1.0
+    own_lane = lanes() == EXPONENTS + lax.broadcasted_iota(jnp.int32, (8, 128), 0)
+    for m in range(modules):
+        exact = grad_ref[m] + fold_ref[m]
+        largest = jnp.max(jnp.abs(exact), axis=1, keepdims=True)
+        power = jnp.ceil(jnp.log2(jnp.maximum(largest, 1e-30)))
+        exact = jnp.clip(exact * jnp.exp2(GRAD_BITS - power), -limit, limit)
+        words[m, 0:UPPER, :] = (nearest(exact) << LOWER_BITS) | lower_ref[m]
+        powers = jnp.sum(jnp.where(own_lane, power + BIAS, 0.0), axis=0, keepdims=True)
+        words[m, UPPER:CHUNK, :] = upper_ref[m : m + 1, :] | ((norms + powers).astype(jnp.int32) << 24)
     copies = []
     for q in range(peers):
         m = module_ref[path_of(q, chips)]
         start = q * CHUNK
-        chunk_ref[start : start + UPPER, :] = words[m]
-        chunk_ref[start + SQUARES : start + CHUNK, :] = tail
+        chunk[start : start + UPPER, :] = words[m, 0:UPPER, :]
+        chunk[start + UPPER : start + CHUNK, :] = words[m, UPPER:CHUNK, :]
         if (q + 1) % (peers // PIECES) == 0:
             piece = pl.ds(len(copies) * (peers // PIECES) * CHUNK, (peers // PIECES) * CHUNK)
             sem = sems.at[len(copies)]
-            copies.append(pltpu.make_async_copy(chunk_ref.at[piece], chunk_out.at[piece], sem))
+            copies.append(pltpu.make_async_copy(chunk.at[piece], chunk_out.at[piece], sem))
             copies[-1].start()
     for copy in copies:
         copy.wait()
@@ -122,17 +126,16 @@
     core = lax.axis_index("path_2")
     chip = lax.axis_index("path_0") * lax.axis_size("path_1") + lax.axis_index("path_1")
     module = module_ref[chip * 2 + core]
-    tail = chunk_ref[pl.ds(SQUARES, peers, stride=CHUNK), :]
-    lane = lax.broadcasted_iota(jnp.int32, (peers, 128), 1)
-    power = jnp.where(lane == module + modules, tail, 0).astype(jnp.float32)
-    power = jnp.sum(power, axis=1, keepdims=True)
-    scale = jnp.broadcast_to(1.0 / jnp.exp2(GRAD_BITS - power), (peers, 128))
+    power = (chunk_ref[pl.ds(UPPER, peers, stride=CHUNK), :] >> 24) & 255
+    scale = 1.0 / jnp.exp2(GRAD_BITS + BIAS - power.astype(jnp.float32))
     row = lax.broadcasted_iota(jnp.int32, (8, 128), 0)
+    own_lane = lanes() == EXPONENTS + row
     for q in range(peers):
         start = q * CHUNK
         words = chunk_ref[start : start + UPPER, :]
-        grad_ref[q] = (words >> LOWER_BITS).astype(jnp.float32) * scale[q : q + 1, :]
-        upper = (chunk_ref[start + UPPER : start + SQUARES, :] >> (row * 4)) & 15
+        of_row = jnp.sum(jnp.where(own_lane, scale[q : q + 1, :], 0.0), axis=1, keepdims=True)
+        grad_ref[q] = (words >> LOWER_BITS).astype(jnp.float32) * of_row
+        upper = (chunk_ref[start + UPPER : start + CHUNK, :] >> (row * 3)) & 7
         whole = ((upper << LOWER_BITS) | (words & ((1 << LOWER_BITS) - 1))) - 32768
         decay_ref[q] = whole.astype(jnp.float32) * (momentum_rate / MOMENTUM_SCALE)
     for m in range(modules):
@@ -140,7 +143,7 @@
             grad = jnp.where(core == half, mine_ref[m], other_ref[m])
             grad = jnp.where(core == 0, grad, pltpu.roll(grad, 64, 1))
             own_grad_ref[m, half * 8 : half * 8 + 8, :] = grad[:, 0:64]
-    own_ref[...] = (lane[0:1, :] == module).astype(jnp.float32)
+    own_ref[...] = (lanes()[0:1, :] == 4 * module).astype(jnp.float32)
 
 
 def step_kernel(
@@ -148,7 +151,13 @@
     update_out, new_out, update, new, sems,
 ):
     peers, modules = update.shape[0], new.shape[0]
-    norm_squares = jnp.sum(squares_ref[...], axis=0, keepdims=True)
+    lane = lanes()
+    norm_squares = jnp.broadcast_to(jnp.sum(squares_ref[...], axis=0, keepdims=True), (8, 128))
+    for byte in range(4):
+        weight = 256.0**byte / SQUARES_SCALE
+        norm_squares = jnp.where(lane & 3 == byte, norm_squares * weight, norm_squares)
+    norm_squares += pltpu.roll(norm_squares, 127, 1)
+    norm_squares = (norm_squares + pltpu.roll(norm_squares, 126, 1))[0:1, :]
     shrink = jnp.minimum(1.0, limit / jnp.sqrt(norm_squares + 1e-06))
     own = jnp.sum(jnp.where(own_ref[...] > 0.0, shrink, 0.0), axis=1, keepdims=True)
     each = peers // PIECES
@@ -160,9 +169,8 @@
         update[tiles] = step.astype(jnp.bfloat16)
         copies.append(pltpu.make_async_copy(update.at[tiles], update_out.at[tiles], sems.at[piece]))
         copies[-1].start()
-    lane = lax.broadcasted_iota(jnp.int32, (1, 128), 1)
-    for m in range(modules):
-        k = jnp.sum(jnp.where(lane == m, shrink, 0.0), axis=1, keepdims=True)
+    for m in range(modules):
+        k = jnp.sum(jnp.where(lane[0:1, :] == 4 * m, shrink, 0.0), axis=1, keepdims=True)
         new[m] = momentum_rate * momentum_ref[m] + own_grad_ref[m] * k
     copies.append(pltpu.make_async_copy(new, new_out, sems.at[PIECES]))
     copies[-1].start()
@@ -180,40 +188,37 @@
     column_tiles = lax.all_to_all(tiles, TILES, 0, 0, tiled=True)
     other = lax.ppermute(momentum, "path_2", [(0, 1), (1, 0)])
     module_tiles = shape((modules, 8, 128), jnp.float32)
-    chunk_rows = shape((peers * CHUNK, 128), jnp.int32)
-    chunks, *packed = kernel(
+    packed = kernel(
         momentum_kernel,
         "pack_momentum",
         out_shape=(
-            chunk_rows,
             shape((modules, 8, 128), jnp.int32),
+            shape((modules, 128), jnp.int32),
             module_tiles,
             shape((modules, 128), jnp.float32),
         ),
         in_specs=[SMEM, VMEM, VMEM],
         out_specs=(VMEM,) * 4,
-        scratch_shapes=[
-            pltpu.VMEM((modules, 8, 128), jnp.int32),
-            pltpu.SMEM((modules,), jnp.int32),
-        ],
+        scratch_shapes=[pltpu.SMEM((modules,), jnp.int32)],
     )(path_module, momentum, other)
-    _, chunks, grad = kernel(
+    chunks, grad = kernel(
         gather_kernel,
         "gather_modules",
-        out_shape=(chunk_rows, chunk_rows, module_tiles),
+        out_shape=(shape((peers * CHUNK, 128), jnp.int32), module_tiles),
         in_specs=[SMEM, VMEM, VMEM, VMEM, VMEM, VMEM],
-        out_specs=(VMEM, HBM, VMEM),
-        input_output_aliases={5: 0},
+        out_specs=(HBM, VMEM),
         scratch_shapes=[pltpu.VMEM((modules, 8, 128), jnp.float32)] * 4
         + [
-            pltpu.VMEM((modules, 8, 128), jnp.int32),
+            pltpu.VMEM((modules, 16, 128), jnp.int32),
+            pltpu.VMEM((peers * CHUNK, 128), jnp.int32),
             pltpu.SemaphoreType.DMA((PIECES,)),
         ],
-    )(path_module, column_tiles, *packed, chunks)
+    )(path_module, column_tiles, *packed)
     chunks = lax.all_to_all(chunks.reshape(peers, CHUNK, 1, 128), TILES, 0, 0, tiled=True)
     other = lax.ppermute(grad, "path_2", [(0, 1), (1, 0)])
     chunks, other = lax.optimization_barrier((chunks, other))
-    squares = jnp.sum(chunks[:, SQUARES].astype(jnp.float32) * (1.0 / SQUARES_SCALE), axis=0)
+    squares = lax.shift_right_logical(chunks[:, UPPER], 24).astype(jnp.float32)
+    squares = jnp.sum(squares, axis=0)
     squares = lax.all_to_all(
         jnp.broadcast_to(squares, (shards, 1, 128)), "shard", 0, 0, tiled=True
     )

time: 63.9 us -> 63.3 us (level)
  waiting for transfers between devices: 25.7 us -> 25 us
    all_to_all x1, waiting for transfers between devices: 11.5 us -> 10.8 us  [local(): lax.all_to_all(chunks.reshape(peers, CHUNK, 1, 128), TILES, 0, 0, tiled=T...]
where the time goes in v5:
time: 63.3 us; the launch traced here: 62.5 us
  starting transfers between devices  32 us (51%)
  waiting for transfers between devices  25 us (39%)
  Pallas kernels  4.14 us (7%)
  between operations  0.71 us (1%)
    all_to_all x1, starting transfers between devices, local(): column_tiles = lax.all_to_all(tiles, TILES, 0, 0, tiled=True)  15.1 us
    all_to_all x1, waiting for transfers between devices, local(): lax.all_to_all(chunks.reshape(peers, CHUNK, 1, 128), TILES, 0, 0, tiled=T...  10.8 us
    all_to_all x1, starting transfers between devices, local(): lax.all_to_all(jnp.broadcast_to(squares, (shards, 1, 128)), 'shard', 0, 0...  6.82 us
    all_to_all x1, waiting for transfers between devices, local(): column_tiles = lax.all_to_all(tiles, TILES, 0, 0, tiled=True)  6.64 us
    all_to_all x1, waiting for transfers between devices, local(): lax.all_to_all(jnp.broadcast_to(squares, (shards, 1, 128)), 'shard', 0, 0...  5.71 us
    all_to_all x1, starting transfers between devices, local(): lax.all_to_all(chunks.reshape(peers, CHUNK, 1, 128), TILES, 0, 0, tiled=T...  5.54 us
    ppermute x1, starting transfers between devices, local(): other = lax.ppermute(momentum, 'path_2', [(0, 1), (1, 0)])  2.26 us
    ppermute x1, starting transfers between devices, local(): other = lax.ppermute(grad, 'path_2', [(0, 1), (1, 0)])  2.26 us
  transfers between devices with their start and end apart: 5, of which 5 were waited for; matrix products, arithmetic and copies ran while one was open for 0% of the time, Pallas kernels for 3%

profile of v5, /device:TPU:1, one launch (start us, length us, event | category | flops | bytes accessed | tf_op | source)
XLA Modules:
  0.0 62.5 jit_solution(2160203418971704038)
XLA Ops:
  0.6 0.0 copy-start
  0.6 0.0 copy-start.1
  0.6 15.1 %all-to-all-start = ((bf16[64,8,128]{2,1,0:T(8,128)(2,1)}), bf16[64,8,128]{2,1,0:T(8,128)(2,1)S(1)}, u32[]{:S(2)}, u32[]{:S(2)}) async-start(bf16[64,8,128]{2,1,0:T(8,128)(2,1)} %bitcast.15), calls=%async_computation | async-start | bytes 262144 | tf_op jit(solution)/shard_map/all_to_all | solution.py:188
  15.7 0.0 copy-done
  15.7 2.3 %collective-permute-start = (f32[16,16,64]{2,1,0:T(8,128)S(1)}, f32[16,16,64]{2,1,0:T(8,128)S(1)}, u32[]{:S(2)}, u32[]{:S(2)}) collective-permute-start(f32[16,16,64]{2,1,0:T(8,128)S(1)} %copy-done), channel_id=1, source_target_pairs={{0,8},{8,0},{1,9},{9,1},{2,10},{10,2},{3,11},{11,3},{4,12},{12,4},... | collective-permute-start | bytes 196616 | tf_op jit(solution)/shard_map/ppermute | solution.py:189
  18.0 1.0 %collective-permute-done.other_ref = f32[16,16,64]{2,1,0:T(8,128)S(1)} collective-permute-done((f32[16,16,64]{2,1,0:T(8,128)S(1)}, f32[16,16,64]{2,1,0:T(8,128)S(1)}, u32[]{:S(2)}, u32[]{:S(2)}) %collective-permute-start) | collective-permute-done | bytes 65568 | tf_op jit(solution)/shard_map/ppermute | solution.py:189
  19.0 0.0 copy-done.1
  19.0 0.8 %pack_momentum.1 = (s32[16,8,128]{2,1,0:T(8,128)S(1)}, s32[16,128]{1,0:T(8,128)S(1)}, f32[16,8,128]{2,1,0:T(8,128)S(1)}, f32[16,128]{1,0:T(8,128)S(1)}) custom-call(s32[64]{0:T(128)S(1)} %copy-done.1, f32[16,16,64]{2,1,0:T(8,128)S(1)} %copy-done, f32[16,16,64]{2,1,0:T(8,128)S(1)} %collective-permute-done.other_ref), custom_call_target="tpu_custom_call" | custom-call | tf_op jit(solution)/shard_map/pack_momentum/pallas_call | solution.py:191
  19.8 6.6 %all-to-all-done.column_ref = bf16[64,8,128]{2,1,0:T(8,128)(2,1)S(1)} async-done(((bf16[64,8,128]{2,1,0:T(8,128)(2,1)}), bf16[64,8,128]{2,1,0:T(8,128)(2,1)S(1)}, u32[]{:S(2)}, u32[]{:S(2)}) %all-to-all-start) | async-done | bytes 131104 | tf_op jit(solution)/shard_map/all_to_all | solution.py:188
  26.5 1.6 %gather_modules.1 = (s32[576,128]{1,0:T(8,128)}, f32[16,8,128]{2,1,0:T(8,128)S(1)}) custom-call(s32[64]{0:T(128)S(1)} %copy-done.1, bf16[64,8,128]{2,1,0:T(8,128)(2,1)S(1)} %all-to-all-done.column_ref, s32[16,8,128]{2,1,0:T(8,128)S(1)} %get-tuple-element.16.lower_ref, s32[16,128]{1,0:T(8,128)S(1)} %get-tuple-element.17.upper_ref, ...), custom_call_target="tpu_custom_call" | custom-call | tf_op jit(solution)/shard_map/gather_modules/pallas_call | solution.py:204
  28.0 5.5 %all-to-all-start.1 = ((s32[64,9,1,128]{3,2,1,0:T(1,128)}), s32[64,9,1,128]{3,2,1,0:T(1,128)S(1)}, u32[]{:S(2)}, u32[]{:S(2)}) async-start(s32[64,9,1,128]{3,2,1,0:T(1,128)} %bitcast.3), calls=%async_computation.1 | async-start | bytes 589824 | tf_op jit(solution)/shard_map/all_to_all | solution.py:217
  33.6 2.3 %collective-permute-start.1 = (f32[16,8,128]{2,1,0:T(8,128)S(1)}, f32[16,8,128]{2,1,0:T(8,128)S(1)}, u32[]{:S(2)}, u32[]{:S(2)}) collective-permute-start(f32[16,8,128]{2,1,0:T(8,128)S(1)} %get-tuple-element.21.mine_ref), channel_id=1, source_target_pairs={{0,8},{8,0},{1,9},{9,1},{2,10},{10,2},{3,11},{11,3},{4,12},{12,4},... | collective-permute-start | bytes 196616 | tf_op jit(solution)/shard_map/ppermute | solution.py:218
  35.9 0.9 %collective-permute-done.1.other_ref = f32[16,8,128]{2,1,0:T(8,128)S(1)} collective-permute-done((f32[16,8,128]{2,1,0:T(8,128)S(1)}, f32[16,8,128]{2,1,0:T(8,128)S(1)}, u32[]{:S(2)}, u32[]{:S(2)}) %collective-permute-start.1) | collective-permute-done | bytes 65568 | tf_op jit(solution)/shard_map/ppermute | solution.py:218
  36.7 10.8 %all-to-all-done.1 = s32[64,9,1,128]{3,2,1,0:T(1,128)S(1)} async-done(((s32[64,9,1,128]{3,2,1,0:T(1,128)}), s32[64,9,1,128]{3,2,1,0:T(1,128)S(1)}, u32[]{:S(2)}, u32[]{:S(2)}) %all-to-all-start.1) | async-done | bytes 294944 | tf_op jit(solution)/shard_map/all_to_all | solution.py:217
  47.6 0.1 convert_reduce_fusion
  47.7 0.6 broadcast_in_dim.3
  48.3 6.8 %all-to-all-start.2 = ((f32[8,1,128]{2,1,0:T(1,128)}), f32[8,1,128]{2,1,0:T(1,128)S(1)}, u32[]{:S(2)}, u32[]{:S(2)}) async-start(f32[8,1,128]{2,1,0:T(1,128)} %broadcast_in_dim.3), calls=%async_computation.2 | async-start | bytes 8192 | tf_op jit(solution)/shard_map/all_to_all | solution.py:222
  55.1 0.7 %assemble.1 = (f32[64,8,128]{2,1,0:T(8,128)S(1)}, f32[64,8,128]{2,1,0:T(8,128)S(1)}, f32[16,16,64]{2,1,0:T(8,128)S(1)}, f32[1,128]{1,0:T(1,128)S(1)}) custom-call(s32[64]{0:T(128)S(1)} %copy-done.1, s32[576,128]{1,0:T(8,128)S(1)} %bitcast.13, f32[16,8,128]{2,1,0:T(8,128)S(1)} %get-tuple-element.21.mine_ref, f32[16,8,128]{2,1,0:T(8,128)S(1)} %collective-permute-done.1.other_ref), custom_call_target="tpu_custom_call" | custom-call | tf_op jit(solution)/shard_map/assemble/pallas_call | solution.py:226
  55.8 5.7 %all-to-all-done.2 = f32[8,1,128]{2,1,0:T(1,128)S(1)} async-done(((f32[8,1,128]{2,1,0:T(1,128)}), f32[8,1,128]{2,1,0:T(1,128)S(1)}, u32[]{:S(2)}, u32[]{:S(2)}) %all-to-all-start.2) | async-done | bytes 4128 | tf_op jit(solution)/shard_map/all_to_all | solution.py:222
  61.5 1.0 %step.1 = (bf16[64,8,128]{2,1,0:T(8,128)(2,1)}, f32[16,16,64]{2,1,0:T(8,128)}) custom-call(f32[8,128]{1,0:T(8,128)S(1)} %bitcast.14, f32[64,8,128]{2,1,0:T(8,128)S(1)} %get-tuple-element.24.refs_1_, f32[64,8,128]{2,1,0:T(8,128)S(1)} %get-tuple-element.25.refs_2_, f32[16,16,64]{2,1,0:T(8,128)S(1)} %get-tuple-element.26.refs_3_, ...), custom_call_target="tpu_custom_call" | custom-call | tf_op jit(solution)/shard_map/step/pallas_call | solution.py:239
Async XLA Ops:
  0.6 15.1 %copy-start = (f32[16,16,64]{2,1,0:T(8,128)S(1)}, f32[16,16,64]{2,1,0:T(8,128)}, u32[]{:S(2)}) copy-start(f32[16,16,64]{2,1,0:T(8,128)} %refs_5_.1) | copy-start | bytes 196612
  0.6 18.4 %copy-start.1 = (s32[64]{0:T(128)S(1)}, s32[64]{0:T(128)}, u32[]{:S(2)}) copy-start(s32[64]{0:T(128)} %module_ref.5) | copy-start | bytes 772
  0.6 25.8 %all-to-all-start = ((bf16[64,8,128]{2,1,0:T(8,128)(2,1)}), bf16[64,8,128]{2,1,0:T(8,128)(2,1)S(1)}, u32[]{:S(2)}, u32[]{:S(2)}) async-start(bf16[64,8,128]{2,1,0:T(8,128)(2,1)} %bitcast.15), calls=%async_computation | async-start | bytes 262144 | tf_op jit(solution)/shard_map/all_to_all | solution.py:188
  15.7 3.2 %collective-permute-start = (f32[16,16,64]{2,1,0:T(8,128)S(1)}, f32[16,16,64]{2,1,0:T(8,128)S(1)}, u32[]{:S(2)}, u32[]{:S(2)}) collective-permute-start(f32[16,16,64]{2,1,0:T(8,128)S(1)} %copy-done), channel_id=1, source_target_pairs={{0,8},{8,0},{1,9},{9,1},{2,10},{10,2},{3,11},{11,3},{4,12},{12,4},... | collective-permute-start | bytes 196616 | tf_op jit(solution)/shard_map/ppermute | solution.py:189
  28.0 19.5 %all-to-all-start.1 = ((s32[64,9,1,128]{3,2,1,0:T(1,128)}), s32[64,9,1,128]{3,2,1,0:T(1,128)S(1)}, u32[]{:S(2)}, u32[]{:S(2)}) async-start(s32[64,9,1,128]{3,2,1,0:T(1,128)} %bitcast.3), calls=%async_computation.1 | async-start | bytes 589824 | tf_op jit(solution)/shard_map/all_to_all | solution.py:217
  33.6 3.2 %collective-permute-start.1 = (f32[16,8,128]{2,1,0:T(8,128)S(1)}, f32[16,8,128]{2,1,0:T(8,128)S(1)}, u32[]{:S(2)}, u32[]{:S(2)}) collective-permute-start(f32[16,8,128]{2,1,0:T(8,128)S(1)} %get-tuple-element.21.mine_ref), channel_id=1, source_target_pairs={{0,8},{8,0},{1,9},{9,1},{2,10},{10,2},{3,11},{11,3},{4,12},{12,4},... | collective-permute-start | bytes 196616 | tf_op jit(solution)/shard_map/ppermute | solution.py:218
  48.3 13.3 %all-to-all-start.2 = ((f32[8,1,128]{2,1,0:T(1,128)}), f32[8,1,128]{2,1,0:T(1,128)S(1)}, u32[]{:S(2)}, u32[]{:S(2)}) async-start(f32[8,1,128]{2,1,0:T(1,128)} %broadcast_in_dim.3), calls=%async_computation.2 | async-start | bytes 8192 | tf_op jit(solution)/shard_map/all_to_all | solution.py:222

commit v6 on v5

--- a/solution.py
+++ b/solution.py
@@ -44,13 +44,16 @@
 
 
 def momentum_kernel(
-    module_ref, mine_ref, other_ref, lower_ref, upper_ref, fold_ref, count_ref, count
+    module_ref, mine_ref, other_ref, lower_ref, upper_ref, fold_ref, count_ref, own_ref, count
 ):
     peers, modules = module_ref.shape[0], mine_ref.shape[0]
     for m in range(modules):
         count[m] = 0
     for q in range(peers):
         count[module_ref[q]] += 1
+    chip = lax.axis_index("path_0") * lax.axis_size("path_1") + lax.axis_index("path_1")
+    module = module_ref[chip * 2 + lax.axis_index("path_2")]
+    own_ref[...] = (lanes()[0:1, :] == 4 * module).astype(jnp.float32)
     first_core = lax.axis_index("path_2") == 0
     row = lax.broadcasted_iota(jnp.int32, (8, 128), 0)
     for m in range(modules):
@@ -119,35 +122,17 @@
         copy.wait()
 
 
-def assemble_kernel(
-    module_ref, chunk_ref, mine_ref, other_ref, grad_ref, decay_ref, own_grad_ref, own_ref
-):
-    peers, modules = grad_ref.shape[0], mine_ref.shape[0]
+def columns_kernel(mine_ref, other_ref, grad_ref):
     core = lax.axis_index("path_2")
-    chip = lax.axis_index("path_0") * lax.axis_size("path_1") + lax.axis_index("path_1")
-    module = module_ref[chip * 2 + core]
-    power = (chunk_ref[pl.ds(UPPER, peers, stride=CHUNK), :] >> 24) & 255
-    scale = 1.0 / jnp.exp2(GRAD_BITS + BIAS - power.astype(jnp.float32))
-    row = lax.broadcasted_iota(jnp.int32, (8, 128), 0)
-    own_lane = lanes() == EXPONENTS + row
-    for q in range(peers):
-        start = q * CHUNK
-        words = chunk_ref[start : start + UPPER, :]
-        of_row = jnp.sum(jnp.where(own_lane, scale[q : q + 1, :], 0.0), axis=1, keepdims=True)
-        grad_ref[q] = (words >> LOWER_BITS).astype(jnp.float32) * of_row
-        upper = (chunk_ref[start + UPPER : start + CHUNK, :] >> (row * 3)) & 7
-        whole = ((upper << LOWER_BITS) | (words & ((1 << LOWER_BITS) - 1))) - 32768
-        decay_ref[q] = whole.astype(jnp.float32) * (momentum_rate / MOMENTUM_SCALE)
-    for m in range(modules):
+    for m in range(mine_ref.shape[0]):
         for half in range(2):
             grad = jnp.where(core == half, mine_ref[m], other_ref[m])
             grad = jnp.where(core == 0, grad, pltpu.roll(grad, 64, 1))
-            own_grad_ref[m, half * 8 : half * 8 + 8, :] = grad[:, 0:64]
-    own_ref[...] = (lanes()[0:1, :] == 4 * module).astype(jnp.float32)
+            grad_ref[m, half * 8 : half * 8 + 8, :] = grad[:, 0:64]
 
 
 def step_kernel(
-    limit, squares_ref, grad_ref, decay_ref, own_grad_ref, own_ref, momentum_ref,
+    limit, squares_ref, chunk_ref, own_grad_ref, own_ref, momentum_ref,
     update_out, new_out, update, new, sems,
 ):
     peers, modules = update.shape[0], new.shape[0]
@@ -160,15 +145,27 @@
     norm_squares = (norm_squares + pltpu.roll(norm_squares, 126, 1))[0:1, :]
     shrink = jnp.minimum(1.0, limit / jnp.sqrt(norm_squares + 1e-06))
     own = jnp.sum(jnp.where(own_ref[...] > 0.0, shrink, 0.0), axis=1, keepdims=True)
+    power = lax.shift_right_logical(chunk_ref[pl.ds(UPPER, peers, stride=CHUNK), :], 24)
+    scale = own / jnp.exp2(GRAD_BITS + BIAS - power.astype(jnp.float32))
+    row = lax.broadcasted_iota(jnp.int32, (8, 128), 0)
+    own_lane = lane == EXPONENTS + row
     each = peers // PIECES
     copies = []
-    for piece in range(PIECES):
-        tiles = slice(piece * each, (piece + 1) * each)
-        clipped = grad_ref[tiles] * own.reshape(1, 1, 1)
-        step = outer_rate * (clipped + momentum_rate * (decay_ref[tiles] + clipped))
-        update[tiles] = step.astype(jnp.bfloat16)
-        copies.append(pltpu.make_async_copy(update.at[tiles], update_out.at[tiles], sems.at[piece]))
-        copies[-1].start()
+    for q in range(peers):
+        start = q * CHUNK
+        words = chunk_ref[start : start + UPPER, :]
+        of_row = jnp.sum(jnp.where(own_lane, scale[q : q + 1, :], 0.0), axis=1, keepdims=True)
+        clipped = (words >> LOWER_BITS).astype(jnp.float32) * of_row
+        upper = (chunk_ref[start + UPPER : start + CHUNK, :] >> (row * 3)) & 7
+        whole = ((upper << LOWER_BITS) | (words & ((1 << LOWER_BITS) - 1))) - 32768
+        decay = whole.astype(jnp.float32) * (momentum_rate / MOMENTUM_SCALE)
+        step = outer_rate * (clipped + momentum_rate * (decay + clipped))
+        update[q] = step.astype(jnp.bfloat16)
+        if (q + 1) % each == 0:
+            piece = pl.ds(q + 1 - each, each)
+            sem = sems.at[len(copies)]
+            copies.append(pltpu.make_async_copy(update.at[piece], update_out.at[piece], sem))
+            copies[-1].start()
     for m in range(modules):
         k = jnp.sum(jnp.where(lane[0:1, :] == 4 * m, shrink, 0.0), axis=1, keepdims=True)
         new[m] = momentum_rate * momentum_ref[m] + own_grad_ref[m] * k
@@ -188,7 +185,7 @@
     column_tiles = lax.all_to_all(tiles, TILES, 0, 0, tiled=True)
     other = lax.ppermute(momentum, "path_2", [(0, 1), (1, 0)])
     module_tiles = shape((modules, 8, 128), jnp.float32)
-    packed = kernel(
+    *packed, own = kernel(
         momentum_kernel,
         "pack_momentum",
         out_shape=(
@@ -196,9 +193,10 @@
             shape((modules, 128), jnp.int32),
             module_tiles,
             shape((modules, 128), jnp.float32),
+            shape((1, 128), jnp.float32),
         ),
         in_specs=[SMEM, VMEM, VMEM],
-        out_specs=(VMEM,) * 4,
+        out_specs=(VMEM,) * 5,
         scratch_shapes=[pltpu.SMEM((modules,), jnp.int32)],
     )(path_module, momentum, other)
     chunks, grad = kernel(
@@ -216,25 +214,19 @@
     )(path_module, column_tiles, *packed)
     chunks = lax.all_to_all(chunks.reshape(peers, CHUNK, 1, 128), TILES, 0, 0, tiled=True)
     other = lax.ppermute(grad, "path_2", [(0, 1), (1, 0)])
-    chunks, other = lax.optimization_barrier((chunks, other))
+    columns_grad = kernel(
+        columns_kernel,
+        "state_columns",
+        out_shape=shape(momentum.shape, jnp.float32),
+        in_specs=[VMEM] * 2,
+        out_specs=VMEM,
+    )(grad, other)
+    chunks, columns_grad = lax.optimization_barrier((chunks, columns_grad))
     squares = lax.shift_right_logical(chunks[:, UPPER], 24).astype(jnp.float32)
     squares = jnp.sum(squares, axis=0)
     squares = lax.all_to_all(
         jnp.broadcast_to(squares, (shards, 1, 128)), "shard", 0, 0, tiled=True
     )
-    path_tiles = shape((peers, 8, 128), jnp.float32)
-    assembled = kernel(
-        assemble_kernel,
-        "assemble",
-        out_shape=(
-            path_tiles,
-            path_tiles,
-            shape(momentum.shape, jnp.float32),
-            shape((1, 128), jnp.float32),
-        ),
-        in_specs=[SMEM, VMEM, VMEM, VMEM],
-        out_specs=(VMEM,) * 4,
-    )(path_module, chunks.reshape(peers * CHUNK, 128), grad, other)
     limit = clip_ratio * float(rows * shards * columns) ** 0.5
     update, new_momentum = kernel(
         lambda *refs: step_kernel(limit, *refs),
@@ -243,14 +235,20 @@
             shape((peers, 8, 128), jnp.bfloat16),
             shape(momentum.shape, jnp.float32),
         ),
-        in_specs=[VMEM] * 6,
+        in_specs=[VMEM] * 5,
         out_specs=(HBM, HBM),
         scratch_shapes=[
             pltpu.VMEM((peers, 8, 128), jnp.bfloat16),
             pltpu.VMEM(momentum.shape, jnp.float32),
             pltpu.SemaphoreType.DMA((PIECES + 1,)),
         ],
-    )(squares.reshape(shards, 128), *assembled, momentum)
+    )(
+        squares.reshape(shards, 128),
+        chunks.reshape(peers * CHUNK, 128),
+        columns_grad,
+        own,
+        momentum,
+    )
     update = update.reshape(2, peers // 2, 8, 128).transpose(0, 2, 1, 3).reshape(deltas.shape)
     return (update, new_momentum)
 

time: 63.3 us -> 62.7 us (level)
  blocking collectives: 0 us -> 13.1 us
  starting transfers between devices: 32 us -> 25.1 us
  waiting for transfers between devices: 25 us -> 19.2 us
    all_to_all x0 -> x1, blocking collectives: none -> 13.1 us  [local(): lax.all_to_all(jnp.broadcast_to(squares, (shards, 1, 128)), 'shard', 0, 0...]
    all_to_all x1 -> x0, starting transfers between devices: 6.82 us -> none  [local(): lax.all_to_all(jnp.broadcast_to(squares, (shards, 1, 128)), 'shard', 0, 0...]
    all_to_all x1 -> x0, waiting for transfers between devices: 5.71 us -> none  [local(): lax.all_to_all(jnp.broadcast_to(squares, (shards, 1, 128)), 'shard', 0, 0...]
    pallas_call x1, Pallas kernels: 0.74 us -> 0.1 us  [local(): kernel(columns_kernel, 'state_columns', out_shape=shape(momentum.shape, j...]
  transfers between devices with their start and end apart: 5 -> 4, of which waited for: 5 -> 4; matrix products, arithmetic and copies ran while one was open for 0% -> 0% of each run, Pallas kernels for 3% -> 2%
where the time goes in v6:
time: 62.7 us; the launch traced here: 62 us
  starting transfers between devices  25.1 us (40%)
  waiting for transfers between devices  19.2 us (31%)
  blocking collectives  13.1 us (21%)
  Pallas kernels  3.66 us (6%)
  between operations  0.71 us (1%)
    all_to_all x1, starting transfers between devices, local(): column_tiles = lax.all_to_all(tiles, TILES, 0, 0, tiled=True)  15.1 us
    all_to_all x1, blocking collectives, local(): lax.all_to_all(jnp.broadcast_to(squares, (shards, 1, 128)), 'shard', 0, 0...  13.1 us
    all_to_all x1, waiting for transfers between devices, local(): lax.all_to_all(chunks.reshape(peers, CHUNK, 1, 128), TILES, 0, 0, tiled=T...  10.7 us
    all_to_all x1, waiting for transfers between devices, local(): column_tiles = lax.all_to_all(tiles, TILES, 0, 0, tiled=True)  6.64 us
    all_to_all x1, starting transfers between devices, local(): lax.all_to_all(chunks.reshape(peers, CHUNK, 1, 128), TILES, 0, 0, tiled=T...  5.54 us
    ppermute x1, starting transfers between devices, local(): other = lax.ppermute(momentum, 'path_2', [(0, 1), (1, 0)])  2.26 us
    ppermute x1, starting transfers between devices, local(): other = lax.ppermute(grad, 'path_2', [(0, 1), (1, 0)])  2.26 us
    pallas_call x1, Pallas kernels, local(): kernel(gather_kernel, 'gather_modules', out_shape=(shape((peers * CHUNK,...  1.58 us
  transfers between devices with their start and end apart: 4, of which 4 were waited for; matrix products, arithmetic and copies ran while one was open for 0% of the time, Pallas kernels for 2%

profile of v6, /device:TPU:1, one launch (start us, length us, event | category | flops | bytes accessed | tf_op | source)
XLA Modules:
  0.0 62.0 jit_solution(13808920736098077796)
XLA Ops:
  0.6 0.0 copy-start
  0.6 0.0 copy-start.1
  0.6 15.1 %all-to-all-start = ((bf16[64,8,128]{2,1,0:T(8,128)(2,1)}), bf16[64,8,128]{2,1,0:T(8,128)(2,1)S(1)}, u32[]{:S(2)}, u32[]{:S(2)}) async-start(bf16[64,8,128]{2,1,0:T(8,128)(2,1)} %bitcast.15), calls=%async_computation | async-start | bytes 262144 | tf_op jit(solution)/shard_map/all_to_all | solution.py:185
  15.7 0.0 copy-done
  15.7 2.3 %collective-permute-start = (f32[16,16,64]{2,1,0:T(8,128)S(1)}, f32[16,16,64]{2,1,0:T(8,128)S(1)}, u32[]{:S(2)}, u32[]{:S(2)}) collective-permute-start(f32[16,16,64]{2,1,0:T(8,128)S(1)} %copy-done), channel_id=1, source_target_pairs={{0,8},{8,0},{1,9},{9,1},{2,10},{10,2},{3,11},{11,3},{4,12},{12,4},... | collective-permute-start | bytes 196616 | tf_op jit(solution)/shard_map/ppermute | solution.py:186
  18.0 1.0 %collective-permute-done.other_ref = f32[16,16,64]{2,1,0:T(8,128)S(1)} collective-permute-done((f32[16,16,64]{2,1,0:T(8,128)S(1)}, f32[16,16,64]{2,1,0:T(8,128)S(1)}, u32[]{:S(2)}, u32[]{:S(2)}) %collective-permute-start) | collective-permute-done | bytes 65568 | tf_op jit(solution)/shard_map/ppermute | solution.py:186
  19.0 0.0 copy-done.1
  19.0 0.8 %pack_momentum.1 = (s32[16,8,128]{2,1,0:T(8,128)S(1)}, s32[16,128]{1,0:T(8,128)S(1)}, f32[16,8,128]{2,1,0:T(8,128)S(1)}, f32[16,128]{1,0:T(8,128)S(1)}, f32[1,128]{1,0:T(1,128)S(1)}) custom-call(s32[64]{0:T(128)S(1)} %copy-done.1, f32[16,16,64]{2,1,0:T(8,128)S(1)} %copy-done, f32[16,16,64]{2,1,0:T(8,128)S(1)} %collective-permute-done.other_ref), custom_call_target="tpu_custom_call" | custom-call | tf_op jit(solution)/shard_map/pack_momentum/pallas_call | solution.py:188
  19.8 6.6 %all-to-all-done.column_ref = bf16[64,8,128]{2,1,0:T(8,128)(2,1)S(1)} async-done(((bf16[64,8,128]{2,1,0:T(8,128)(2,1)}), bf16[64,8,128]{2,1,0:T(8,128)(2,1)S(1)}, u32[]{:S(2)}, u32[]{:S(2)}) %all-to-all-start) | async-done | bytes 131104 | tf_op jit(solution)/shard_map/all_to_all | solution.py:185
  26.5 1.6 %gather_modules.1 = (s32[576,128]{1,0:T(8,128)}, f32[16,8,128]{2,1,0:T(8,128)S(1)}) custom-call(s32[64]{0:T(128)S(1)} %copy-done.1, bf16[64,8,128]{2,1,0:T(8,128)(2,1)S(1)} %all-to-all-done.column_ref, s32[16,8,128]{2,1,0:T(8,128)S(1)} %get-tuple-element.13.lower_ref, s32[16,128]{1,0:T(8,128)S(1)} %get-tuple-element.14.upper_ref, ...), custom_call_target="tpu_custom_call" | custom-call | tf_op jit(solution)/shard_map/gather_modules/pallas_call | solution.py:202
  28.1 5.5 %all-to-all-start.1 = ((s32[64,9,1,128]{3,2,1,0:T(1,128)}), s32[64,9,1,128]{3,2,1,0:T(1,128)S(1)}, u32[]{:S(2)}, u32[]{:S(2)}) async-start(s32[64,9,1,128]{3,2,1,0:T(1,128)} %bitcast.3), calls=%async_computation.1 | async-start | bytes 589824 | tf_op jit(solution)/shard_map/all_to_all | solution.py:215
  33.6 2.3 %collective-permute-start.1 = (f32[16,8,128]{2,1,0:T(8,128)S(1)}, f32[16,8,128]{2,1,0:T(8,128)S(1)}, u32[]{:S(2)}, u32[]{:S(2)}) collective-permute-start(f32[16,8,128]{2,1,0:T(8,128)S(1)} %get-tuple-element.18.mine_ref), channel_id=1, source_target_pairs={{0,8},{8,0},{1,9},{9,1},{2,10},{10,2},{3,11},{11,3},{4,12},{12,4},... | collective-permute-start | bytes 196616 | tf_op jit(solution)/shard_map/ppermute | solution.py:216
  35.9 0.9 %collective-permute-done.1.other_ref = f32[16,8,128]{2,1,0:T(8,128)S(1)} collective-permute-done((f32[16,8,128]{2,1,0:T(8,128)S(1)}, f32[16,8,128]{2,1,0:T(8,128)S(1)}, u32[]{:S(2)}, u32[]{:S(2)}) %collective-permute-start.1) | collective-permute-done | bytes 65568 | tf_op jit(solution)/shard_map/ppermute | solution.py:216
  36.8 0.1 state_columns.1.refs_2_
  36.9 10.7 %all-to-all-done.1 = s32[64,9,1,128]{3,2,1,0:T(1,128)S(1)} async-done(((s32[64,9,1,128]{3,2,1,0:T(1,128)}), s32[64,9,1,128]{3,2,1,0:T(1,128)S(1)}, u32[]{:S(2)}, u32[]{:S(2)}) %all-to-all-start.1) | async-done | bytes 294944 | tf_op jit(solution)/shard_map/all_to_all | solution.py:215
  47.6 0.1 convert_reduce_fusion
  47.7 13.1 %all_to_all.15 = f32[8,1,128]{2,1,0:T(1,128)S(1)} all-to-all(f32[8,1,128]{2,1,0:T(1,128)S(1)} %broadcast_in_dim.3), channel_id=1, replica_groups=mesh['path_0'=4,'path_1'=8,'path_2'=2,'shard'=8] {'shard'}, dimensions={0} | all-to-all | bytes 8192 | tf_op jit(solution)/shard_map/all_to_all | solution.py:227
  60.8 1.1 %step.1 = (bf16[64,8,128]{2,1,0:T(8,128)(2,1)}, f32[16,16,64]{2,1,0:T(8,128)}) custom-call(f32[8,128]{1,0:T(8,128)S(1)} %bitcast.14, s32[576,128]{1,0:T(8,128)S(1)} %bitcast.13, f32[16,16,64]{2,1,0:T(8,128)S(1)} %state_columns.1.refs_2_, f32[1,128]{1,0:T(1,128)S(1)} %get-tuple-element.21.refs_3_, f32[16,16,64]{2,1,0:T(8,128)S(1)} %copy-done), custom_call_target="tpu_custom_call" | custom-call | tf_op jit(solution)/shard_map/step/pallas_call | solution.py:231
  (1 shorter events, 0.0 us)
Async XLA Ops:
  0.6 15.1 %copy-start = (f32[16,16,64]{2,1,0:T(8,128)S(1)}, f32[16,16,64]{2,1,0:T(8,128)}, u32[]{:S(2)}) copy-start(f32[16,16,64]{2,1,0:T(8,128)} %refs_4_.1) | copy-start | bytes 196612
  0.6 18.4 %copy-start.1 = (s32[64]{0:T(128)S(1)}, s32[64]{0:T(128)}, u32[]{:S(2)}) copy-start(s32[64]{0:T(128)} %module_ref.3) | copy-start | bytes 772
  0.6 25.8 %all-to-all-start = ((bf16[64,8,128]{2,1,0:T(8,128)(2,1)}), bf16[64,8,128]{2,1,0:T(8,128)(2,1)S(1)}, u32[]{:S(2)}, u32[]{:S(2)}) async-start(bf16[64,8,128]{2,1,0:T(8,128)(2,1)} %bitcast.15), calls=%async_computation | async-start | bytes 262144 | tf_op jit(solution)/shard_map/all_to_all | solution.py:185
  15.7 3.2 %collective-permute-start = (f32[16,16,64]{2,1,0:T(8,128)S(1)}, f32[16,16,64]{2,1,0:T(8,128)S(1)}, u32[]{:S(2)}, u32[]{:S(2)}) collective-permute-start(f32[16,16,64]{2,1,0:T(8,128)S(1)} %copy-done), channel_id=1, source_target_pairs={{0,8},{8,0},{1,9},{9,1},{2,10},{10,2},{3,11},{11,3},{4,12},{12,4},... | collective-permute-start | bytes 196616 | tf_op jit(solution)/shard_map/ppermute | solution.py:186
  28.1 19.5 %all-to-all-start.1 = ((s32[64,9,1,128]{3,2,1,0:T(1,128)}), s32[64,9,1,128]{3,2,1,0:T(1,128)S(1)}, u32[]{:S(2)}, u32[]{:S(2)}) async-start(s32[64,9,1,128]{3,2,1,0:T(1,128)} %bitcast.3), calls=%async_computation.1 | async-start | bytes 589824 | tf_op jit(solution)/shard_map/all_to_all | solution.py:215
  33.6 3.2 %collective-permute-start.1 = (f32[16,8,128]{2,1,0:T(8,128)S(1)}, f32[16,8,128]{2,1,0:T(8,128)S(1)}, u32[]{:S(2)}, u32[]{:S(2)}) collective-permute-start(f32[16,8,128]{2,1,0:T(8,128)S(1)} %get-tuple-element.18.mine_ref), channel_id=1, source_target_pairs={{0,8},{8,0},{1,9},{9,1},{2,10},{10,2},{3,11},{11,3},{4,12},{12,4},... | collective-permute-start | bytes 196616 | tf_op jit(solution)/shard_map/ppermute | solution.py:216

commit v7 on v6

--- a/solution.py
+++ b/solution.py
@@ -16,6 +16,7 @@
 UPPER, CHUNK = 8, 9
 GRAD_BITS, LOWER_BITS = 18, 13
 EXPONENTS, BIAS = 64, 128
+MODULE_BITS, PACKED = 4, 8
 MOMENTUM_SCALE = 8191.0
 SQUARES_SCALE = 128.0
 FOLD = momentum_rate * momentum_rate / (1.0 + momentum_rate)
@@ -44,13 +45,20 @@
 
 
 def momentum_kernel(
-    module_ref, mine_ref, other_ref, lower_ref, upper_ref, fold_ref, count_ref, own_ref, count
+    module_ref, mine_ref, other_ref,
+    lower_ref, upper_ref, fold_ref, count_ref, peer_ref, own_ref, count,
 ):
     peers, modules = module_ref.shape[0], mine_ref.shape[0]
     for m in range(modules):
         count[m] = 0
     for q in range(peers):
         count[module_ref[q]] += 1
+    for word in range(peers // PACKED):
+        packed = 0
+        for k in range(PACKED):
+            m = module_ref[path_of(word * PACKED + k, peers // 2)]
+            packed = packed | (m << (k * MODULE_BITS))
+        peer_ref[word : word + 1, :] = jnp.full((1, 128), packed)
     chip = lax.axis_index("path_0") * lax.axis_size("path_1") + lax.axis_index("path_1")
     module = module_ref[chip * 2 + lax.axis_index("path_2")]
     own_ref[...] = (lanes()[0:1, :] == 4 * module).astype(jnp.float32)
@@ -74,15 +82,19 @@
 
 
 def gather_kernel(
-    module_ref, column_ref, lower_ref, upper_ref, fold_ref, count_ref, chunk_out, grad_ref, *scratch
+    column_ref, lower_ref, upper_ref, fold_ref, count_ref, peer_ref, chunk_out, grad_ref, *scratch
 ):
     *sums, words, chunk, sems = scratch
     peers, modules = column_ref.shape[0], grad_ref.shape[0]
-    chips = peers // 2
+    packed = [peer_ref[word, 0] for word in range(peers // PACKED)]
+    module_of = [
+        (packed[q // PACKED] >> (q % PACKED * MODULE_BITS)) & (2**MODULE_BITS - 1)
+        for q in range(peers)
+    ]
     for total in sums:
         total[...] = jnp.zeros_like(total)
     for q in range(peers):
-        m = module_ref[path_of(q, chips)]
+        m = module_of[q]
         total = sums[q % len(sums)]
         total[m] += column_ref[q].astype(jnp.float32)
     for m in range(modules):
@@ -109,7 +121,7 @@
         words[m, UPPER:CHUNK, :] = upper_ref[m : m + 1, :] | ((norms + powers).astype(jnp.int32) << 24)
     copies = []
     for q in range(peers):
-        m = module_ref[path_of(q, chips)]
+        m = module_of[q]
         start = q * CHUNK
         chunk[start : start + UPPER, :] = words[m, 0:UPPER, :]
         chunk[start + UPPER : start + CHUNK, :] = words[m, UPPER:CHUNK, :]
@@ -193,17 +205,18 @@
             shape((modules, 128), jnp.int32),
             module_tiles,
             shape((modules, 128), jnp.float32),
+            shape((peers // PACKED, 128), jnp.int32),
             shape((1, 128), jnp.float32),
         ),
         in_specs=[SMEM, VMEM, VMEM],
-        out_specs=(VMEM,) * 5,
+        out_specs=(VMEM,) * 6,
         scratch_shapes=[pltpu.SMEM((modules,), jnp.int32)],
     )(path_module, momentum, other)
     chunks, grad = kernel(
         gather_kernel,
         "gather_modules",
         out_shape=(shape((peers * CHUNK, 128), jnp.int32), module_tiles),
-        in_specs=[SMEM, VMEM, VMEM, VMEM, VMEM, VMEM],
+        in_specs=[VMEM] * 6,
         out_specs=(HBM, VMEM),
         scratch_shapes=[pltpu.VMEM((modules, 8, 128), jnp.float32)] * 4
         + [
@@ -211,7 +224,7 @@
             pltpu.VMEM((peers * CHUNK, 128), jnp.int32),
             pltpu.SemaphoreType.DMA((PIECES,)),
         ],
-    )(path_module, column_tiles, *packed)
+    )(column_tiles, *packed)
     chunks = lax.all_to_all(chunks.reshape(peers, CHUNK, 1, 128), TILES, 0, 0, tiled=True)
     other = lax.ppermute(grad, "path_2", [(0, 1), (1, 0)])
     columns_grad = kernel(

time: 62.7 us -> 62.2 us (level)
  no operation moved by 1% of the time
where the time goes in v7:
time: 62.2 us; the launch traced here: 61.5 us
  starting transfers between devices  25.1 us (40%)
  waiting for transfers between devices  19.2 us (31%)
  blocking collectives  13.1 us (21%)
  Pallas kernels  3.18 us (5%)
  between operations  0.71 us (1%)
    all_to_all x1, starting transfers between devices, local(): column_tiles = lax.all_to_all(tiles, TILES, 0, 0, tiled=True)  15.1 us
    all_to_all x1, blocking collectives, local(): lax.all_to_all(jnp.broadcast_to(squares, (shards, 1, 128)), 'shard', 0, 0...  13.1 us
    all_to_all x1, waiting for transfers between devices, local(): lax.all_to_all(chunks.reshape(peers, CHUNK, 1, 128), TILES, 0, 0, tiled=T...  10.7 us
    all_to_all x1, waiting for transfers between devices, local(): column_tiles = lax.all_to_all(tiles, TILES, 0, 0, tiled=True)  6.62 us
    all_to_all x1, starting transfers between devices, local(): lax.all_to_all(chunks.reshape(peers, CHUNK, 1, 128), TILES, 0, 0, tiled=T...  5.54 us
    ppermute x1, starting transfers between devices, local(): other = lax.ppermute(momentum, 'path_2', [(0, 1), (1, 0)])  2.26 us
    ppermute x1, starting transfers between devices, local(): other = lax.ppermute(grad, 'path_2', [(0, 1), (1, 0)])  2.26 us
  transfers between devices with their start and end apart: 4, of which 4 were waited for; matrix products, arithmetic and copies ran while one was open for 0% of the time, Pallas kernels for 2%

profile of v7, /device:TPU:1, one launch (start us, length us, event | category | flops | bytes accessed | tf_op | source)
XLA Modules:
  0.0 61.5 jit_solution(3340226774583511535)
XLA Ops:
  0.6 0.0 copy-start
  0.6 0.0 copy-start.1
  0.6 15.1 %all-to-all-start = ((bf16[64,8,128]{2,1,0:T(8,128)(2,1)}), bf16[64,8,128]{2,1,0:T(8,128)(2,1)S(1)}, u32[]{:S(2)}, u32[]{:S(2)}) async-start(bf16[64,8,128]{2,1,0:T(8,128)(2,1)} %bitcast.15), calls=%async_computation | async-start | bytes 262144 | tf_op jit(solution)/shard_map/all_to_all | solution.py:197
  15.7 0.0 copy-done
  15.7 2.3 %collective-permute-start = (f32[16,16,64]{2,1,0:T(8,128)S(1)}, f32[16,16,64]{2,1,0:T(8,128)S(1)}, u32[]{:S(2)}, u32[]{:S(2)}) collective-permute-start(f32[16,16,64]{2,1,0:T(8,128)S(1)} %copy-done), channel_id=1, source_target_pairs={{0,8},{8,0},{1,9},{9,1},{2,10},{10,2},{3,11},{11,3},{4,12},{12,4},... | collective-permute-start | bytes 196616 | tf_op jit(solution)/shard_map/ppermute | solution.py:198
  18.0 1.0 %collective-permute-done.other_ref = f32[16,16,64]{2,1,0:T(8,128)S(1)} collective-permute-done((f32[16,16,64]{2,1,0:T(8,128)S(1)}, f32[16,16,64]{2,1,0:T(8,128)S(1)}, u32[]{:S(2)}, u32[]{:S(2)}) %collective-permute-start) | collective-permute-done | bytes 65568 | tf_op jit(solution)/shard_map/ppermute | solution.py:198
  19.0 0.0 copy-done.1
  19.0 0.9 %pack_momentum.1 = (s32[16,8,128]{2,1,0:T(8,128)S(1)}, s32[16,128]{1,0:T(8,128)S(1)}, f32[16,8,128]{2,1,0:T(8,128)S(1)}, f32[16,128]{1,0:T(8,128)S(1)}, s32[8,128]{1,0:T(8,128)S(1)}, /*index=5*/f32[1,128]{1,0:T(1,128)S(1)}) custom-call(s32[64]{0:T(128)S(1)} %copy-done.1, f32[16,16,64]{2,1,0:T(8,128)S(1)} %copy-done, ...), custom_call_target="tpu_custom_call" | custom-call | tf_op jit(solution)/shard_map/pack_momentum/pallas_call | solution.py:200
  19.9 6.6 %all-to-all-done.column_ref = bf16[64,8,128]{2,1,0:T(8,128)(2,1)S(1)} async-done(((bf16[64,8,128]{2,1,0:T(8,128)(2,1)}), bf16[64,8,128]{2,1,0:T(8,128)(2,1)S(1)}, u32[]{:S(2)}, u32[]{:S(2)}) %all-to-all-start) | async-done | bytes 131104 | tf_op jit(solution)/shard_map/all_to_all | solution.py:197
  26.5 1.1 %gather_modules.1 = (s32[576,128]{1,0:T(8,128)}, f32[16,8,128]{2,1,0:T(8,128)S(1)}) custom-call(bf16[64,8,128]{2,1,0:T(8,128)(2,1)S(1)} %all-to-all-done.column_ref, s32[16,8,128]{2,1,0:T(8,128)S(1)} %get-tuple-element.14.lower_ref, s32[16,128]{1,0:T(8,128)S(1)} %get-tuple-element.15.upper_ref, f32[16,8,128]{2,1,0:T(8,128)S(1)} %get-tuple-element.16.fold_ref, ...), custom_call_target="tpu_custom_call" | custom-call | tf_op jit(solution)/shard_map/gather_modules/pallas_call | solution.py:215
  27.6 5.5 %all-to-all-start.1 = ((s32[64,9,1,128]{3,2,1,0:T(1,128)}), s32[64,9,1,128]{3,2,1,0:T(1,128)S(1)}, u32[]{:S(2)}, u32[]{:S(2)}) async-start(s32[64,9,1,128]{3,2,1,0:T(1,128)} %bitcast.3), calls=%async_computation.1 | async-start | bytes 589824 | tf_op jit(solution)/shard_map/all_to_all | solution.py:228
  33.1 2.3 %collective-permute-start.1 = (f32[16,8,128]{2,1,0:T(8,128)S(1)}, f32[16,8,128]{2,1,0:T(8,128)S(1)}, u32[]{:S(2)}, u32[]{:S(2)}) collective-permute-start(f32[16,8,128]{2,1,0:T(8,128)S(1)} %get-tuple-element.20.mine_ref), channel_id=1, source_target_pairs={{0,8},{8,0},{1,9},{9,1},{2,10},{10,2},{3,11},{11,3},{4,12},{12,4},... | collective-permute-start | bytes 196616 | tf_op jit(solution)/shard_map/ppermute | solution.py:229
  35.4 0.9 %collective-permute-done.1.other_ref = f32[16,8,128]{2,1,0:T(8,128)S(1)} collective-permute-done((f32[16,8,128]{2,1,0:T(8,128)S(1)}, f32[16,8,128]{2,1,0:T(8,128)S(1)}, u32[]{:S(2)}, u32[]{:S(2)}) %collective-permute-start.1) | collective-permute-done | bytes 65568 | tf_op jit(solution)/shard_map/ppermute | solution.py:229
  36.3 0.1 state_columns.1.refs_2_
  36.4 10.7 %all-to-all-done.1 = s32[64,9,1,128]{3,2,1,0:T(1,128)S(1)} async-done(((s32[64,9,1,128]{3,2,1,0:T(1,128)}), s32[64,9,1,128]{3,2,1,0:T(1,128)S(1)}, u32[]{:S(2)}, u32[]{:S(2)}) %all-to-all-start.1) | async-done | bytes 294944 | tf_op jit(solution)/shard_map/all_to_all | solution.py:228
  47.1 0.1 convert_reduce_fusion
  47.2 13.1 %all_to_all.15 = f32[8,1,128]{2,1,0:T(1,128)S(1)} all-to-all(f32[8,1,128]{2,1,0:T(1,128)S(1)} %broadcast_in_dim.3), channel_id=1, replica_groups=mesh['path_0'=4,'path_1'=8,'path_2'=2,'shard'=8] {'shard'}, dimensions={0} | all-to-all | bytes 8192 | tf_op jit(solution)/shard_map/all_to_all | solution.py:240
  60.3 1.1 %step.1 = (bf16[64,8,128]{2,1,0:T(8,128)(2,1)}, f32[16,16,64]{2,1,0:T(8,128)}) custom-call(f32[8,128]{1,0:T(8,128)S(1)} %bitcast.14, s32[576,128]{1,0:T(8,128)S(1)} %bitcast.13, f32[16,16,64]{2,1,0:T(8,128)S(1)} %state_columns.1.refs_2_, f32[1,128]{1,0:T(1,128)S(1)} %get-tuple-element.23.refs_3_, f32[16,16,64]{2,1,0:T(8,128)S(1)} %copy-done), custom_call_target="tpu_custom_call" | custom-call | tf_op jit(solution)/shard_map/step/pallas_call | solution.py:244
  (1 shorter events, 0.0 us)
Async XLA Ops:
  0.6 15.1 %copy-start = (f32[16,16,64]{2,1,0:T(8,128)S(1)}, f32[16,16,64]{2,1,0:T(8,128)}, u32[]{:S(2)}) copy-start(f32[16,16,64]{2,1,0:T(8,128)} %refs_4_.1) | copy-start | bytes 196612
  0.6 18.4 %copy-start.1 = (s32[64]{0:T(128)S(1)}, s32[64]{0:T(128)}, u32[]{:S(2)}) copy-start(s32[64]{0:T(128)} %module_ref.1) | copy-start | bytes 772
  0.6 25.8 %all-to-all-start = ((bf16[64,8,128]{2,1,0:T(8,128)(2,1)}), bf16[64,8,128]{2,1,0:T(8,128)(2,1)S(1)}, u32[]{:S(2)}, u32[]{:S(2)}) async-start(bf16[64,8,128]{2,1,0:T(8,128)(2,1)} %bitcast.15), calls=%async_computation | async-start | bytes 262144 | tf_op jit(solution)/shard_map/all_to_all | solution.py:197
  15.7 3.2 %collective-permute-start = (f32[16,16,64]{2,1,0:T(8,128)S(1)}, f32[16,16,64]{2,1,0:T(8,128)S(1)}, u32[]{:S(2)}, u32[]{:S(2)}) collective-permute-start(f32[16,16,64]{2,1,0:T(8,128)S(1)} %copy-done), channel_id=1, source_target_pairs={{0,8},{8,0},{1,9},{9,1},{2,10},{10,2},{3,11},{11,3},{4,12},{12,4},... | collective-permute-start | bytes 196616 | tf_op jit(solution)/shard_map/ppermute | solution.py:198
  27.6 19.5 %all-to-all-start.1 = ((s32[64,9,1,128]{3,2,1,0:T(1,128)}), s32[64,9,1,128]{3,2,1,0:T(1,128)S(1)}, u32[]{:S(2)}, u32[]{:S(2)}) async-start(s32[64,9,1,128]{3,2,1,0:T(1,128)} %bitcast.3), calls=%async_computation.1 | async-start | bytes 589824 | tf_op jit(solution)/shard_map/all_to_all | solution.py:228
  33.1 3.2 %collective-permute-start.1 = (f32[16,8,128]{2,1,0:T(8,128)S(1)}, f32[16,8,128]{2,1,0:T(8,128)S(1)}, u32[]{:S(2)}, u32[]{:S(2)}) collective-permute-start(f32[16,8,128]{2,1,0:T(8,128)S(1)} %get-tuple-element.20.mine_ref), channel_id=1, source_target_pairs={{0,8},{8,0},{1,9},{9,1},{2,10},{10,2},{3,11},{11,3},{4,12},{12,4},... | collective-permute-start | bytes 196616 | tf_op jit(solution)/shard_map/ppermute | solution.py:229

commit v8 on v7

--- a/solution.py
+++ b/solution.py
@@ -82,9 +82,9 @@
 
 
 def gather_kernel(
-    column_ref, lower_ref, upper_ref, fold_ref, count_ref, peer_ref, chunk_out, grad_ref, *scratch
+    column_ref, lower_ref, upper_ref, fold_ref, count_ref, peer_ref, chunk_ref, grad_ref, *scratch
 ):
-    *sums, words, chunk, sems = scratch
+    *sums, words = scratch
     peers, modules = column_ref.shape[0], grad_ref.shape[0]
     packed = [peer_ref[word, 0] for word in range(peers // PACKED)]
     module_of = [
@@ -119,32 +119,42 @@
         words[m, 0:UPPER, :] = (nearest(exact) << LOWER_BITS) | lower_ref[m]
         powers = jnp.sum(jnp.where(own_lane, power + BIAS, 0.0), axis=0, keepdims=True)
         words[m, UPPER:CHUNK, :] = upper_ref[m : m + 1, :] | ((norms + powers).astype(jnp.int32) << 24)
-    copies = []
     for q in range(peers):
         m = module_of[q]
         start = q * CHUNK
-        chunk[start : start + UPPER, :] = words[m, 0:UPPER, :]
-        chunk[start + UPPER : start + CHUNK, :] = words[m, UPPER:CHUNK, :]
-        if (q + 1) % (peers // PIECES) == 0:
-            piece = pl.ds(len(copies) * (peers // PIECES) * CHUNK, (peers // PIECES) * CHUNK)
-            sem = sems.at[len(copies)]
-            copies.append(pltpu.make_async_copy(chunk.at[piece], chunk_out.at[piece], sem))
-            copies[-1].start()
-    for copy in copies:
-        copy.wait()
-
-
-def columns_kernel(mine_ref, other_ref, grad_ref):
+        chunk_ref[start : start + UPPER, :] = words[m, 0:UPPER, :]
+        chunk_ref[start + UPPER : start + CHUNK, :] = words[m, UPPER:CHUNK, :]
+
+
+def assemble_kernel(chunk_ref, own_ref, grad_ref, decay_ref, mask_ref):
+    peers = grad_ref.shape[0]
+    power = lax.shift_right_logical(chunk_ref[pl.ds(UPPER, peers, stride=CHUNK), :], 24)
+    scale = 1.0 / jnp.exp2(GRAD_BITS + BIAS - power.astype(jnp.float32))
+    row = lax.broadcasted_iota(jnp.int32, (8, 128), 0)
+    own_lane = lanes() == EXPONENTS + row
+    for q in range(peers):
+        start = q * CHUNK
+        words = chunk_ref[start : start + UPPER, :]
+        of_row = jnp.sum(jnp.where(own_lane, scale[q : q + 1, :], 0.0), axis=1, keepdims=True)
+        grad_ref[q] = (words >> LOWER_BITS).astype(jnp.float32) * of_row
+        upper = (chunk_ref[start + UPPER : start + CHUNK, :] >> (row * 3)) & 7
+        whole = ((upper << LOWER_BITS) | (words & ((1 << LOWER_BITS) - 1))) - 32768
+        decay_ref[q] = whole.astype(jnp.float32) * (momentum_rate / MOMENTUM_SCALE)
+    mask_ref[...] = own_ref[...]
+
+
+def columns_kernel(mine_ref, other_ref, mask_ref, grad_ref, own_ref):
     core = lax.axis_index("path_2")
     for m in range(mine_ref.shape[0]):
         for half in range(2):
             grad = jnp.where(core == half, mine_ref[m], other_ref[m])
             grad = jnp.where(core == 0, grad, pltpu.roll(grad, 64, 1))
             grad_ref[m, half * 8 : half * 8 + 8, :] = grad[:, 0:64]
+    own_ref[...] = mask_ref[...]
 
 
 def step_kernel(
-    limit, squares_ref, chunk_ref, own_grad_ref, own_ref, momentum_ref,
+    limit, squares_ref, grad_ref, decay_ref, own_grad_ref, own_ref, momentum_ref,
     update_out, new_out, update, new, sems,
 ):
     peers, modules = update.shape[0], new.shape[0]
@@ -157,27 +167,15 @@
     norm_squares = (norm_squares + pltpu.roll(norm_squares, 126, 1))[0:1, :]
     shrink = jnp.minimum(1.0, limit / jnp.sqrt(norm_squares + 1e-06))
     own = jnp.sum(jnp.where(own_ref[...] > 0.0, shrink, 0.0), axis=1, keepdims=True)
-    power = lax.shift_right_logical(chunk_ref[pl.ds(UPPER, peers, stride=CHUNK), :], 24)
-    scale = own / jnp.exp2(GRAD_BITS + BIAS - power.astype(jnp.float32))
-    row = lax.broadcasted_iota(jnp.int32, (8, 128), 0)
-    own_lane = lane == EXPONENTS + row
     each = peers // PIECES
     copies = []
-    for q in range(peers):
-        start = q * CHUNK
-        words = chunk_ref[start : start + UPPER, :]
-        of_row = jnp.sum(jnp.where(own_lane, scale[q : q + 1, :], 0.0), axis=1, keepdims=True)
-        clipped = (words >> LOWER_BITS).astype(jnp.float32) * of_row
-        upper = (chunk_ref[start + UPPER : start + CHUNK, :] >> (row * 3)) & 7
-        whole = ((upper << LOWER_BITS) | (words & ((1 << LOWER_BITS) - 1))) - 32768
-        decay = whole.astype(jnp.float32) * (momentum_rate / MOMENTUM_SCALE)
-        step = outer_rate * (clipped + momentum_rate * (decay + clipped))
-        update[q] = step.astype(jnp.bfloat16)
-        if (q + 1) % each == 0:
-            piece = pl.ds(q + 1 - each, each)
-            sem = sems.at[len(copies)]
-            copies.append(pltpu.make_async_copy(update.at[piece], update_out.at[piece], sem))
-            copies[-1].start()
+    for piece in range(PIECES):
+        tiles = slice(piece * each, (piece + 1) * each)
+        clipped = grad_ref[tiles] * own.reshape(1, 1, 1)
+        step = outer_rate * (clipped + momentum_rate * (decay_ref[tiles] + clipped))
+        update[tiles] = step.astype(jnp.bfloat16)
+        copies.append(pltpu.make_async_copy(update.at[tiles], update_out.at[tiles], sems.at[piece]))
+        copies[-1].start()
     for m in range(modules):
         k = jnp.sum(jnp.where(lane[0:1, :] == 4 * m, shrink, 0.0), axis=1, keepdims=True)
         new[m] = momentum_rate * momentum_ref[m] + own_grad_ref[m] * k
@@ -217,29 +215,32 @@
         "gather_modules",
         out_shape=(shape((peers * CHUNK, 128), jnp.int32), module_tiles),
         in_specs=[VMEM] * 6,
-        out_specs=(HBM, VMEM),
+        out_specs=(VMEM, VMEM),
         scratch_shapes=[pltpu.VMEM((modules, 8, 128), jnp.float32)] * 4
-        + [
-            pltpu.VMEM((modules, 16, 128), jnp.int32),
-            pltpu.VMEM((peers * CHUNK, 128), jnp.int32),
-            pltpu.SemaphoreType.DMA((PIECES,)),
-        ],
+        + [pltpu.VMEM((modules, 16, 128), jnp.int32)],
     )(column_tiles, *packed)
     chunks = lax.all_to_all(chunks.reshape(peers, CHUNK, 1, 128), TILES, 0, 0, tiled=True)
+    squares = lax.shift_right_logical(chunks[:, UPPER], 24).astype(jnp.float32)
+    squares = jnp.broadcast_to(jnp.sum(squares, axis=0), (shards, 1, 128))
+    squares, grad = lax.optimization_barrier((squares, grad))
+    squares = lax.all_to_all(squares, "shard", 0, 0, tiled=True)
     other = lax.ppermute(grad, "path_2", [(0, 1), (1, 0)])
-    columns_grad = kernel(
+    path_tiles = shape((peers, 8, 128), jnp.float32)
+    *assembled, own = kernel(
+        assemble_kernel,
+        "assemble",
+        out_shape=(path_tiles, path_tiles, shape((1, 128), jnp.float32)),
+        in_specs=[VMEM] * 2,
+        out_specs=(VMEM,) * 3,
+        cost_estimate=pl.CostEstimate(flops=1 << 30, bytes_accessed=2 << 20, transcendentals=0),
+    )(chunks.reshape(peers * CHUNK, 128), own)
+    columns_grad, own = kernel(
         columns_kernel,
         "state_columns",
-        out_shape=shape(momentum.shape, jnp.float32),
-        in_specs=[VMEM] * 2,
-        out_specs=VMEM,
-    )(grad, other)
-    chunks, columns_grad = lax.optimization_barrier((chunks, columns_grad))
-    squares = lax.shift_right_logical(chunks[:, UPPER], 24).astype(jnp.float32)
-    squares = jnp.sum(squares, axis=0)
-    squares = lax.all_to_all(
-        jnp.broadcast_to(squares, (shards, 1, 128)), "shard", 0, 0, tiled=True
-    )
+        out_shape=(shape(momentum.shape, jnp.float32), shape((1, 128), jnp.float32)),
+        in_specs=[VMEM] * 3,
+        out_specs=(VMEM,) * 2,
+    )(grad, other, own)
     limit = clip_ratio * float(rows * shards * columns) ** 0.5
     update, new_momentum = kernel(
         lambda *refs: step_kernel(limit, *refs),
@@ -248,7 +249,7 @@
             shape((peers, 8, 128), jnp.bfloat16),
             shape(momentum.shape, jnp.float32),
         ),
-        in_specs=[VMEM] * 5,
+        in_specs=[VMEM] * 6,
         out_specs=(HBM, HBM),
         scratch_shapes=[
             pltpu.VMEM((peers, 8, 128), jnp.bfloat16),
@@ -257,7 +258,7 @@
         ],
     )(
         squares.reshape(shards, 128),
-        chunks.reshape(peers * CHUNK, 128),
+        *assembled,
         columns_grad,
         own,
         momentum,

time: 62.2 us -> 61.2 us (0.984)
  waiting for transfers between devices: 19.2 us -> 10.2 us
  blocking collectives: 13.1 us -> 18.7 us
  starting transfers between devices: 25.1 us -> 27.7 us
  Pallas kernels: 3.18 us -> 2.47 us
    all_to_all x1, waiting for transfers between devices: 10.7 us -> 1.89 us  [local(): squares = lax.all_to_all(squares, 'shard', 0, 0, tiled=True)]
    all_to_all x1, blocking collectives: 13.1 us -> 18.7 us  [local(): lax.all_to_all(chunks.reshape(peers, CHUNK, 1, 128), TILES, 0, 0, tiled=T...]
    ppermute x1, starting transfers between devices: 2.26 us -> 3.56 us  [local(): other = lax.ppermute(grad, 'path_2', [(0, 1), (1, 0)])]
    all_to_all x1, starting transfers between devices: 5.54 us -> 6.82 us  [local(): squares = lax.all_to_all(squares, 'shard', 0, 0, tiled=True)]
    pallas_call x1, Pallas kernels: 1.08 us -> 0.35 us  [local(): kernel(gather_kernel, 'gather_modules', out_shape=(shape((peers * CHUNK,...]
where the time goes in v8:
time: 61.2 us; the launch traced here: 60.5 us
  starting transfers between devices  27.7 us (45%)
  blocking collectives  18.7 us (31%)
  waiting for transfers between devices  10.2 us (17%)
  Pallas kernels  2.47 us (4%)
  between operations  0.71 us (1%)
    all_to_all x1, blocking collectives, local(): lax.all_to_all(chunks.reshape(peers, CHUNK, 1, 128), TILES, 0, 0, tiled=T...  18.7 us
    all_to_all x1, starting transfers between devices, local(): column_tiles = lax.all_to_all(tiles, TILES, 0, 0, tiled=True)  15.1 us
    all_to_all x1, starting transfers between devices, local(): squares = lax.all_to_all(squares, 'shard', 0, 0, tiled=True)  6.82 us
    all_to_all x1, waiting for transfers between devices, local(): column_tiles = lax.all_to_all(tiles, TILES, 0, 0, tiled=True)  6.62 us
    ppermute x1, starting transfers between devices, local(): other = lax.ppermute(grad, 'path_2', [(0, 1), (1, 0)])  3.56 us
    ppermute x1, starting transfers between devices, local(): other = lax.ppermute(momentum, 'path_2', [(0, 1), (1, 0)])  2.26 us
    all_to_all x1, waiting for transfers between devices, local(): squares = lax.all_to_all(squares, 'shard', 0, 0, tiled=True)  1.89 us
  transfers between devices with their start and end apart: 4, of which 4 were waited for; matrix products, arithmetic and copies ran while one was open for 0% of the time, Pallas kernels for 2%

profile of v8, /device:TPU:1, one launch (start us, length us, event | category | flops | bytes accessed | tf_op | source)
XLA Modules:
  0.0 60.5 jit_solution(10645368101150514103)
XLA Ops:
  0.6 0.0 copy-start
  0.6 0.0 copy-start.1
  0.6 15.1 %all-to-all-start = ((bf16[64,8,128]{2,1,0:T(8,128)(2,1)}), bf16[64,8,128]{2,1,0:T(8,128)(2,1)S(1)}, u32[]{:S(2)}, u32[]{:S(2)}) async-start(bf16[64,8,128]{2,1,0:T(8,128)(2,1)} %bitcast.16), calls=%async_computation | async-start | bytes 262144 | tf_op jit(solution)/shard_map/all_to_all | solution.py:195
  15.7 0.0 copy-done
  15.7 2.3 %collective-permute-start = (f32[16,16,64]{2,1,0:T(8,128)S(1)}, f32[16,16,64]{2,1,0:T(8,128)S(1)}, u32[]{:S(2)}, u32[]{:S(2)}) collective-permute-start(f32[16,16,64]{2,1,0:T(8,128)S(1)} %copy-done), channel_id=1, source_target_pairs={{0,8},{8,0},{1,9},{9,1},{2,10},{10,2},{3,11},{11,3},{4,12},{12,4},... | collective-permute-start | bytes 196616 | tf_op jit(solution)/shard_map/ppermute | solution.py:196
  18.0 1.0 %collective-permute-done.other_ref = f32[16,16,64]{2,1,0:T(8,128)S(1)} collective-permute-done((f32[16,16,64]{2,1,0:T(8,128)S(1)}, f32[16,16,64]{2,1,0:T(8,128)S(1)}, u32[]{:S(2)}, u32[]{:S(2)}) %collective-permute-start) | collective-permute-done | bytes 65568 | tf_op jit(solution)/shard_map/ppermute | solution.py:196
  19.0 0.0 copy-done.1
  19.0 0.9 %pack_momentum.1 = (s32[16,8,128]{2,1,0:T(8,128)S(1)}, s32[16,128]{1,0:T(8,128)S(1)}, f32[16,8,128]{2,1,0:T(8,128)S(1)}, f32[16,128]{1,0:T(8,128)S(1)}, s32[8,128]{1,0:T(8,128)S(1)}, /*index=5*/f32[1,128]{1,0:T(1,128)S(1)}) custom-call(s32[64]{0:T(128)S(1)} %copy-done.1, f32[16,16,64]{2,1,0:T(8,128)S(1)} %copy-done, ...), custom_call_target="tpu_custom_call" | custom-call | tf_op jit(solution)/shard_map/pack_momentum/pallas_call | solution.py:198
  19.9 6.6 %all-to-all-done.column_ref = bf16[64,8,128]{2,1,0:T(8,128)(2,1)S(1)} async-done(((bf16[64,8,128]{2,1,0:T(8,128)(2,1)}), bf16[64,8,128]{2,1,0:T(8,128)(2,1)S(1)}, u32[]{:S(2)}, u32[]{:S(2)}) %all-to-all-start) | async-done | bytes 131104 | tf_op jit(solution)/shard_map/all_to_all | solution.py:195
  26.5 0.3 gather_modules.1
  26.8 18.7 %all_to_all.15 = s32[64,9,1,128]{3,2,1,0:T(1,128)S(1)} all-to-all(s32[64,9,1,128]{3,2,1,0:T(1,128)S(1)} %bitcast.14), channel_id=1, replica_groups=mesh['path_0'=4,'path_1'=8,'path_2'=2,'shard'=8] {'path_2','path_0','pat..., dimensions={0} | all-to-all | bytes 589824 | tf_op jit(solution)/shard_map/all_to_all | solution.py:222
  45.5 0.1 fusion.1
  45.6 0.6 broadcast_in_dim.3
  46.2 6.8 %all-to-all-start.2 = ((f32[8,1,128]{2,1,0:T(1,128)}), f32[8,1,128]{2,1,0:T(1,128)S(1)}, u32[]{:S(2)}, u32[]{:S(2)}) async-start(f32[8,1,128]{2,1,0:T(1,128)} %broadcast_in_dim.3), calls=%async_computation.2 | async-start | bytes 8192 | tf_op jit(solution)/shard_map/all_to_all | solution.py:226
  53.0 3.6 %collective-permute-start.1 = (f32[16,8,128]{2,1,0:T(8,128)S(1)}, f32[16,8,128]{2,1,0:T(8,128)S(1)}, u32[]{:S(2)}, u32[]{:S(2)}) collective-permute-start(f32[16,8,128]{2,1,0:T(8,128)S(1)} %get-tuple-element.30.mine_ref), channel_id=1, source_target_pairs={{0,8},{8,0},{1,9},{9,1},{2,10},{10,2},{3,11},{11,3},{4,12},{12,4},... | collective-permute-start | bytes 196616 | tf_op jit(solution)/shard_map/ppermute | solution.py:227
  56.6 0.2 assemble.1
  56.8 0.7 %collective-permute-done.1.other_ref = f32[16,8,128]{2,1,0:T(8,128)S(1)} collective-permute-done((f32[16,8,128]{2,1,0:T(8,128)S(1)}, f32[16,8,128]{2,1,0:T(8,128)S(1)}, u32[]{:S(2)}, u32[]{:S(2)}) %collective-permute-start.1) | collective-permute-done | bytes 65568 | tf_op jit(solution)/shard_map/ppermute | solution.py:227
  57.5 0.1 state_columns.1
  57.6 1.9 %all-to-all-done.2 = f32[8,1,128]{2,1,0:T(1,128)S(1)} async-done(((f32[8,1,128]{2,1,0:T(1,128)}), f32[8,1,128]{2,1,0:T(1,128)S(1)}, u32[]{:S(2)}, u32[]{:S(2)}) %all-to-all-start.2) | async-done | bytes 4128 | tf_op jit(solution)/shard_map/all_to_all | solution.py:226
  59.5 1.0 %step.1 = (bf16[64,8,128]{2,1,0:T(8,128)(2,1)}, f32[16,16,64]{2,1,0:T(8,128)}) custom-call(f32[8,128]{1,0:T(8,128)S(1)} %bitcast.15, f32[64,8,128]{2,1,0:T(8,128)S(1)} %get-tuple-element.28.refs_1_, f32[64,8,128]{2,1,0:T(8,128)S(1)} %get-tuple-element.29.refs_2_, f32[16,16,64]{2,1,0:T(8,128)S(1)} %get-tuple-element.32.refs_3_, ...), custom_call_target="tpu_custom_call" | custom-call | tf_op jit(solution)/shard_map/step/pallas_call | solution.py:245
Async XLA Ops:
  0.6 15.1 %copy-start = (f32[16,16,64]{2,1,0:T(8,128)S(1)}, f32[16,16,64]{2,1,0:T(8,128)}, u32[]{:S(2)}) copy-start(f32[16,16,64]{2,1,0:T(8,128)} %refs_5_.1) | copy-start | bytes 196612
  0.6 18.4 %copy-start.1 = (s32[64]{0:T(128)S(1)}, s32[64]{0:T(128)}, u32[]{:S(2)}) copy-start(s32[64]{0:T(128)} %module_ref.1) | copy-start | bytes 772
  0.6 25.8 %all-to-all-start = ((bf16[64,8,128]{2,1,0:T(8,128)(2,1)}), bf16[64,8,128]{2,1,0:T(8,128)(2,1)S(1)}, u32[]{:S(2)}, u32[]{:S(2)}) async-start(bf16[64,8,128]{2,1,0:T(8,128)(2,1)} %bitcast.16), calls=%async_computation | async-start | bytes 262144 | tf_op jit(solution)/shard_map/all_to_all | solution.py:195
  15.7 3.2 %collective-permute-start = (f32[16,16,64]{2,1,0:T(8,128)S(1)}, f32[16,16,64]{2,1,0:T(8,128)S(1)}, u32[]{:S(2)}, u32[]{:S(2)}) collective-permute-start(f32[16,16,64]{2,1,0:T(8,128)S(1)} %copy-done), channel_id=1, source_target_pairs={{0,8},{8,0},{1,9},{9,1},{2,10},{10,2},{3,11},{11,3},{4,12},{12,4},... | collective-permute-start | bytes 196616 | tf_op jit(solution)/shard_map/ppermute | solution.py:196
  46.2 13.3 %all-to-all-start.2 = ((f32[8,1,128]{2,1,0:T(1,128)}), f32[8,1,128]{2,1,0:T(1,128)S(1)}, u32[]{:S(2)}, u32[]{:S(2)}) async-start(f32[8,1,128]{2,1,0:T(1,128)} %broadcast_in_dim.3), calls=%async_computation.2 | async-start | bytes 8192 | tf_op jit(solution)/shard_map/all_to_all | solution.py:226
  53.0 4.5 %collective-permute-start.1 = (f32[16,8,128]{2,1,0:T(8,128)S(1)}, f32[16,8,128]{2,1,0:T(8,128)S(1)}, u32[]{:S(2)}, u32[]{:S(2)}) collective-permute-start(f32[16,8,128]{2,1,0:T(8,128)S(1)} %get-tuple-element.30.mine_ref), channel_id=1, source_target_pairs={{0,8},{8,0},{1,9},{9,1},{2,10},{10,2},{3,11},{11,3},{4,12},{12,4},... | collective-permute-start | bytes 196616 | tf_op jit(solution)/shard_map/ppermute | solution.py:227

commit v9 on v8

--- a/solution.py
+++ b/solution.py
@@ -119,9 +119,9 @@
         words[m, 0:UPPER, :] = (nearest(exact) << LOWER_BITS) | lower_ref[m]
         powers = jnp.sum(jnp.where(own_lane, power + BIAS, 0.0), axis=0, keepdims=True)
         words[m, UPPER:CHUNK, :] = upper_ref[m : m + 1, :] | ((norms + powers).astype(jnp.int32) << 24)
-    for q in range(peers):
-        m = module_of[q]
-        start = q * CHUNK
+    for path in range(peers):
+        m = module_of[path % 2 * (peers // 2) + path // 2]
+        start = path * CHUNK
         chunk_ref[start : start + UPPER, :] = words[m, 0:UPPER, :]
         chunk_ref[start + UPPER : start + CHUNK, :] = words[m, UPPER:CHUNK, :]
 
@@ -133,9 +133,11 @@
     row = lax.broadcasted_iota(jnp.int32, (8, 128), 0)
     own_lane = lanes() == EXPONENTS + row
     for q in range(peers):
-        start = q * CHUNK
+        path = path_of(q, peers // 2)
+        start = path * CHUNK
         words = chunk_ref[start : start + UPPER, :]
-        of_row = jnp.sum(jnp.where(own_lane, scale[q : q + 1, :], 0.0), axis=1, keepdims=True)
+        of_row = jnp.where(own_lane, scale[path : path + 1, :], 0.0)
+        of_row = jnp.sum(of_row, axis=1, keepdims=True)
         grad_ref[q] = (words >> LOWER_BITS).astype(jnp.float32) * of_row
         upper = (chunk_ref[start + UPPER : start + CHUNK, :] >> (row * 3)) & 7
         whole = ((upper << LOWER_BITS) | (words & ((1 << LOWER_BITS) - 1))) - 32768
@@ -219,7 +221,7 @@
         scratch_shapes=[pltpu.VMEM((modules, 8, 128), jnp.float32)] * 4
         + [pltpu.VMEM((modules, 16, 128), jnp.int32)],
     )(column_tiles, *packed)
-    chunks = lax.all_to_all(chunks.reshape(peers, CHUNK, 1, 128), TILES, 0, 0, tiled=True)
+    chunks = lax.all_to_all(chunks.reshape(peers, CHUNK, 1, 128), PATH, 0, 0, tiled=True)
     squares = lax.shift_right_logical(chunks[:, UPPER], 24).astype(jnp.float32)
     squares = jnp.broadcast_to(jnp.sum(squares, axis=0), (shards, 1, 128))
     squares, grad = lax.optimization_barrier((squares, grad))

time: 61.2 us -> 59.5 us (0.972)
  blocking collectives: 18.7 us -> 17.2 us
  waiting for transfers between devices: 10.2 us -> 11.2 us
  starting transfers between devices: 27.7 us -> 26.8 us
    all_to_all x1, blocking collectives: 18.7 us -> 17.2 us  [local(): lax.all_to_all(chunks.reshape(peers, CHUNK, 1, 128), PATH, 0, 0, tiled=True)]
    all_to_all x1, waiting for transfers between devices: 1.89 us -> 2.85 us  [local(): squares = lax.all_to_all(squares, 'shard', 0, 0, tiled=True)]
    ppermute x1, starting transfers between devices: 3.56 us -> 2.61 us  [local(): other = lax.ppermute(grad, 'path_2', [(0, 1), (1, 0)])]
where the time goes in v9:
time: 59.5 us; the launch traced here: 59 us
  starting transfers between devices  26.8 us (45%)
  blocking collectives  17.2 us (29%)
  waiting for transfers between devices  11.2 us (19%)
  Pallas kernels  2.47 us (4%)
  between operations  0.71 us (1%)
  local copies, waits for them, and re-layouts  0.61 us (1%)
    all_to_all x1, blocking collectives, local(): lax.all_to_all(chunks.reshape(peers, CHUNK, 1, 128), PATH, 0, 0, tiled=True)  17.2 us
    all_to_all x1, starting transfers between devices, local(): column_tiles = lax.all_to_all(tiles, TILES, 0, 0, tiled=True)  15.1 us
    all_to_all x1, starting transfers between devices, local(): squares = lax.all_to_all(squares, 'shard', 0, 0, tiled=True)  6.82 us
    all_to_all x1, waiting for transfers between devices, local(): column_tiles = lax.all_to_all(tiles, TILES, 0, 0, tiled=True)  6.62 us
    all_to_all x1, waiting for transfers between devices, local(): squares = lax.all_to_all(squares, 'shard', 0, 0, tiled=True)  2.85 us
    ppermute x1, starting transfers between devices, local(): other = lax.ppermute(grad, 'path_2', [(0, 1), (1, 0)])  2.61 us
    ppermute x1, starting transfers between devices, local(): other = lax.ppermute(momentum, 'path_2', [(0, 1), (1, 0)])  2.26 us
  transfers between devices with their start and end apart: 4, of which 4 were waited for; matrix products, arithmetic and copies ran while one was open for 0% of the time, Pallas kernels for 2%

profile of v9, /device:TPU:1, one launch (start us, length us, event | category | flops | bytes accessed | tf_op | source)
XLA Modules:
  0.0 59.0 jit_solution(13522045723272062705)
XLA Ops:
  0.6 0.0 copy-start
  0.6 0.0 copy-start.1
  0.6 15.1 %all-to-all-start = ((bf16[64,8,128]{2,1,0:T(8,128)(2,1)}), bf16[64,8,128]{2,1,0:T(8,128)(2,1)S(1)}, u32[]{:S(2)}, u32[]{:S(2)}) async-start(bf16[64,8,128]{2,1,0:T(8,128)(2,1)} %bitcast.16), calls=%async_computation | async-start | bytes 262144 | tf_op jit(solution)/shard_map/all_to_all | solution.py:197
  15.7 0.0 copy-done
  15.7 2.3 %collective-permute-start = (f32[16,16,64]{2,1,0:T(8,128)S(1)}, f32[16,16,64]{2,1,0:T(8,128)S(1)}, u32[]{:S(2)}, u32[]{:S(2)}) collective-permute-start(f32[16,16,64]{2,1,0:T(8,128)S(1)} %copy-done), channel_id=1, source_target_pairs={{0,8},{8,0},{1,9},{9,1},{2,10},{10,2},{3,11},{11,3},{4,12},{12,4},... | collective-permute-start | bytes 196616 | tf_op jit(solution)/shard_map/ppermute | solution.py:198
  18.0 1.0 %collective-permute-done.other_ref = f32[16,16,64]{2,1,0:T(8,128)S(1)} collective-permute-done((f32[16,16,64]{2,1,0:T(8,128)S(1)}, f32[16,16,64]{2,1,0:T(8,128)S(1)}, u32[]{:S(2)}, u32[]{:S(2)}) %collective-permute-start) | collective-permute-done | bytes 65568 | tf_op jit(solution)/shard_map/ppermute | solution.py:198
  19.0 0.0 copy-done.1
  19.0 0.9 %pack_momentum.1 = (s32[16,8,128]{2,1,0:T(8,128)S(1)}, s32[16,128]{1,0:T(8,128)S(1)}, f32[16,8,128]{2,1,0:T(8,128)S(1)}, f32[16,128]{1,0:T(8,128)S(1)}, s32[8,128]{1,0:T(8,128)S(1)}, /*index=5*/f32[1,128]{1,0:T(1,128)S(1)}) custom-call(s32[64]{0:T(128)S(1)} %copy-done.1, f32[16,16,64]{2,1,0:T(8,128)S(1)} %copy-done, ...), custom_call_target="tpu_custom_call" | custom-call | tf_op jit(solution)/shard_map/pack_momentum/pallas_call | solution.py:200
  19.9 6.6 %all-to-all-done.column_ref = bf16[64,8,128]{2,1,0:T(8,128)(2,1)S(1)} async-done(((bf16[64,8,128]{2,1,0:T(8,128)(2,1)}), bf16[64,8,128]{2,1,0:T(8,128)(2,1)S(1)}, u32[]{:S(2)}, u32[]{:S(2)}) %all-to-all-start) | async-done | bytes 131104 | tf_op jit(solution)/shard_map/all_to_all | solution.py:197
  26.5 0.3 gather_modules.1
  26.8 17.2 %all_to_all.15 = s32[64,9,1,128]{3,2,1,0:T(1,128)S(1)} all-to-all(s32[64,9,1,128]{3,2,1,0:T(1,128)S(1)} %bitcast.14), channel_id=1, replica_groups=mesh['path_0'=4,'path_1'=8,'path_2'=2,'shard'=8] {'path_0','path_1','pat..., dimensions={0} | all-to-all | bytes 589824 | tf_op jit(solution)/shard_map/all_to_all | solution.py:224
  44.1 0.1 fusion.1
  44.1 0.6 %broadcast_in_dim.3 = f32[8,1,128]{2,1,0:T(1,128)} broadcast(f32[128]{0:T(128)S(1)} %fusion.1), dimensions={2} | broadcast | bytes 4608 | tf_op jit(solution)/shard_map/broadcast_in_dim | solution.py:226
  44.7 6.8 %all-to-all-start.2 = ((f32[8,1,128]{2,1,0:T(1,128)}), f32[8,1,128]{2,1,0:T(1,128)S(1)}, u32[]{:S(2)}, u32[]{:S(2)}) async-start(f32[8,1,128]{2,1,0:T(1,128)} %broadcast_in_dim.3), calls=%async_computation.2 | async-start | bytes 8192 | tf_op jit(solution)/shard_map/all_to_all | solution.py:228
  51.6 2.6 %collective-permute-start.1 = (f32[16,8,128]{2,1,0:T(8,128)S(1)}, f32[16,8,128]{2,1,0:T(8,128)S(1)}, u32[]{:S(2)}, u32[]{:S(2)}) collective-permute-start(f32[16,8,128]{2,1,0:T(8,128)S(1)} %get-tuple-element.30.mine_ref), channel_id=1, source_target_pairs={{0,8},{8,0},{1,9},{9,1},{2,10},{10,2},{3,11},{11,3},{4,12},{12,4},... | collective-permute-start | bytes 196616 | tf_op jit(solution)/shard_map/ppermute | solution.py:229
  54.2 0.2 assemble.1
  54.4 0.7 %collective-permute-done.1.other_ref = f32[16,8,128]{2,1,0:T(8,128)S(1)} collective-permute-done((f32[16,8,128]{2,1,0:T(8,128)S(1)}, f32[16,8,128]{2,1,0:T(8,128)S(1)}, u32[]{:S(2)}, u32[]{:S(2)}) %collective-permute-start.1) | collective-permute-done | bytes 65568 | tf_op jit(solution)/shard_map/ppermute | solution.py:229
  55.1 0.1 state_columns.1
  55.2 2.8 %all-to-all-done.2 = f32[8,1,128]{2,1,0:T(1,128)S(1)} async-done(((f32[8,1,128]{2,1,0:T(1,128)}), f32[8,1,128]{2,1,0:T(1,128)S(1)}, u32[]{:S(2)}, u32[]{:S(2)}) %all-to-all-start.2) | async-done | bytes 4128 | tf_op jit(solution)/shard_map/all_to_all | solution.py:228
  58.0 1.0 %step.1 = (bf16[64,8,128]{2,1,0:T(8,128)(2,1)}, f32[16,16,64]{2,1,0:T(8,128)}) custom-call(f32[8,128]{1,0:T(8,128)S(1)} %bitcast.15, f32[64,8,128]{2,1,0:T(8,128)S(1)} %get-tuple-element.28.refs_1_, f32[64,8,128]{2,1,0:T(8,128)S(1)} %get-tuple-element.29.refs_2_, f32[16,16,64]{2,1,0:T(8,128)S(1)} %get-tuple-element.32.refs_3_, ...), custom_call_target="tpu_custom_call" | custom-call | tf_op jit(solution)/shard_map/step/pallas_call | solution.py:247
Async XLA Ops:
  0.6 15.1 %copy-start = (f32[16,16,64]{2,1,0:T(8,128)S(1)}, f32[16,16,64]{2,1,0:T(8,128)}, u32[]{:S(2)}) copy-start(f32[16,16,64]{2,1,0:T(8,128)} %refs_5_.1) | copy-start | bytes 196612
  0.6 18.4 %copy-start.1 = (s32[64]{0:T(128)S(1)}, s32[64]{0:T(128)}, u32[]{:S(2)}) copy-start(s32[64]{0:T(128)} %module_ref.1) | copy-start | bytes 772
  0.6 25.8 %all-to-all-start = ((bf16[64,8,128]{2,1,0:T(8,128)(2,1)}), bf16[64,8,128]{2,1,0:T(8,128)(2,1)S(1)}, u32[]{:S(2)}, u32[]{:S(2)}) async-start(bf16[64,8,128]{2,1,0:T(8,128)(2,1)} %bitcast.16), calls=%async_computation | async-start | bytes 262144 | tf_op jit(solution)/shard_map/all_to_all | solution.py:197
  15.7 3.2 %collective-permute-start = (f32[16,16,64]{2,1,0:T(8,128)S(1)}, f32[16,16,64]{2,1,0:T(8,128)S(1)}, u32[]{:S(2)}, u32[]{:S(2)}) collective-permute-start(f32[16,16,64]{2,1,0:T(8,128)S(1)} %copy-done), channel_id=1, source_target_pairs={{0,8},{8,0},{1,9},{9,1},{2,10},{10,2},{3,11},{11,3},{4,12},{12,4},... | collective-permute-start | bytes 196616 | tf_op jit(solution)/shard_map/ppermute | solution.py:198
  44.7 13.3 %all-to-all-start.2 = ((f32[8,1,128]{2,1,0:T(1,128)}), f32[8,1,128]{2,1,0:T(1,128)S(1)}, u32[]{:S(2)}, u32[]{:S(2)}) async-start(f32[8,1,128]{2,1,0:T(1,128)} %broadcast_in_dim.3), calls=%async_computation.2 | async-start | bytes 8192 | tf_op jit(solution)/shard_map/all_to_all | solution.py:228
  51.6 3.5 %collective-permute-start.1 = (f32[16,8,128]{2,1,0:T(8,128)S(1)}, f32[16,8,128]{2,1,0:T(8,128)S(1)}, u32[]{:S(2)}, u32[]{:S(2)}) collective-permute-start(f32[16,8,128]{2,1,0:T(8,128)S(1)} %get-tuple-element.30.mine_ref), channel_id=1, source_target_pairs={{0,8},{8,0},{1,9},{9,1},{2,10},{10,2},{3,11},{11,3},{4,12},{12,4},... | collective-permute-start | bytes 196616 | tf_op jit(solution)/shard_map/ppermute | solution.py:229

commit v10 on v9

--- a/solution.py
+++ b/solution.py
@@ -8,6 +8,9 @@
 
 PATH = ("path_0", "path_1", "path_2")
 TILES = ("path_2", "path_0", "path_1")
+
+SHARD = ("shard_2", "shard_1", "shard_0")
+SHARD_ORDER = ("shard_1", "shard_2", "shard_0")
 
 outer_rate = 0.7
 momentum_rate = 0.9
@@ -124,6 +127,16 @@
         start = path * CHUNK
         chunk_ref[start : start + UPPER, :] = words[m, 0:UPPER, :]
         chunk_ref[start + UPPER : start + CHUNK, :] = words[m, UPPER:CHUNK, :]
+
+
+def squares_kernel(chunk_ref, squares_out, squares, sem):
+    peers = chunk_ref.shape[0] // CHUNK
+    norms = lax.shift_right_logical(chunk_ref[pl.ds(UPPER, peers, stride=CHUNK), :], 24)
+    norms = jnp.sum(norms.astype(jnp.float32), axis=0, keepdims=True)
+    squares[...] = jnp.broadcast_to(norms, squares.shape)
+    copy = pltpu.make_async_copy(squares, squares_out, sem)
+    copy.start()
+    copy.wait()
 
 
 def assemble_kernel(chunk_ref, own_ref, grad_ref, decay_ref, mask_ref):
@@ -191,7 +204,7 @@
     modules, rows, width = momentum.shape
     columns = deltas.shape[2]
     peers = lax.axis_size(PATH)
-    shards = lax.axis_size("shard")
+    shards = lax.axis_size(SHARD)
     shape = jax.ShapeDtypeStruct
     tiles = deltas.reshape(2, 8, peers // 2, 128).transpose(0, 2, 1, 3).reshape(peers, 8, 128)
     column_tiles = lax.all_to_all(tiles, TILES, 0, 0, tiled=True)
@@ -222,10 +235,18 @@
         + [pltpu.VMEM((modules, 16, 128), jnp.int32)],
     )(column_tiles, *packed)
     chunks = lax.all_to_all(chunks.reshape(peers, CHUNK, 1, 128), PATH, 0, 0, tiled=True)
-    squares = lax.shift_right_logical(chunks[:, UPPER], 24).astype(jnp.float32)
-    squares = jnp.broadcast_to(jnp.sum(squares, axis=0), (shards, 1, 128))
+    chunks = chunks.reshape(peers * CHUNK, 128)
+    squares = kernel(
+        squares_kernel,
+        "sum_squares",
+        out_shape=shape((shards, 128), jnp.float32),
+        in_specs=[VMEM],
+        out_specs=HBM,
+        scratch_shapes=[pltpu.VMEM((shards, 128), jnp.float32), pltpu.SemaphoreType.DMA],
+    )(chunks)
+    squares = squares.reshape(shards, 1, 128)
     squares, grad = lax.optimization_barrier((squares, grad))
-    squares = lax.all_to_all(squares, "shard", 0, 0, tiled=True)
+    squares = lax.all_to_all(squares, SHARD_ORDER, 0, 0, tiled=True)
     other = lax.ppermute(grad, "path_2", [(0, 1), (1, 0)])
     path_tiles = shape((peers, 8, 128), jnp.float32)
     *assembled, own = kernel(
@@ -235,7 +256,7 @@
         in_specs=[VMEM] * 2,
         out_specs=(VMEM,) * 3,
         cost_estimate=pl.CostEstimate(flops=1 << 30, bytes_accessed=2 << 20, transcendentals=0),
-    )(chunks.reshape(peers * CHUNK, 128), own)
+    )(chunks, own)
     columns_grad, own = kernel(
         columns_kernel,
         "state_columns",
@@ -271,8 +292,8 @@
 
 def solution(mesh):
     finer = Mesh(
-        mesh.devices.reshape(4, 8, 2, mesh.shape["shard"]), ("path_0", "path_1", "path_2", "shard")
+        mesh.devices.reshape(4, 8, 2, 2, 2, 2), (*PATH, *SHARD)
     )
-    in_specs = (P(PATH, "shard", None), P(None, "shard", PATH), P())
-    out_specs = (P(PATH, "shard", None), P(None, "shard", PATH))
+    in_specs = (P(PATH, SHARD, None), P(None, SHARD, PATH), P())
+    out_specs = (P(PATH, SHARD, None), P(None, SHARD, PATH))
     return jax.shard_map(local, mesh=finer, in_specs=in_specs, out_specs=out_specs, check_vma=False)

time: 59.5 us -> 59.5 us (level)
  Pallas kernels: 2.47 us -> 3.09 us
  local copies, waits for them, and re-layouts: 0.61 us -> 0.01 us
    pallas_call x0 -> x1, Pallas kernels: none -> 0.62 us  [local(): kernel(squares_kernel, 'sum_squares', out_shape=shape((shards, 128), jnp....]
    broadcast_in_dim x1 -> x0, local copies, waits for them, and re-layouts: 0.6 us -> none  [local(): squares = jnp.broadcast_to(jnp.sum(squares, axis=0), (shards, 1, 128))]
where the time goes in v10:
time: 59.5 us; the launch traced here: 59 us
  starting transfers between devices  26.8 us (45%)
  blocking collectives  17.2 us (29%)
  waiting for transfers between devices  11.1 us (19%)
  Pallas kernels  3.09 us (5%)
  between operations  0.72 us (1%)
    all_to_all x1, blocking collectives, local(): lax.all_to_all(chunks.reshape(peers, CHUNK, 1, 128), PATH, 0, 0, tiled=True)  17.2 us
    all_to_all x1, starting transfers between devices, local(): column_tiles = lax.all_to_all(tiles, TILES, 0, 0, tiled=True)  15.1 us
    all_to_all x1, starting transfers between devices, local(): squares = lax.all_to_all(squares, SHARD_ORDER, 0, 0, tiled=True)  6.83 us
    all_to_all x1, waiting for transfers between devices, local(): column_tiles = lax.all_to_all(tiles, TILES, 0, 0, tiled=True)  6.62 us
    all_to_all x1, waiting for transfers between devices, local(): squares = lax.all_to_all(squares, SHARD_ORDER, 0, 0, tiled=True)  2.83 us
    ppermute x1, starting transfers between devices, local(): other = lax.ppermute(grad, 'path_2', [(0, 1), (1, 0)])  2.61 us
    ppermute x1, starting transfers between devices, local(): other = lax.ppermute(momentum, 'path_2', [(0, 1), (1, 0)])  2.26 us
  transfers between devices with their start and end apart: 4, of which 4 were waited for; matrix products, arithmetic and copies ran while one was open for 0% of the time, Pallas kernels for 2%

profile of v10, /device:TPU:1, one launch (start us, length us, event | category | flops | bytes accessed | tf_op | source)
XLA Modules:
  0.0 59.0 jit_solution(5069039367627358143)
XLA Ops:
  0.6 0.0 copy-start
  0.6 0.0 copy-start.1
  0.6 15.1 %all-to-all-start = ((bf16[64,8,128]{2,1,0:T(8,128)(2,1)}), bf16[64,8,128]{2,1,0:T(8,128)(2,1)S(1)}, u32[]{:S(2)}, u32[]{:S(2)}) async-start(bf16[64,8,128]{2,1,0:T(8,128)(2,1)} %bitcast.19), calls=%async_computation | async-start | bytes 262144 | tf_op jit(solution)/shard_map/all_to_all | solution.py:210
  15.7 0.0 copy-done
  15.7 2.3 %collective-permute-start = (f32[16,16,64]{2,1,0:T(8,128)S(1)}, f32[16,16,64]{2,1,0:T(8,128)S(1)}, u32[]{:S(2)}, u32[]{:S(2)}) collective-permute-start(f32[16,16,64]{2,1,0:T(8,128)S(1)} %copy-done), channel_id=1, source_target_pairs={{0,8},{8,0},{1,9},{9,1},{2,10},{10,2},{3,11},{11,3},{4,12},{12,4},... | collective-permute-start | bytes 196616 | tf_op jit(solution)/shard_map/ppermute | solution.py:211
  18.0 1.0 %collective-permute-done.other_ref = f32[16,16,64]{2,1,0:T(8,128)S(1)} collective-permute-done((f32[16,16,64]{2,1,0:T(8,128)S(1)}, f32[16,16,64]{2,1,0:T(8,128)S(1)}, u32[]{:S(2)}, u32[]{:S(2)}) %collective-permute-start) | collective-permute-done | bytes 65568 | tf_op jit(solution)/shard_map/ppermute | solution.py:211
  19.0 0.0 copy-done.1
  19.0 0.9 %pack_momentum.1 = (s32[16,8,128]{2,1,0:T(8,128)S(1)}, s32[16,128]{1,0:T(8,128)S(1)}, f32[16,8,128]{2,1,0:T(8,128)S(1)}, f32[16,128]{1,0:T(8,128)S(1)}, s32[8,128]{1,0:T(8,128)S(1)}, /*index=5*/f32[1,128]{1,0:T(1,128)S(1)}) custom-call(s32[64]{0:T(128)S(1)} %copy-done.1, f32[16,16,64]{2,1,0:T(8,128)S(1)} %copy-done, ...), custom_call_target="tpu_custom_call" | custom-call | tf_op jit(solution)/shard_map/pack_momentum/pallas_call | solution.py:213
  19.9 6.6 %all-to-all-done.column_ref = bf16[64,8,128]{2,1,0:T(8,128)(2,1)S(1)} async-done(((bf16[64,8,128]{2,1,0:T(8,128)(2,1)}), bf16[64,8,128]{2,1,0:T(8,128)(2,1)S(1)}, u32[]{:S(2)}, u32[]{:S(2)}) %all-to-all-start) | async-done | bytes 131104 | tf_op jit(solution)/shard_map/all_to_all | solution.py:210
  26.5 0.4 gather_modules.1
  26.8 17.2 %all_to_all.15 = s32[64,9,1,128]{3,2,1,0:T(1,128)S(1)} all-to-all(s32[64,9,1,128]{3,2,1,0:T(1,128)S(1)} %bitcast.17), channel_id=1, replica_groups=mesh['path_0'=4,'path_1'=8,'path_2'=2,'shard_2'=2,'shard_1'=2,'shard_0'=..., dimensions={0} | all-to-all | bytes 589824 | tf_op jit(solution)/shard_map/all_to_all | solution.py:237
  44.1 0.6 %sum_squares.1 = f32[8,128]{1,0:T(8,128)} custom-call(s32[576,128]{1,0:T(8,128)S(1)} %bitcast.15), custom_call_target="tpu_custom_call" | custom-call | tf_op jit(solution)/shard_map/sum_squares/pallas_call | solution.py:239
  44.7 6.8 %all-to-all-start.2 = ((f32[8,1,128]{2,1,0:T(1,128)}), f32[8,1,128]{2,1,0:T(1,128)S(1)}, u32[]{:S(2)}, u32[]{:S(2)}) async-start(f32[8,1,128]{2,1,0:T(1,128)} %bitcast.6), calls=%async_computation.2 | async-start | bytes 8192 | tf_op jit(solution)/shard_map/all_to_all | solution.py:249
  51.5 2.6 %collective-permute-start.1 = (f32[16,8,128]{2,1,0:T(8,128)S(1)}, f32[16,8,128]{2,1,0:T(8,128)S(1)}, u32[]{:S(2)}, u32[]{:S(2)}) collective-permute-start(f32[16,8,128]{2,1,0:T(8,128)S(1)} %get-tuple-element.30.mine_ref), channel_id=1, source_target_pairs={{0,8},{8,0},{1,9},{9,1},{2,10},{10,2},{3,11},{11,3},{4,12},{12,4},... | collective-permute-start | bytes 196616 | tf_op jit(solution)/shard_map/ppermute | solution.py:250
  54.1 0.2 assemble.1
  54.3 0.7 %collective-permute-done.1.other_ref = f32[16,8,128]{2,1,0:T(8,128)S(1)} collective-permute-done((f32[16,8,128]{2,1,0:T(8,128)S(1)}, f32[16,8,128]{2,1,0:T(8,128)S(1)}, u32[]{:S(2)}, u32[]{:S(2)}) %collective-permute-start.1) | collective-permute-done | bytes 65568 | tf_op jit(solution)/shard_map/ppermute | solution.py:250
  55.0 0.1 state_columns.1
  55.1 2.8 %all-to-all-done.2 = f32[8,1,128]{2,1,0:T(1,128)S(1)} async-done(((f32[8,1,128]{2,1,0:T(1,128)}), f32[8,1,128]{2,1,0:T(1,128)S(1)}, u32[]{:S(2)}, u32[]{:S(2)}) %all-to-all-start.2) | async-done | bytes 4128 | tf_op jit(solution)/shard_map/all_to_all | solution.py:249
  58.0 1.0 %step.1 = (bf16[64,8,128]{2,1,0:T(8,128)(2,1)}, f32[16,16,64]{2,1,0:T(8,128)}) custom-call(f32[8,128]{1,0:T(8,128)S(1)} %bitcast.18, f32[64,8,128]{2,1,0:T(8,128)S(1)} %get-tuple-element.28.refs_1_, f32[64,8,128]{2,1,0:T(8,128)S(1)} %get-tuple-element.29.refs_2_, f32[16,16,64]{2,1,0:T(8,128)S(1)} %get-tuple-element.32.refs_3_, ...), custom_call_target="tpu_custom_call" | custom-call | tf_op jit(solution)/shard_map/step/pallas_call | solution.py:268
Async XLA Ops:
  0.6 15.1 %copy-start = (f32[16,16,64]{2,1,0:T(8,128)S(1)}, f32[16,16,64]{2,1,0:T(8,128)}, u32[]{:S(2)}) copy-start(f32[16,16,64]{2,1,0:T(8,128)} %refs_5_.1) | copy-start | bytes 196612
  0.6 18.4 %copy-start.1 = (s32[64]{0:T(128)S(1)}, s32[64]{0:T(128)}, u32[]{:S(2)}) copy-start(s32[64]{0:T(128)} %module_ref.1) | copy-start | bytes 772
  0.6 25.8 %all-to-all-start = ((bf16[64,8,128]{2,1,0:T(8,128)(2,1)}), bf16[64,8,128]{2,1,0:T(8,128)(2,1)S(1)}, u32[]{:S(2)}, u32[]{:S(2)}) async-start(bf16[64,8,128]{2,1,0:T(8,128)(2,1)} %bitcast.19), calls=%async_computation | async-start | bytes 262144 | tf_op jit(solution)/shard_map/all_to_all | solution.py:210
  15.7 3.2 %collective-permute-start = (f32[16,16,64]{2,1,0:T(8,128)S(1)}, f32[16,16,64]{2,1,0:T(8,128)S(1)}, u32[]{:S(2)}, u32[]{:S(2)}) collective-permute-start(f32[16,16,64]{2,1,0:T(8,128)S(1)} %copy-done), channel_id=1, source_target_pairs={{0,8},{8,0},{1,9},{9,1},{2,10},{10,2},{3,11},{11,3},{4,12},{12,4},... | collective-permute-start | bytes 196616 | tf_op jit(solution)/shard_map/ppermute | solution.py:211
  44.7 13.3 %all-to-all-start.2 = ((f32[8,1,128]{2,1,0:T(1,128)}), f32[8,1,128]{2,1,0:T(1,128)S(1)}, u32[]{:S(2)}, u32[]{:S(2)}) async-start(f32[8,1,128]{2,1,0:T(1,128)} %bitcast.6), calls=%async_computation.2 | async-start | bytes 8192 | tf_op jit(solution)/shard_map/all_to_all | solution.py:249
  51.5 3.5 %collective-permute-start.1 = (f32[16,8,128]{2,1,0:T(8,128)S(1)}, f32[16,8,128]{2,1,0:T(8,128)S(1)}, u32[]{:S(2)}, u32[]{:S(2)}) collective-permute-start(f32[16,8,128]{2,1,0:T(8,128)S(1)} %get-tuple-element.30.mine_ref), channel_id=1, source_target_pairs={{0,8},{8,0},{1,9},{9,1},{2,10},{10,2},{3,11},{11,3},{4,12},{12,4},... | collective-permute-start | bytes 196616 | tf_op jit(solution)/shard_map/ppermute | solution.py:250

commit v11 on v10

--- a/solution.py
+++ b/solution.py
@@ -70,7 +70,7 @@
     for m in range(modules):
         count_ref[m : m + 1, :] = jnp.full((1, 128), count[m].astype(jnp.float32))
         mine = jnp.where(first_core, mine_ref[m, 0:8, :], mine_ref[m, 8:16, :])
-        other = jnp.where(first_core, other_ref[m, 0:8, :], other_ref[m, 8:16, :])
+        other = other_ref[m]
         momentum = jnp.concatenate(
             [jnp.where(first_core, mine, other), jnp.where(first_core, other, mine)], axis=1
         )
@@ -208,7 +208,8 @@
     shape = jax.ShapeDtypeStruct
     tiles = deltas.reshape(2, 8, peers // 2, 128).transpose(0, 2, 1, 3).reshape(peers, 8, 128)
     column_tiles = lax.all_to_all(tiles, TILES, 0, 0, tiled=True)
-    other = lax.ppermute(momentum, "path_2", [(0, 1), (1, 0)])
+    half = jnp.where(lax.axis_index("path_2") == 0, momentum[:, 8:16], momentum[:, 0:8])
+    other = lax.ppermute(half, "path_2", [(0, 1), (1, 0)])
     module_tiles = shape((modules, 8, 128), jnp.float32)
     *packed, own = kernel(
         momentum_kernel,

time: 59.5 us -> 59.5 us (level)
  no operation moved by 1% of the time
where the time goes in v11:
time: 59.5 us; the launch traced here: 59 us
  starting transfers between devices  26.8 us (45%)
  blocking collectives  17.2 us (29%)
  waiting for transfers between devices  11.1 us (19%)
  Pallas kernels  3.09 us (5%)
  between operations  0.73 us (1%)
    all_to_all x1, blocking collectives, local(): lax.all_to_all(chunks.reshape(peers, CHUNK, 1, 128), PATH, 0, 0, tiled=True)  17.2 us
    all_to_all x1, starting transfers between devices, local(): column_tiles = lax.all_to_all(tiles, TILES, 0, 0, tiled=True)  15.1 us
    all_to_all x1, starting transfers between devices, local(): squares = lax.all_to_all(squares, SHARD_ORDER, 0, 0, tiled=True)  6.83 us
    all_to_all x1, waiting for transfers between devices, local(): column_tiles = lax.all_to_all(tiles, TILES, 0, 0, tiled=True)  6.68 us
    all_to_all x1, waiting for transfers between devices, local(): squares = lax.all_to_all(squares, SHARD_ORDER, 0, 0, tiled=True)  2.83 us
    ppermute x1, starting transfers between devices, local(): other = lax.ppermute(grad, 'path_2', [(0, 1), (1, 0)])  2.61 us
    ppermute x1, starting transfers between devices, local(): other = lax.ppermute(half, 'path_2', [(0, 1), (1, 0)])  2.26 us
  transfers between devices with their start and end apart: 4, of which 4 were waited for; matrix products, arithmetic and copies ran while one was open for 0% of the time, Pallas kernels for 2%

profile of v11, /device:TPU:1, one launch (start us, length us, event | category | flops | bytes accessed | tf_op | source)
XLA Modules:
  0.0 59.0 jit_solution(5838507684441178049)
XLA Ops:
  0.6 0.0 copy-start
  0.6 15.1 %all-to-all-start = ((bf16[64,8,128]{2,1,0:T(8,128)(2,1)}), bf16[64,8,128]{2,1,0:T(8,128)(2,1)S(1)}, u32[]{:S(2)}, u32[]{:S(2)}) async-start(bf16[64,8,128]{2,1,0:T(8,128)(2,1)} %bitcast.19), calls=%async_computation | async-start | bytes 262144 | tf_op jit(solution)/shard_map/all_to_all | solution.py:210
  15.7 0.0 copy-done
  15.7 0.0 copy-start.1
  15.8 2.3 %collective-permute-start = (f32[16,8,64]{2,1,0:T(8,128)S(1)}, f32[16,8,64]{2,1,0:T(8,128)S(1)}, u32[]{:S(2)}, u32[]{:S(2)}) collective-permute-start(f32[16,8,64]{2,1,0:T(8,128)S(1)} %slice_select_fusion), channel_id=1, source_target_pairs={{0,8},{8,0},{1,9},{9,1},{2,10},{10,2},{3,11},{11,3},{4,12},{12,4},... | collective-permute-start | bytes 98312 | tf_op jit(solution)/shard_map/ppermute | solution.py:212
  18.0 0.9 %collective-permute-done.other_ref = f32[16,8,64]{2,1,0:T(8,128)S(1)} collective-permute-done((f32[16,8,64]{2,1,0:T(8,128)S(1)}, f32[16,8,64]{2,1,0:T(8,128)S(1)}, u32[]{:S(2)}, u32[]{:S(2)}) %collective-permute-start) | collective-permute-done | bytes 32800 | tf_op jit(solution)/shard_map/ppermute | solution.py:212
  18.9 0.0 copy-done.1
  18.9 0.9 %pack_momentum.1 = (s32[16,8,128]{2,1,0:T(8,128)S(1)}, s32[16,128]{1,0:T(8,128)S(1)}, f32[16,8,128]{2,1,0:T(8,128)S(1)}, f32[16,128]{1,0:T(8,128)S(1)}, s32[8,128]{1,0:T(8,128)S(1)}, /*index=5*/f32[1,128]{1,0:T(1,128)S(1)}) custom-call(s32[64]{0:T(128)S(1)} %copy-done.1, f32[16,16,64]{2,1,0:T(8,128)S(1)} %copy-done, ...), custom_call_target="tpu_custom_call" | custom-call | tf_op jit(solution)/shard_map/pack_momentum/pallas_call | solution.py:214
  19.8 6.7 %all-to-all-done.column_ref = bf16[64,8,128]{2,1,0:T(8,128)(2,1)S(1)} async-done(((bf16[64,8,128]{2,1,0:T(8,128)(2,1)}), bf16[64,8,128]{2,1,0:T(8,128)(2,1)S(1)}, u32[]{:S(2)}, u32[]{:S(2)}) %all-to-all-start) | async-done | bytes 131104 | tf_op jit(solution)/shard_map/all_to_all | solution.py:210
  26.5 0.4 gather_modules.1
  26.8 17.2 %all_to_all.15 = s32[64,9,1,128]{3,2,1,0:T(1,128)S(1)} all-to-all(s32[64,9,1,128]{3,2,1,0:T(1,128)S(1)} %bitcast.17), channel_id=1, replica_groups=mesh['path_0'=4,'path_1'=8,'path_2'=2,'shard_2'=2,'shard_1'=2,'shard_0'=..., dimensions={0} | all-to-all | bytes 589824 | tf_op jit(solution)/shard_map/all_to_all | solution.py:238
  44.1 0.6 %sum_squares.1 = f32[8,128]{1,0:T(8,128)} custom-call(s32[576,128]{1,0:T(8,128)S(1)} %bitcast.15), custom_call_target="tpu_custom_call" | custom-call | tf_op jit(solution)/shard_map/sum_squares/pallas_call | solution.py:240
  44.7 6.8 %all-to-all-start.2 = ((f32[8,1,128]{2,1,0:T(1,128)}), f32[8,1,128]{2,1,0:T(1,128)S(1)}, u32[]{:S(2)}, u32[]{:S(2)}) async-start(f32[8,1,128]{2,1,0:T(1,128)} %bitcast.6), calls=%async_computation.2 | async-start | bytes 8192 | tf_op jit(solution)/shard_map/all_to_all | solution.py:250
  51.5 2.6 %collective-permute-start.1 = (f32[16,8,128]{2,1,0:T(8,128)S(1)}, f32[16,8,128]{2,1,0:T(8,128)S(1)}, u32[]{:S(2)}, u32[]{:S(2)}) collective-permute-start(f32[16,8,128]{2,1,0:T(8,128)S(1)} %get-tuple-element.30.mine_ref), channel_id=1, source_target_pairs={{0,8},{8,0},{1,9},{9,1},{2,10},{10,2},{3,11},{11,3},{4,12},{12,4},... | collective-permute-start | bytes 196616 | tf_op jit(solution)/shard_map/ppermute | solution.py:251
  54.1 0.2 assemble.1
  54.3 0.7 %collective-permute-done.1.other_ref = f32[16,8,128]{2,1,0:T(8,128)S(1)} collective-permute-done((f32[16,8,128]{2,1,0:T(8,128)S(1)}, f32[16,8,128]{2,1,0:T(8,128)S(1)}, u32[]{:S(2)}, u32[]{:S(2)}) %collective-permute-start.1) | collective-permute-done | bytes 65568 | tf_op jit(solution)/shard_map/ppermute | solution.py:251
  55.0 0.1 state_columns.1
  55.1 2.8 %all-to-all-done.2 = f32[8,1,128]{2,1,0:T(1,128)S(1)} async-done(((f32[8,1,128]{2,1,0:T(1,128)}), f32[8,1,128]{2,1,0:T(1,128)S(1)}, u32[]{:S(2)}, u32[]{:S(2)}) %all-to-all-start.2) | async-done | bytes 4128 | tf_op jit(solution)/shard_map/all_to_all | solution.py:250
  57.9 1.0 %step.1 = (bf16[64,8,128]{2,1,0:T(8,128)(2,1)}, f32[16,16,64]{2,1,0:T(8,128)}) custom-call(f32[8,128]{1,0:T(8,128)S(1)} %bitcast.18, f32[64,8,128]{2,1,0:T(8,128)S(1)} %get-tuple-element.28.refs_1_, f32[64,8,128]{2,1,0:T(8,128)S(1)} %get-tuple-element.29.refs_2_, f32[16,16,64]{2,1,0:T(8,128)S(1)} %get-tuple-element.32.refs_3_, ...), custom_call_target="tpu_custom_call" | custom-call | tf_op jit(solution)/shard_map/step/pallas_call | solution.py:269
  (1 shorter events, 0.0 us)
Async XLA Ops:
  0.6 15.1 %copy-start = (f32[16,16,64]{2,1,0:T(8,128)S(1)}, f32[16,16,64]{2,1,0:T(8,128)}, u32[]{:S(2)}) copy-start(f32[16,16,64]{2,1,0:T(8,128)} %refs_5_.1) | copy-start | bytes 196612
  0.6 25.8 %all-to-all-start = ((bf16[64,8,128]{2,1,0:T(8,128)(2,1)}), bf16[64,8,128]{2,1,0:T(8,128)(2,1)S(1)}, u32[]{:S(2)}, u32[]{:S(2)}) async-start(bf16[64,8,128]{2,1,0:T(8,128)(2,1)} %bitcast.19), calls=%async_computation | async-start | bytes 262144 | tf_op jit(solution)/shard_map/all_to_all | solution.py:210
  15.7 3.2 %copy-start.1 = (s32[64]{0:T(128)S(1)}, s32[64]{0:T(128)}, u32[]{:S(2)}) copy-start(s32[64]{0:T(128)} %module_ref.1) | copy-start | bytes 772
  15.8 3.2 %collective-permute-start = (f32[16,8,64]{2,1,0:T(8,128)S(1)}, f32[16,8,64]{2,1,0:T(8,128)S(1)}, u32[]{:S(2)}, u32[]{:S(2)}) collective-permute-start(f32[16,8,64]{2,1,0:T(8,128)S(1)} %slice_select_fusion), channel_id=1, source_target_pairs={{0,8},{8,0},{1,9},{9,1},{2,10},{10,2},{3,11},{11,3},{4,12},{12,4},... | collective-permute-start | bytes 98312 | tf_op jit(solution)/shard_map/ppermute | solution.py:212
  44.7 13.3 %all-to-all-start.2 = ((f32[8,1,128]{2,1,0:T(1,128)}), f32[8,1,128]{2,1,0:T(1,128)S(1)}, u32[]{:S(2)}, u32[]{:S(2)}) async-start(f32[8,1,128]{2,1,0:T(1,128)} %bitcast.6), calls=%async_computation.2 | async-start | bytes 8192 | tf_op jit(solution)/shard_map/all_to_all | solution.py:250
  51.5 3.5 %collective-permute-start.1 = (f32[16,8,128]{2,1,0:T(8,128)S(1)}, f32[16,8,128]{2,1,0:T(8,128)S(1)}, u32[]{:S(2)}, u32[]{:S(2)}) collective-permute-start(f32[16,8,128]{2,1,0:T(8,128)S(1)} %get-tuple-element.30.mine_ref), channel_id=1, source_target_pairs={{0,8},{8,0},{1,9},{9,1},{2,10},{10,2},{3,11},{11,3},{4,12},{12,4},... | collective-permute-start | bytes 196616 | tf_op jit(solution)/shard_map/ppermute | solution.py:251

commit v12 on v10

--- a/solution.py
+++ b/solution.py
@@ -23,6 +23,8 @@
 MOMENTUM_SCALE = 8191.0
 SQUARES_SCALE = 128.0
 FOLD = momentum_rate * momentum_rate / (1.0 + momentum_rate)
+GRAD_RATE = outer_rate * (1.0 + momentum_rate)
+MOMENTUM_RATE = outer_rate * momentum_rate * momentum_rate
 KERNEL_BYTES = 4 << 20
 VMEM = pl.BlockSpec(memory_space=pltpu.VMEM)
 SMEM = pl.BlockSpec(memory_space=pltpu.SMEM)
@@ -150,11 +152,11 @@
         start = path * CHUNK
         words = chunk_ref[start : start + UPPER, :]
         of_row = jnp.where(own_lane, scale[path : path + 1, :], 0.0)
-        of_row = jnp.sum(of_row, axis=1, keepdims=True)
+        of_row = jnp.sum(of_row, axis=1, keepdims=True) * GRAD_RATE
         grad_ref[q] = (words >> LOWER_BITS).astype(jnp.float32) * of_row
         upper = (chunk_ref[start + UPPER : start + CHUNK, :] >> (row * 3)) & 7
         whole = ((upper << LOWER_BITS) | (words & ((1 << LOWER_BITS) - 1))) - 32768
-        decay_ref[q] = whole.astype(jnp.float32) * (momentum_rate / MOMENTUM_SCALE)
+        decay_ref[q] = whole.astype(jnp.float32) * (MOMENTUM_RATE / MOMENTUM_SCALE)
     mask_ref[...] = own_ref[...]
 
 
@@ -186,8 +188,7 @@
     copies = []
     for piece in range(PIECES):
         tiles = slice(piece * each, (piece + 1) * each)
-        clipped = grad_ref[tiles] * own.reshape(1, 1, 1)
-        step = outer_rate * (clipped + momentum_rate * (decay_ref[tiles] + clipped))
+        step = grad_ref[tiles] * own.reshape(1, 1, 1) + decay_ref[tiles]
         update[tiles] = step.astype(jnp.bfloat16)
         copies.append(pltpu.make_async_copy(update.at[tiles], update_out.at[tiles], sems.at[piece]))
         copies[-1].start()

time: 59.5 us -> 59.5 us (level)
  no operation moved by 1% of the time
where the time goes in v12:
time: 59.5 us; the launch traced here: 59 us
  starting transfers between devices  26.8 us (45%)
  blocking collectives  17.2 us (29%)
  waiting for transfers between devices  11.1 us (19%)
  Pallas kernels  3.08 us (5%)
  between operations  0.72 us (1%)
    all_to_all x1, blocking collectives, local(): lax.all_to_all(chunks.reshape(peers, CHUNK, 1, 128), PATH, 0, 0, tiled=True)  17.2 us
    all_to_all x1, starting transfers between devices, local(): column_tiles = lax.all_to_all(tiles, TILES, 0, 0, tiled=True)  15.1 us
    all_to_all x1, starting transfers between devices, local(): squares = lax.all_to_all(squares, SHARD_ORDER, 0, 0, tiled=True)  6.83 us
    all_to_all x1, waiting for transfers between devices, local(): column_tiles = lax.all_to_all(tiles, TILES, 0, 0, tiled=True)  6.62 us
    all_to_all x1, waiting for transfers between devices, local(): squares = lax.all_to_all(squares, SHARD_ORDER, 0, 0, tiled=True)  2.83 us
    ppermute x1, starting transfers between devices, local(): other = lax.ppermute(grad, 'path_2', [(0, 1), (1, 0)])  2.61 us
    ppermute x1, starting transfers between devices, local(): other = lax.ppermute(momentum, 'path_2', [(0, 1), (1, 0)])  2.26 us
  transfers between devices with their start and end apart: 4, of which 4 were waited for; matrix products, arithmetic and copies ran while one was open for 0% of the time, Pallas kernels for 2%

profile of v12, /device:TPU:1, one launch (start us, length us, event | category | flops | bytes accessed | tf_op | source)
XLA Modules:
  0.0 59.0 jit_solution(17351324199883591353)
XLA Ops:
  0.6 0.0 copy-start
  0.6 0.0 copy-start.1
  0.6 15.1 %all-to-all-start = ((bf16[64,8,128]{2,1,0:T(8,128)(2,1)}), bf16[64,8,128]{2,1,0:T(8,128)(2,1)S(1)}, u32[]{:S(2)}, u32[]{:S(2)}) async-start(bf16[64,8,128]{2,1,0:T(8,128)(2,1)} %bitcast.19), calls=%async_computation | async-start | bytes 262144 | tf_op jit(solution)/shard_map/all_to_all | solution.py:211
  15.7 0.0 copy-done
  15.7 2.3 %collective-permute-start = (f32[16,16,64]{2,1,0:T(8,128)S(1)}, f32[16,16,64]{2,1,0:T(8,128)S(1)}, u32[]{:S(2)}, u32[]{:S(2)}) collective-permute-start(f32[16,16,64]{2,1,0:T(8,128)S(1)} %copy-done), channel_id=1, source_target_pairs={{0,8},{8,0},{1,9},{9,1},{2,10},{10,2},{3,11},{11,3},{4,12},{12,4},... | collective-permute-start | bytes 196616 | tf_op jit(solution)/shard_map/ppermute | solution.py:212
  18.0 1.0 %collective-permute-done.other_ref = f32[16,16,64]{2,1,0:T(8,128)S(1)} collective-permute-done((f32[16,16,64]{2,1,0:T(8,128)S(1)}, f32[16,16,64]{2,1,0:T(8,128)S(1)}, u32[]{:S(2)}, u32[]{:S(2)}) %collective-permute-start) | collective-permute-done | bytes 65568 | tf_op jit(solution)/shard_map/ppermute | solution.py:212
  19.0 0.0 copy-done.1
  19.0 0.9 %pack_momentum.1 = (s32[16,8,128]{2,1,0:T(8,128)S(1)}, s32[16,128]{1,0:T(8,128)S(1)}, f32[16,8,128]{2,1,0:T(8,128)S(1)}, f32[16,128]{1,0:T(8,128)S(1)}, s32[8,128]{1,0:T(8,128)S(1)}, /*index=5*/f32[1,128]{1,0:T(1,128)S(1)}) custom-call(s32[64]{0:T(128)S(1)} %copy-done.1, f32[16,16,64]{2,1,0:T(8,128)S(1)} %copy-done, ...), custom_call_target="tpu_custom_call" | custom-call | tf_op jit(solution)/shard_map/pack_momentum/pallas_call | solution.py:214
  19.9 6.6 %all-to-all-done.column_ref = bf16[64,8,128]{2,1,0:T(8,128)(2,1)S(1)} async-done(((bf16[64,8,128]{2,1,0:T(8,128)(2,1)}), bf16[64,8,128]{2,1,0:T(8,128)(2,1)S(1)}, u32[]{:S(2)}, u32[]{:S(2)}) %all-to-all-start) | async-done | bytes 131104 | tf_op jit(solution)/shard_map/all_to_all | solution.py:211
  26.5 0.4 gather_modules.1
  26.8 17.2 %all_to_all.15 = s32[64,9,1,128]{3,2,1,0:T(1,128)S(1)} all-to-all(s32[64,9,1,128]{3,2,1,0:T(1,128)S(1)} %bitcast.17), channel_id=1, replica_groups=mesh['path_0'=4,'path_1'=8,'path_2'=2,'shard_2'=2,'shard_1'=2,'shard_0'=..., dimensions={0} | all-to-all | bytes 589824 | tf_op jit(solution)/shard_map/all_to_all | solution.py:238
  44.1 0.6 %sum_squares.1 = f32[8,128]{1,0:T(8,128)} custom-call(s32[576,128]{1,0:T(8,128)S(1)} %bitcast.15), custom_call_target="tpu_custom_call" | custom-call | tf_op jit(solution)/shard_map/sum_squares/pallas_call | solution.py:240
  44.7 6.8 %all-to-all-start.2 = ((f32[8,1,128]{2,1,0:T(1,128)}), f32[8,1,128]{2,1,0:T(1,128)S(1)}, u32[]{:S(2)}, u32[]{:S(2)}) async-start(f32[8,1,128]{2,1,0:T(1,128)} %bitcast.6), calls=%async_computation.2 | async-start | bytes 8192 | tf_op jit(solution)/shard_map/all_to_all | solution.py:250
  51.5 2.6 %collective-permute-start.1 = (f32[16,8,128]{2,1,0:T(8,128)S(1)}, f32[16,8,128]{2,1,0:T(8,128)S(1)}, u32[]{:S(2)}, u32[]{:S(2)}) collective-permute-start(f32[16,8,128]{2,1,0:T(8,128)S(1)} %get-tuple-element.30.mine_ref), channel_id=1, source_target_pairs={{0,8},{8,0},{1,9},{9,1},{2,10},{10,2},{3,11},{11,3},{4,12},{12,4},... | collective-permute-start | bytes 196616 | tf_op jit(solution)/shard_map/ppermute | solution.py:251
  54.1 0.2 assemble.1
  54.3 0.7 %collective-permute-done.1.other_ref = f32[16,8,128]{2,1,0:T(8,128)S(1)} collective-permute-done((f32[16,8,128]{2,1,0:T(8,128)S(1)}, f32[16,8,128]{2,1,0:T(8,128)S(1)}, u32[]{:S(2)}, u32[]{:S(2)}) %collective-permute-start.1) | collective-permute-done | bytes 65568 | tf_op jit(solution)/shard_map/ppermute | solution.py:251
  55.0 0.1 state_columns.1
  55.1 2.8 %all-to-all-done.2 = f32[8,1,128]{2,1,0:T(1,128)S(1)} async-done(((f32[8,1,128]{2,1,0:T(1,128)}), f32[8,1,128]{2,1,0:T(1,128)S(1)}, u32[]{:S(2)}, u32[]{:S(2)}) %all-to-all-start.2) | async-done | bytes 4128 | tf_op jit(solution)/shard_map/all_to_all | solution.py:250
  58.0 1.0 %step.1 = (bf16[64,8,128]{2,1,0:T(8,128)(2,1)}, f32[16,16,64]{2,1,0:T(8,128)}) custom-call(f32[8,128]{1,0:T(8,128)S(1)} %bitcast.18, f32[64,8,128]{2,1,0:T(8,128)S(1)} %get-tuple-element.28.refs_1_, f32[64,8,128]{2,1,0:T(8,128)S(1)} %get-tuple-element.29.refs_2_, f32[16,16,64]{2,1,0:T(8,128)S(1)} %get-tuple-element.32.refs_3_, ...), custom_call_target="tpu_custom_call" | custom-call | tf_op jit(solution)/shard_map/step/pallas_call | solution.py:269
Async XLA Ops:
  0.6 15.1 %copy-start = (f32[16,16,64]{2,1,0:T(8,128)S(1)}, f32[16,16,64]{2,1,0:T(8,128)}, u32[]{:S(2)}) copy-start(f32[16,16,64]{2,1,0:T(8,128)} %refs_5_.1) | copy-start | bytes 196612
  0.6 18.4 %copy-start.1 = (s32[64]{0:T(128)S(1)}, s32[64]{0:T(128)}, u32[]{:S(2)}) copy-start(s32[64]{0:T(128)} %module_ref.1) | copy-start | bytes 772
  0.6 25.8 %all-to-all-start = ((bf16[64,8,128]{2,1,0:T(8,128)(2,1)}), bf16[64,8,128]{2,1,0:T(8,128)(2,1)S(1)}, u32[]{:S(2)}, u32[]{:S(2)}) async-start(bf16[64,8,128]{2,1,0:T(8,128)(2,1)} %bitcast.19), calls=%async_computation | async-start | bytes 262144 | tf_op jit(solution)/shard_map/all_to_all | solution.py:211
  15.7 3.2 %collective-permute-start = (f32[16,16,64]{2,1,0:T(8,128)S(1)}, f32[16,16,64]{2,1,0:T(8,128)S(1)}, u32[]{:S(2)}, u32[]{:S(2)}) collective-permute-start(f32[16,16,64]{2,1,0:T(8,128)S(1)} %copy-done), channel_id=1, source_target_pairs={{0,8},{8,0},{1,9},{9,1},{2,10},{10,2},{3,11},{11,3},{4,12},{12,4},... | collective-permute-start | bytes 196616 | tf_op jit(solution)/shard_map/ppermute | solution.py:212
  44.7 13.3 %all-to-all-start.2 = ((f32[8,1,128]{2,1,0:T(1,128)}), f32[8,1,128]{2,1,0:T(1,128)S(1)}, u32[]{:S(2)}, u32[]{:S(2)}) async-start(f32[8,1,128]{2,1,0:T(1,128)} %bitcast.6), calls=%async_computation.2 | async-start | bytes 8192 | tf_op jit(solution)/shard_map/all_to_all | solution.py:250
  51.5 3.5 %collective-permute-start.1 = (f32[16,8,128]{2,1,0:T(8,128)S(1)}, f32[16,8,128]{2,1,0:T(8,128)S(1)}, u32[]{:S(2)}, u32[]{:S(2)}) collective-permute-start(f32[16,8,128]{2,1,0:T(8,128)S(1)} %get-tuple-element.30.mine_ref), channel_id=1, source_target_pairs={{0,8},{8,0},{1,9},{9,1},{2,10},{10,2},{3,11},{11,3},{4,12},{12,4},... | collective-permute-start | bytes 196616 | tf_op jit(solution)/shard_map/ppermute | solution.py:251

commit v13 on v10

--- a/solution.py
+++ b/solution.py
@@ -27,7 +27,7 @@
 VMEM = pl.BlockSpec(memory_space=pltpu.VMEM)
 SMEM = pl.BlockSpec(memory_space=pltpu.SMEM)
 HBM = pl.BlockSpec(memory_space=pl.ANY)
-PIECES = 4
+PIECES = 8
 
 
 def path_of(peer, chips):

time: 59.5 us -> 59.5 us (level)
  no operation moved by 1% of the time
where the time goes in v13:
time: 59.5 us; the launch traced here: 59 us
  starting transfers between devices  26.8 us (45%)
  blocking collectives  17.2 us (29%)
  waiting for transfers between devices  11.1 us (19%)
  Pallas kernels  3.12 us (5%)
  between operations  0.72 us (1%)
    all_to_all x1, blocking collectives, local(): lax.all_to_all(chunks.reshape(peers, CHUNK, 1, 128), PATH, 0, 0, tiled=True)  17.2 us
    all_to_all x1, starting transfers between devices, local(): column_tiles = lax.all_to_all(tiles, TILES, 0, 0, tiled=True)  15.1 us
    all_to_all x1, starting transfers between devices, local(): squares = lax.all_to_all(squares, SHARD_ORDER, 0, 0, tiled=True)  6.83 us
    all_to_all x1, waiting for transfers between devices, local(): column_tiles = lax.all_to_all(tiles, TILES, 0, 0, tiled=True)  6.62 us
    all_to_all x1, waiting for transfers between devices, local(): squares = lax.all_to_all(squares, SHARD_ORDER, 0, 0, tiled=True)  2.83 us
    ppermute x1, starting transfers between devices, local(): other = lax.ppermute(grad, 'path_2', [(0, 1), (1, 0)])  2.61 us
    ppermute x1, starting transfers between devices, local(): other = lax.ppermute(momentum, 'path_2', [(0, 1), (1, 0)])  2.26 us
  transfers between devices with their start and end apart: 4, of which 4 were waited for; matrix products, arithmetic and copies ran while one was open for 0% of the time, Pallas kernels for 2%

profile of v13, /device:TPU:1, one launch (start us, length us, event | category | flops | bytes accessed | tf_op | source)
XLA Modules:
  0.0 59.0 jit_solution(3501133268758078665)
XLA Ops:
  0.6 0.0 copy-start
  0.6 0.0 copy-start.1
  0.6 15.1 %all-to-all-start = ((bf16[64,8,128]{2,1,0:T(8,128)(2,1)}), bf16[64,8,128]{2,1,0:T(8,128)(2,1)S(1)}, u32[]{:S(2)}, u32[]{:S(2)}) async-start(bf16[64,8,128]{2,1,0:T(8,128)(2,1)} %bitcast.19), calls=%async_computation | async-start | bytes 262144 | tf_op jit(solution)/shard_map/all_to_all | solution.py:210
  15.7 0.0 copy-done
  15.7 2.3 %collective-permute-start = (f32[16,16,64]{2,1,0:T(8,128)S(1)}, f32[16,16,64]{2,1,0:T(8,128)S(1)}, u32[]{:S(2)}, u32[]{:S(2)}) collective-permute-start(f32[16,16,64]{2,1,0:T(8,128)S(1)} %copy-done), channel_id=1, source_target_pairs={{0,8},{8,0},{1,9},{9,1},{2,10},{10,2},{3,11},{11,3},{4,12},{12,4},... | collective-permute-start | bytes 196616 | tf_op jit(solution)/shard_map/ppermute | solution.py:211
  18.0 1.0 %collective-permute-done.other_ref = f32[16,16,64]{2,1,0:T(8,128)S(1)} collective-permute-done((f32[16,16,64]{2,1,0:T(8,128)S(1)}, f32[16,16,64]{2,1,0:T(8,128)S(1)}, u32[]{:S(2)}, u32[]{:S(2)}) %collective-permute-start) | collective-permute-done | bytes 65568 | tf_op jit(solution)/shard_map/ppermute | solution.py:211
  19.0 0.0 copy-done.1
  19.0 0.9 %pack_momentum.1 = (s32[16,8,128]{2,1,0:T(8,128)S(1)}, s32[16,128]{1,0:T(8,128)S(1)}, f32[16,8,128]{2,1,0:T(8,128)S(1)}, f32[16,128]{1,0:T(8,128)S(1)}, s32[8,128]{1,0:T(8,128)S(1)}, /*index=5*/f32[1,128]{1,0:T(1,128)S(1)}) custom-call(s32[64]{0:T(128)S(1)} %copy-done.1, f32[16,16,64]{2,1,0:T(8,128)S(1)} %copy-done, ...), custom_call_target="tpu_custom_call" | custom-call | tf_op jit(solution)/shard_map/pack_momentum/pallas_call | solution.py:213
  19.9 6.6 %all-to-all-done.column_ref = bf16[64,8,128]{2,1,0:T(8,128)(2,1)S(1)} async-done(((bf16[64,8,128]{2,1,0:T(8,128)(2,1)}), bf16[64,8,128]{2,1,0:T(8,128)(2,1)S(1)}, u32[]{:S(2)}, u32[]{:S(2)}) %all-to-all-start) | async-done | bytes 131104 | tf_op jit(solution)/shard_map/all_to_all | solution.py:210
  26.5 0.4 gather_modules.1
  26.8 17.2 %all_to_all.15 = s32[64,9,1,128]{3,2,1,0:T(1,128)S(1)} all-to-all(s32[64,9,1,128]{3,2,1,0:T(1,128)S(1)} %bitcast.17), channel_id=1, replica_groups=mesh['path_0'=4,'path_1'=8,'path_2'=2,'shard_2'=2,'shard_1'=2,'shard_0'=..., dimensions={0} | all-to-all | bytes 589824 | tf_op jit(solution)/shard_map/all_to_all | solution.py:237
  44.1 0.6 %sum_squares.1 = f32[8,128]{1,0:T(8,128)} custom-call(s32[576,128]{1,0:T(8,128)S(1)} %bitcast.15), custom_call_target="tpu_custom_call" | custom-call | tf_op jit(solution)/shard_map/sum_squares/pallas_call | solution.py:239
  44.7 6.8 %all-to-all-start.2 = ((f32[8,1,128]{2,1,0:T(1,128)}), f32[8,1,128]{2,1,0:T(1,128)S(1)}, u32[]{:S(2)}, u32[]{:S(2)}) async-start(f32[8,1,128]{2,1,0:T(1,128)} %bitcast.6), calls=%async_computation.2 | async-start | bytes 8192 | tf_op jit(solution)/shard_map/all_to_all | solution.py:249
  51.5 2.6 %collective-permute-start.1 = (f32[16,8,128]{2,1,0:T(8,128)S(1)}, f32[16,8,128]{2,1,0:T(8,128)S(1)}, u32[]{:S(2)}, u32[]{:S(2)}) collective-permute-start(f32[16,8,128]{2,1,0:T(8,128)S(1)} %get-tuple-element.30.mine_ref), channel_id=1, source_target_pairs={{0,8},{8,0},{1,9},{9,1},{2,10},{10,2},{3,11},{11,3},{4,12},{12,4},... | collective-permute-start | bytes 196616 | tf_op jit(solution)/shard_map/ppermute | solution.py:250
  54.1 0.2 assemble.1
  54.3 0.7 %collective-permute-done.1.other_ref = f32[16,8,128]{2,1,0:T(8,128)S(1)} collective-permute-done((f32[16,8,128]{2,1,0:T(8,128)S(1)}, f32[16,8,128]{2,1,0:T(8,128)S(1)}, u32[]{:S(2)}, u32[]{:S(2)}) %collective-permute-start.1) | collective-permute-done | bytes 65568 | tf_op jit(solution)/shard_map/ppermute | solution.py:250
  55.0 0.1 state_columns.1
  55.1 2.8 %all-to-all-done.2 = f32[8,1,128]{2,1,0:T(1,128)S(1)} async-done(((f32[8,1,128]{2,1,0:T(1,128)}), f32[8,1,128]{2,1,0:T(1,128)S(1)}, u32[]{:S(2)}, u32[]{:S(2)}) %all-to-all-start.2) | async-done | bytes 4128 | tf_op jit(solution)/shard_map/all_to_all | solution.py:249
  58.0 1.0 %step.1 = (bf16[64,8,128]{2,1,0:T(8,128)(2,1)}, f32[16,16,64]{2,1,0:T(8,128)}) custom-call(f32[8,128]{1,0:T(8,128)S(1)} %bitcast.18, f32[64,8,128]{2,1,0:T(8,128)S(1)} %get-tuple-element.28.refs_1_, f32[64,8,128]{2,1,0:T(8,128)S(1)} %get-tuple-element.29.refs_2_, f32[16,16,64]{2,1,0:T(8,128)S(1)} %get-tuple-element.32.refs_3_, ...), custom_call_target="tpu_custom_call" | custom-call | tf_op jit(solution)/shard_map/step/pallas_call | solution.py:268
Async XLA Ops:
  0.6 15.1 %copy-start = (f32[16,16,64]{2,1,0:T(8,128)S(1)}, f32[16,16,64]{2,1,0:T(8,128)}, u32[]{:S(2)}) copy-start(f32[16,16,64]{2,1,0:T(8,128)} %refs_5_.1) | copy-start | bytes 196612
  0.6 18.4 %copy-start.1 = (s32[64]{0:T(128)S(1)}, s32[64]{0:T(128)}, u32[]{:S(2)}) copy-start(s32[64]{0:T(128)} %module_ref.1) | copy-start | bytes 772
  0.6 25.8 %all-to-all-start = ((bf16[64,8,128]{2,1,0:T(8,128)(2,1)}), bf16[64,8,128]{2,1,0:T(8,128)(2,1)S(1)}, u32[]{:S(2)}, u32[]{:S(2)}) async-start(bf16[64,8,128]{2,1,0:T(8,128)(2,1)} %bitcast.19), calls=%async_computation | async-start | bytes 262144 | tf_op jit(solution)/shard_map/all_to_all | solution.py:210
  15.7 3.2 %collective-permute-start = (f32[16,16,64]{2,1,0:T(8,128)S(1)}, f32[16,16,64]{2,1,0:T(8,128)S(1)}, u32[]{:S(2)}, u32[]{:S(2)}) collective-permute-start(f32[16,16,64]{2,1,0:T(8,128)S(1)} %copy-done), channel_id=1, source_target_pairs={{0,8},{8,0},{1,9},{9,1},{2,10},{10,2},{3,11},{11,3},{4,12},{12,4},... | collective-permute-start | bytes 196616 | tf_op jit(solution)/shard_map/ppermute | solution.py:211
  44.7 13.3 %all-to-all-start.2 = ((f32[8,1,128]{2,1,0:T(1,128)}), f32[8,1,128]{2,1,0:T(1,128)S(1)}, u32[]{:S(2)}, u32[]{:S(2)}) async-start(f32[8,1,128]{2,1,0:T(1,128)} %bitcast.6), calls=%async_computation.2 | async-start | bytes 8192 | tf_op jit(solution)/shard_map/all_to_all | solution.py:249
  51.5 3.5 %collective-permute-start.1 = (f32[16,8,128]{2,1,0:T(8,128)S(1)}, f32[16,8,128]{2,1,0:T(8,128)S(1)}, u32[]{:S(2)}, u32[]{:S(2)}) collective-permute-start(f32[16,8,128]{2,1,0:T(8,128)S(1)} %get-tuple-element.30.mine_ref), channel_id=1, source_target_pairs={{0,8},{8,0},{1,9},{9,1},{2,10},{10,2},{3,11},{11,3},{4,12},{12,4},... | collective-permute-start | bytes 196616 | tf_op jit(solution)/shard_map/ppermute | solution.py:250
